TPU v7x, 32 devices: a whole 2x2x4 slice. The times are simulated.
32 devices in a mesh: freq: 2 (over y), facet: 16 (over z, x, core).
Axes of the slice: x: 2, y: 2, z: 4, core: 2. Of those that a mesh axis runs over, the one named last changes fastest.
Arguments:
- sky_image: float32 [1024, 2048], P('facet'), may hold values from -6 to 6
- primary_beam: float32 [2, 1024, 2048], P('freq', 'facet'), may hold values from 0.1 to 1
- observed: bfloat16 [8192, 512], P(('freq', 'facet')), may hold values from -6 to 6
- facet_of: int32 [8192], P(('freq', 'facet')), may hold values from 0 to 15, as said below
- tile_slot: int32 [8192], P(('freq', 'facet')), may hold values from 0 to 511
- conv_first: float32 [32, 3, 3], replicated, may hold values from -2 to 2
- bias_first: float32 [32], replicated, may hold values from -3 to 3
- conv_second: float32 [32, 3, 3], replicated, may hold values from -0.375 to 0.375
Outputs:
- residual_tiles: bfloat16 [8192, 512], P(('freq', 'facet'))
- image_next: float32 [1024, 2048], P('facet', 'freq')
Inputs may be any that keep to these rules, and one draw needn't show every extreme that they name: `facet_of`: at most 32 of one device's tiles name one facet; in every frequency group some facet is named by exactly 32 tiles of every device of the group.
All inputs are finite; a program needn't handle non-finite values.
Results may differ from a plain program's by a relative error of at most 0.002.
Values may be sent and summed in bfloat16 or wider, within the bound.
No kernel may reach another device: no remote copies, remote signals or barrier semaphores. Data moves between devices by JAX's collectives and lax.ppermute only.
A program may use at most 64 MiB of HBM per device.

v0:
```python
import functools
import math

import jax
import jax.numpy as jnp
import numpy as np
from jax import lax
from jax.experimental import pallas as pl
from jax.experimental.pallas import tpu as pltpu
from jax.sharding import PartitionSpec as P


S = 16
LANES = 128
BAND = 22
STEP = 0.5
F32 = jnp.float32
BF16 = jnp.bfloat16


def iota(shape, dim):
    return lax.broadcasted_iota(jnp.int32, shape, dim)


def mm(a, b, dims=((1,), (0,))):
    return lax.dot_general(a, b, (dims, ((), ())), preferred_element_type=F32)


def one_hot(cond):
    return jnp.where(cond, 1.0, 0.0).astype(BF16)


def split(x):
    high = x.astype(BF16)
    return high, (x - high.astype(F32)).astype(BF16)


def np_split(x):
    x = np.asarray(x, np.float32)
    high = x.astype(BF16)
    return high, (x - high.astype(np.float32)).astype(BF16)


def tables(rows, cols, sign):
    outer = cols // LANES
    scale = 1.0 / math.sqrt(rows * cols)
    k = np.arange(rows)
    angle = sign * 2.0 * np.pi * ((k[:, None] * k[None, :]) % rows) / rows
    cos_r, sin_r = np.cos(angle) * scale, np.sin(angle) * scale
    if sign < 0:
        row_high, row_low = np_split(np.concatenate([cos_r, sin_r], 0))
        row = np.concatenate([row_high, row_high, row_low], 1)
    else:
        row_high, row_low = np_split(np.concatenate([cos_r, -sin_r], 1))
        row = np.concatenate([row_high, row_high, row_low], 1)
    i2 = np.arange(LANES)
    w = np.arange(outer)
    twist = sign * 2.0 * np.pi * ((w[:, None] * i2[None, :]) % cols) / cols
    inner = sign * 2.0 * np.pi * ((i2[:, None] * i2[None, :]) % LANES) / LANES
    c, s = np.cos(inner), np.sin(inner)
    mat_high, mat_low = np_split(np.block([[c, s], [-s, c]]))
    return (
        row,
        np.stack([np.cos(twist), np.sin(twist)]).astype(np.float32),
        np.stack([mat_high, mat_low]),
    )


def times_i(z, sign):
    re, im = z
    return (-im, re) if sign > 0 else (im, -re)


def add(a, b):
    return (a[0] + b[0], a[1] + b[1])


def sub(a, b):
    return (a[0] - b[0], a[1] - b[1])


def dft4(x, sign):
    s0, s1 = add(x[0], x[2]), sub(x[0], x[2])
    s2, s3 = add(x[1], x[3]), times_i(sub(x[1], x[3]), sign)
    return [add(s0, s2), add(s1, s3), sub(s0, s2), sub(s1, s3)]


def dft16(x, sign):
    mid = [dft4([x[4 * a + b] for a in range(4)], sign) for b in range(4)]
    out = [None] * 16
    for c in range(4):
        turned = []
        for b in range(4):
            re, im = mid[b][c]
            phase = (b * c) % 16
            if phase == 0:
                turned.append((re, im))
            elif phase == 4:
                turned.append(times_i((re, im), sign))
            else:
                wr = math.cos(2.0 * math.pi * phase / 16)
                wi = sign * math.sin(2.0 * math.pi * phase / 16)
                turned.append((re * wr - im * wi, re * wi + im * wr))
        for d, value in enumerate(dft4(turned, sign)):
            out[c + 4 * d] = value
    return out


def swap_matrix(size):
    src = iota((1, size), 1)
    swapped = (src & -256) | ((src & 15) << 4) | ((src >> 4) & 15)
    return one_hot(iota((size, size), 0) == swapped)


def pack_kernel(facets, cap, facet_hbm, slot_hbm, seen_hbm, send_ref, dest_ref, facet_ref, slot_ref, seen_ref, sems):
    tiles, width = seen_ref.shape
    total = facets * cap
    loads = [
        pltpu.make_async_copy(src, dst, sems.at[i])
        for i, (src, dst) in enumerate(
            ((facet_hbm, facet_ref), (slot_hbm, slot_ref), (seen_hbm, seen_ref))
        )
    ]
    for load in loads:
        load.start()
    swap = swap_matrix(width)
    loads[0].wait()
    facet = facet_ref[...]
    member = iota((facets, tiles), 0) == facet
    member_f = jnp.where(member, 1.0, 0.0)
    before = one_hot(iota((tiles, tiles), 0) < iota((tiles, tiles), 1))
    ranks = mm(member_f.astype(BF16), before)
    rank = jnp.sum(member_f * ranks, axis=0, keepdims=True).astype(jnp.int32)
    dest = facet * cap + rank
    dest_ref[...] = dest
    placing = one_hot(iota((total, tiles), 0) == dest)
    loads[2].wait()
    turned = mm(seen_ref[...], swap).astype(BF16)
    packed = mm(placing, turned).astype(BF16)
    loads[1].wait()
    code = slot_ref[...] + 1
    lane = iota((LANES, tiles), 0)
    slots = mm(
        (member_f * (code >> 4).astype(F32)).astype(BF16), one_hot(lane == rank), ((1,), (1,))
    ) + mm(
        (member_f * (code & 15).astype(F32)).astype(BF16),
        one_hot(lane - LANES // 2 == rank),
        ((1,), (1,)),
    )
    parts = width // LANES
    for d in range(facets):
        for part in range(parts):
            send_ref[d, part * cap : (part + 1) * cap, :] = packed[
                d * cap : (d + 1) * cap, part * LANES : (part + 1) * LANES
            ]
        send_ref[d, parts * cap : parts * cap + 8, :] = jnp.broadcast_to(
            slots[d : d + 1, :], (8, LANES)
        ).astype(BF16)


def forward_kernel(
    sky_ref,
    beam_ref,
    row_ref,
    twist_ref,
    mat_ref,
    first_ref,
    bias_ref,
    second_ref,
    high_ref,
    low_ref,
    one_ref,
    two_ref,
):
    prepare(first_ref, bias_ref, second_ref, one_ref, two_ref)
    rows, cols = sky_ref.shape
    outer = cols // LANES
    weighted = sky_ref[...] * beam_ref[...]
    w_high, w_low = split(weighted)
    mid = mm(row_ref[...], jnp.concatenate([w_high, w_low, w_high], axis=0))
    lines = [
        (
            mid[:rows, i * LANES : (i + 1) * LANES],
            mid[rows:, i * LANES : (i + 1) * LANES],
        )
        for i in range(outer)
    ]
    spread = dft16(lines, -1)
    blocks = []
    for w in range(outer):
        re, im = spread[w]
        tr, ti = twist_ref[0, w : w + 1, :], twist_ref[1, w : w + 1, :]
        blocks.append(jnp.concatenate([re * tr - im * ti, re * ti + im * tr], axis=1))
    high, low = split(jnp.concatenate(blocks, axis=0))
    mat_high, mat_low = mat_ref[0], mat_ref[1]
    model = mm(high, mat_high) + mm(low, mat_high) + mm(high, mat_low)
    for w in range(outer):
        for r in range(rows // S):
            for e in range(2):
                piece = model[
                    w * rows + r * S : w * rows + (r + 1) * S, e * LANES : (e + 1) * LANES
                ]
                piece_high, piece_low = split(piece)
                at = (pl.ds(e * 256 + w * S, S), pl.ds(r * LANES, LANES))
                high_ref[at] = piece_high
                low_ref[at] = piece_low


def residual_kernel(facets, cap, got_ref, high_ref, low_ref, res_hbm, sel_ref, own_ref, sems):
    total = facets * cap
    slots = high_ref.shape[1]
    parts = high_ref.shape[0] // LANES
    code = got_ref[:, parts * cap : parts * cap + 8, :].astype(F32).reshape(facets * 8, LANES)
    source = iota((total, facets * 8), 0) // cap
    spread = mm(one_hot(iota((total, facets * 8), 1) == source * 8), code.astype(BF16))
    lane = iota((total, LANES), 1)
    rank = iota((total, LANES), 0) % cap
    kept = jnp.where((lane & (LANES // 2 - 1)) == rank, spread, 0.0).astype(BF16)
    digit = jnp.where(iota((LANES, slots), 0) < LANES // 2, 16.0, 1.0).astype(BF16)
    code_all = mm(kept, digit)
    sel = one_hot(code_all.astype(jnp.int32) == iota((total, slots), 1) + 1)
    sel_ref[...] = sel
    contract = ((1,), (1,))
    predicted = mm(sel, high_ref[...], contract) + mm(sel, low_ref[...], contract)
    saves = []
    pieces = sems.shape[0]
    for i in range(pieces):
        here = facets // pieces
        at = slice(i * here * cap, (i + 1) * here * cap)
        for part in range(parts):
            cols = slice(part * LANES, (part + 1) * LANES)
            seen = got_ref[i * here : (i + 1) * here, part * cap : (part + 1) * cap, :]
            seen = seen.astype(F32).reshape(here * cap, LANES)
            own_ref[at, cols] = (predicted[at, cols] - seen).astype(BF16)
        save = pltpu.make_async_copy(own_ref.at[at, :], res_hbm.at[at, :], sems.at[i])
        save.start()
        saves.append(save)
    for save in saves:
        save.wait()


def window(index, count, cols):
    part = cols // count
    width = min(cols, part + (LANES if count == 2 else 2 * LANES))
    return jnp.clip(index * part - LANES, 0, cols - width), width


def inverse_kernel(
    count,
    res_ref,
    sel_ref,
    row_ref,
    twist_ref,
    mat_ref,
    sky_hbm,
    beam_hbm,
    keep_ref,
    *rest,
):
    send_refs = rest[: count - 1]
    sky_ref, beam_ref, lines_ref, shift_ref, sems = rest[count - 1 :]
    rows, cols = beam_ref.shape
    outer = cols // LANES
    me = lax.axis_index("freq")
    start, width = window(me, count, cols)
    sky_part = sky_hbm.at[:, pl.ds(pl.multiple_of(start, LANES), width)]
    loads = [
        pltpu.make_async_copy(beam_hbm, beam_ref, sems.at[0]),
        pltpu.make_async_copy(sky_part, sky_ref, sems.at[1]),
    ]
    for load in loads:
        load.start()
    grid = mm(res_ref[...], sel_ref[...], ((0,), (0,)))
    blocks = []
    for w in range(outer):
        blocks.append(
            jnp.concatenate(
                [
                    jnp.concatenate(
                        [
                            grid[
                                e * 256 + w * S : e * 256 + (w + 1) * S,
                                r * LANES : (r + 1) * LANES,
                            ]
                            for e in range(2)
                        ],
                        axis=1,
                    )
                    for r in range(rows // S)
                ],
                axis=0,
            )
        )
    high, low = split(jnp.concatenate(blocks, axis=0))
    mat_high, mat_low = mat_ref[0], mat_ref[1]
    mid = mm(high, mat_high) + mm(low, mat_high) + mm(high, mat_low)
    lines = []
    for w in range(outer):
        re = mid[w * rows : (w + 1) * rows, :LANES]
        im = mid[w * rows : (w + 1) * rows, LANES:]
        tr, ti = twist_ref[0, w : w + 1, :], twist_ref[1, w : w + 1, :]
        lines.append((re * tr - im * ti, re * ti + im * tr))
    spread = dft16(lines, 1)
    for i, pair in enumerate(spread):
        for e in range(2):
            high, low = split(pair[e])
            lines_ref[e * rows : (e + 1) * rows, i * LANES : (i + 1) * LANES] = high
            lines_ref[(2 + e) * rows : (3 + e) * rows, i * LANES : (i + 1) * LANES] = low
    back = mm(row_ref[:, : 4 * rows], lines_ref[...]) + mm(
        row_ref[:, 4 * rows :], lines_ref[: 2 * rows, :]
    )
    for load in loads:
        load.wait()
    shift_ref[...] = back * beam_ref[...] * (-STEP)
    for d in range(count):
        start, width = window(lax.rem(me + d, count), count, cols)
        at = pl.ds(pl.multiple_of(start, LANES), width)
        if d == 0:
            keep_ref[...] = shift_ref[:, at] + sky_ref[...]
        else:
            send_refs[d - 1][...] = shift_ref[:, at].astype(BF16)


def sum_kernel(keep_ref, *refs):
    main_ref, near_ref, far_ref = refs[-3:]
    rows = keep_ref.shape[0]
    main = keep_ref[...]
    for ref in refs[:-3]:
        main = main + ref[...].astype(F32)
    main_ref[...] = main
    even = (lax.axis_index("facet") & 1) == 0
    top, bottom = main[0:2], main[rows - 2 : rows]
    near_ref[...] = jnp.where(even, bottom, top)
    far_ref[...] = jnp.where(even, top, bottom)


def prepare(first_ref, bias_ref, second_ref, one_ref, two_ref):
    hidden = first_ref.shape[2]
    depth = one_ref.shape[1]
    full = (BAND + 2) * 9
    bias_high, bias_low = split(bias_ref[...])
    line = iota((8, depth), 0)
    lane = iota((8, depth), 1)
    group = lane * 2731 >> 16
    term = group * 86 >> 8
    col = group - term * 3
    taps = one_hot(((line == col) & (term < 2)) | ((line - 3 == col) & (term == 2)))
    ends = one_hot(((line == 6) & (lane == full)) | ((line == 7) & (lane == full + 1)))
    values = []
    for a in range(3):
        high, low = split(first_ref[a])
        pieces = [high, low, bias_high, bias_low]
        weights = jnp.concatenate([p.astype(F32) for p in pieces], axis=0).astype(BF16)
        values.append(mm(weights, taps, ((0,), (0,))))
        if a == 0:
            offset = mm(weights, ends, ((0,), (0,)))
    lane = iota((hidden, depth), 1)
    yin = lane - (lane * 2731 >> 16) * (BAND + 2)
    for y in range(BAND):
        block = offset
        for a in range(3):
            block = block + jnp.where(yin == y + a, values[a], 0.0)
        one_ref[y * hidden : (y + 1) * hidden, :] = block.astype(BF16)

    wide = two_ref.shape[1]
    tall = BAND + 2
    expand = one_hot(iota((hidden, wide), 0) == (iota((hidden, wide), 1) & (hidden - 1)))
    pieces = [split(second_ref[a]) for a in range(3)]
    gap = iota((tall, wide), 1) // hidden + 2 - iota((tall, wide), 0)
    blocks = []
    for half in range(2):
        lines = [mm(pieces[a][half], expand) for a in range(3)]
        for b in range(3):
            total = jnp.zeros((tall, wide), F32)
            for a in range(3):
                total = jnp.where(gap == a, lines[a][b : b + 1, :], total)
            blocks.append(total)
    two_ref[...] = jnp.concatenate(blocks, axis=0).astype(BF16)


def band_prior(band, one_ref, two_ref, trim=None):
    tall, width = band.shape
    lane = iota((tall, width), 1)
    ones = jnp.where(iota((8, width), 0) < 2, 1.0, 0.0)
    high = band.astype(BF16).astype(F32)
    low = band - high

    def moved(value):
        return (
            jnp.where(lane == 0, 0.0, pltpu.roll(value, 1, 1)),
            jnp.where(lane == width - 1, 0.0, pltpu.roll(value, width - 1, 1)),
        )

    shifted = []
    for value in (high, low):
        left, right = moved(value)
        shifted.append([left, value, right])
    stack = jnp.concatenate(shifted[0] + shifted[1] + shifted[0] + [ones], axis=0).astype(BF16)
    hidden = jnp.maximum(mm(one_ref[...], stack), 0.0)
    if trim is not None:
        inner = one_ref.shape[0] // BAND
        first, last = trim
        hidden = jnp.concatenate(
            [
                jnp.where(first, 0.0, hidden[:inner]),
                hidden[inner:-inner],
                jnp.where(last, 0.0, hidden[-inner:]),
            ],
            axis=0,
        )
    taps = mm(two_ref[...], hidden.astype(BF16))
    parts = [
        taps[b * tall : (b + 1) * tall] + taps[(3 + b) * tall : (4 + b) * tall] for b in range(3)
    ]
    return parts[1] + moved(parts[0])[0] + moved(parts[2])[1]


def prior_kernel(main_ref, near_ref, one_ref, two_ref, sum_ref, base_ref):
    rows, width = main_ref.shape
    tall = BAND + 2
    main, near = main_ref[...], near_ref[...]
    even = (lax.axis_index("facet") & 1) == 0
    base_ref[8 : rows + 8, :] = main
    base_ref[6:8, :] = near
    base_ref[rows + 8 : rows + 10, :] = near
    sum_ref[0:8, :] = jnp.zeros((8, width), F32)
    sum_ref[8 : rows + 8, :] = main
    sum_ref[rows + 8 :, :] = jnp.zeros((8, width), F32)
    spots = [slice(k * BAND + 6, k * BAND + 6 + tall) for k in range((rows + 2) // BAND)]
    for spot in spots[1:-1]:
        share = band_prior(base_ref[spot, :], one_ref, two_ref)
        sum_ref[spot, :] = sum_ref[spot, :] + share
    band = jnp.where(even, base_ref[spots[-1], :], base_ref[spots[0], :])
    share = band_prior(band, one_ref, two_ref)
    sum_ref[spots[0], :] = sum_ref[spots[0], :] + jnp.where(even, 0.0, share)
    sum_ref[spots[-1], :] = sum_ref[spots[-1], :] + jnp.where(even, share, 0.0)


def edge_kernel(count, part, sum_ref, main_ref, far_ref, one_ref, two_ref, out_ref, base_ref, all_ref):
    rows, _ = main_ref.shape
    tall = BAND + 2
    place = lax.axis_index("facet")
    last = lax.axis_size("facet") - 1
    even = (place & 1) == 0
    far = far_ref[...]
    base_ref[0:2, :] = far
    base_ref[2:tall, :] = main_ref[0:BAND, :]
    base_ref[32 : 32 + BAND, :] = main_ref[rows - BAND : rows, :]
    base_ref[32 + BAND : 32 + tall, :] = far
    band = jnp.where(even, base_ref[0:tall, :], base_ref[32 : 32 + tall, :])
    share = band_prior(band, one_ref, two_ref, (place == 0, place == last))
    all_ref[...] = sum_ref[...]
    head, tail = slice(6, 6 + tall), slice(rows + 10 - tall, rows + 10)
    all_ref[head, :] = all_ref[head, :] + jnp.where(even, share, 0.0)
    all_ref[tail, :] = all_ref[tail, :] + jnp.where(even, 0.0, share)
    me = lax.axis_index("freq")
    start, _ = window(me, count, part * count)
    out_ref[...] = all_ref[8 : rows + 8, pl.ds(pl.multiple_of(me * part - start, LANES), part)]


def unpack_kernel(dest_ref, back_ref, out_ref):
    tiles = dest_ref.shape[1]
    total, width = back_ref.shape
    placing = one_hot(iota((total, tiles), 0) == dest_ref[...])
    mine = mm(placing, back_ref[...], ((0,), (0,))).astype(BF16)
    out_ref[...] = mm(mine, swap_matrix(width)).astype(BF16)


def shape(dims, dtype):
    return jax.ShapeDtypeStruct(dims, dtype)


def call(kernel, out_shape, flops, scratch=(), loaded=(), saved=(), limit=16):
    near = pl.BlockSpec(memory_space=pltpu.VMEM)
    far = pl.BlockSpec(memory_space=pltpu.HBM)

    def run(*args):
        return pl.pallas_call(
            kernel,
            out_shape=out_shape,
            in_specs=[far if i in loaded else near for i in range(len(args))],
            out_specs=[far if i in saved else near for i in range(len(out_shape))]
            if isinstance(out_shape, list)
            else near,
            scratch_shapes=scratch,
            compiler_params=pltpu.CompilerParams(vmem_limit_bytes=limit << 20),
            cost_estimate=pl.CostEstimate(flops=flops, bytes_accessed=4 << 20, transcendentals=0),
        )(*args)

    return run


def on_device(sky, beam, observed, facet_of, tile_slot, conv_first, bias_first, conv_second):
    rows, cols = sky.shape
    beam = beam.reshape(rows, cols)
    facets = lax.axis_size("facet")
    count = lax.axis_size("freq")
    tiles, width = observed.shape
    cap = 2 * tiles // facets
    total = facets * cap
    slots = (rows // S) * (cols // S)
    hidden = conv_first.shape[0]
    row_f, twist_f, mat_f = tables(rows, cols, -1)
    row_b, twist_b, mat_b = tables(rows, cols, 1)

    deep = (width // LANES) * cap + 8
    send, dest = call(
        functools.partial(pack_kernel, facets, cap),
        [shape((facets, deep, LANES), BF16), shape((1, tiles), jnp.int32)],
        1 << 28,
        scratch=[
            pltpu.VMEM((1, tiles), jnp.int32),
            pltpu.VMEM((1, tiles), jnp.int32),
            pltpu.VMEM((tiles, width), BF16),
            pltpu.SemaphoreType.DMA((3,)),
        ],
        loaded=(0, 1, 2),
    )(
        *(
            pltpu.with_memory_space_constraint(value, pltpu.HBM)
            for value in (facet_of.reshape(1, tiles), tile_slot.reshape(1, tiles), observed)
        )
    )
    got = lax.all_to_all(send, "facet", split_axis=0, concat_axis=0, tiled=True)

    high, low, first, second = call(
        forward_kernel,
        [
            shape((width, slots), BF16),
            shape((width, slots), BF16),
            shape((hidden * BAND, 9 * (BAND + 2) + 8), BF16),
            shape((6 * (BAND + 2), hidden * BAND), BF16),
        ],
        1 << 30,
    )(
        sky,
        beam,
        row_f,
        twist_f,
        mat_f,
        conv_first.transpose(1, 2, 0),
        bias_first.reshape(1, hidden),
        conv_second.transpose(1, 2, 0),
    )

    residual, select, own = call(
        functools.partial(residual_kernel, facets, cap),
        [shape((total, width), BF16), shape((total, slots), BF16), shape((total, width), BF16)],
        1 << 30,
        scratch=[pltpu.SemaphoreType.DMA((4,))],
        saved=(0,),
    )(got, *(pltpu.with_memory_space_constraint(value, pltpu.VMEM) for value in (high, low)))
    returned = lax.all_to_all(
        residual.reshape(facets, cap, width), "facet", split_axis=0, concat_axis=0, tiled=True
    ).reshape(total, width)

    _, wide = window(0, count, cols)
    keep, *sends = call(
        functools.partial(inverse_kernel, count),
        [shape((rows, wide), F32)] + [shape((rows, wide), BF16)] * (count - 1),
        1 << 30,
        scratch=[
            pltpu.VMEM((rows, wide), F32),
            pltpu.VMEM((rows, cols), F32),
            pltpu.VMEM((4 * rows, cols), BF16),
            pltpu.VMEM((rows, cols), F32),
            pltpu.SemaphoreType.DMA((2,)),
        ],
        loaded=(5, 6),
    )(
        own,
        select,
        row_b,
        twist_b,
        mat_b,
        *(pltpu.with_memory_space_constraint(value, pltpu.HBM) for value in (sky, beam)),
    )

    def beside(value, to):
        pairs = [(p, to(p)) for p in range(facets) if 0 <= to(p) < facets]
        return lax.ppermute(value, "facet", pairs)

    gots = [
        lax.ppermute(value, "freq", [(f, (f + d + 1) % count) for f in range(count)])
        for d, value in enumerate(sends)
    ]
    main, near, far = call(
        sum_kernel,
        [shape((rows, wide), F32), shape((2, wide), F32), shape((2, wide), F32)],
        1 << 24,
    )(keep, *gots)
    far = beside(far, lambda p: p + 1 if p & 1 else p - 1)
    near = beside(near, lambda p: p ^ 1)
    tall_rows = pltpu.VMEM((rows + 16, wide), F32)
    partial = call(
        prior_kernel, shape((rows + 16, wide), F32), 1 << 31, scratch=[tall_rows]
    )(main, near, first, second)
    image = call(
        functools.partial(edge_kernel, count, cols // count),
        shape((rows, cols // count), F32),
        1 << 30,
        scratch=[pltpu.VMEM((64, wide), F32), tall_rows],
    )(partial, main, far, first, second)

    tiles_out = call(unpack_kernel, shape((tiles, width), BF16), 1 << 28)(dest, returned)
    return tiles_out, image


def solution(mesh):
    placed = (
        P("facet", None),
        P("freq", "facet", None),
        P(("freq", "facet"), None),
        P(("freq", "facet")),
        P(("freq", "facet")),
        P(),
        P(),
        P(),
    )

    return jax.shard_map(
        on_device,
        mesh=mesh,
        in_specs=placed,
        out_specs=(P(("freq", "facet"), None), P("facet", "freq")),
        check_vma=False,
    )
```

profile of v0, /device:TPU:1, one launch (start us, length us, event | category | flops | bytes accessed | tf_op | source)
XLA Modules:
  0.0 49.6 jit_solution(7856333584908086913)
XLA Ops:
  0.6 0.0 copy-start.6
  0.6 0.0 copy-start.7
  0.7 2.6 %shard_map.149 = (bf16[16,136,128]{2,1,0:T(8,128)(2,1)}, s32[1,256]{1,0:T(1,128)S(1)}) custom-call(s32[1,256]{1,0:T(1,128)} %bitcast.14, s32[1,256]{1,0:T(1,128)} %bitcast.15, bf16[256,512]{1,0:T(8,128)(2,1)} %seen_hbm.1), custom_call_target="tpu_custom_call" | custom-call | flops 268435456 | bytes 4194304 | tf_op jit(solution)/shard_map/pallas_call | solution.py:478
  3.3 0.0 copy-start
  3.3 0.0 copy-start.1
  3.3 0.0 copy-start.3
  3.3 0.0 copy-start.10
  3.3 7.5 %all-to-all-start = ((bf16[16,136,128]{2,1,0:T(8,128)(2,1)}), bf16[16,136,128]{2,1,0:T(8,128)(2,1)S(1)}, u32[]{:S(2)}, u32[]{:S(2)}) async-start(bf16[16,136,128]{2,1,0:T(8,128)(2,1)} %get-tuple-element.17), calls=%async_computation | async-start | bytes 1114112 | tf_op jit(solution)/shard_map/all_to_all | solution.py:524
  10.8 0.0 copy-start.2
  10.8 0.0 copy-start.4
  10.8 0.0 copy-done.6
  10.8 0.0 copy-done.7
  10.8 0.0 copy-done
  10.8 0.0 copy-done.1
  10.8 0.0 copy-done.3
  10.9 0.0 copy-done.10
  10.9 0.6 %copy-done.2 = f32[32,3,3]{0,2,1:T(4,128)S(1)} copy-done((f32[32,3,3]{0,2,1:T(4,128)S(1)}, f32[32,3,3]{0,2,1:T(4,128)}, u32[]{:S(2)}) %copy-start.2) | copy-done | bytes 1176
  11.5 0.0 copy-done.4
  11.5 1.4 %shard_map.150 = (bf16[512,512]{1,0:T(8,128)(2,1)S(1)}, bf16[512,512]{1,0:T(8,128)(2,1)S(1)}, bf16[704,224]{1,0:T(8,128)(2,1)S(1)}, bf16[144,704]{1,0:T(8,128)(2,1)S(1)}) custom-call(f32[64,2048]{1,0:T(8,128)S(1)} %copy-done, f32[64,2048]{1,0:T(8,128)S(1)} %bitcast.10, bf16[128,192]{1,0:T(8,128)(2,1)S(1)} %copy-done.7, f32[2,16,128]{2,1,0:T(8,128)S(1)} %copy-done.10, ...), custom_call_target="tpu_custom_call" | custom-call | flops 1073741824 | bytes 4194304 | tf_op jit(solution)/shard_map/pallas_call | solution.py:478
  12.9 0.0 copy-start.11
  12.9 0.7 %copy-done.11 = bf16[144,704]{1,0:T(8,128)(2,1)} copy-done((bf16[144,704]{1,0:T(8,128)(2,1)}, bf16[144,704]{1,0:T(8,128)(2,1)S(1)}, u32[]{:S(2)}) %copy-start.11) | copy-done | bytes 202776
  13.6 11.8 %all-to-all-done.got_ref = bf16[16,136,128]{2,1,0:T(8,128)(2,1)S(1)} async-done(((bf16[16,136,128]{2,1,0:T(8,128)(2,1)}), bf16[16,136,128]{2,1,0:T(8,128)(2,1)S(1)}, u32[]{:S(2)}, u32[]{:S(2)}) %all-to-all-start) | async-done | bytes 557088 | tf_op jit(solution)/shard_map/all_to_all | solution.py:524
  25.4 1.8 %shard_map.151 = (bf16[512,512]{1,0:T(8,128)(2,1)}, bf16[512,512]{1,0:T(8,128)(2,1)S(1)}, bf16[512,512]{1,0:T(8,128)(2,1)S(1)}) custom-call(bf16[16,136,128]{2,1,0:T(8,128)(2,1)S(1)} %all-to-all-done.got_ref, bf16[512,512]{1,0:T(8,128)(2,1)S(1)} %get-tuple-element.18.high_ref, bf16[512,512]{1,0:T(8,128)(2,1)S(1)} %get-tuple-element.19.low_ref), custom_call_target="tpu_custom_call" | custom-call | flops 1073741824 | bytes 4194304 | tf_op jit(solution)/shard_map/pallas_call | solution.py:478
  27.2 0.0 copy-start.5
  27.2 0.0 copy-start.8
  27.2 0.0 copy-start.9
  27.3 4.7 %all-to-all-start.1 = ((bf16[16,32,512]{2,1,0:T(8,128)(2,1)}), bf16[16,32,512]{2,1,0:T(8,128)(2,1)S(1)}, u32[]{:S(2)}, u32[]{:S(2)}) async-start(bf16[16,32,512]{2,1,0:T(8,128)(2,1)} %bitcast.6), calls=%async_computation.1 | async-start | bytes 1048576 | tf_op jit(solution)/shard_map/all_to_all | solution.py:553
  32.0 0.0 copy-done.5
  32.0 0.0 copy-done.8
  32.0 0.0 copy-done.9
  32.0 2.9 %shard_map.153 = (f32[64,1152]{1,0:T(8,128)S(1)}, bf16[64,1152]{1,0:T(8,128)(2,1)S(1)}) custom-call(bf16[512,512]{1,0:T(8,128)(2,1)S(1)} %get-tuple-element.21.res_ref, bf16[512,512]{1,0:T(8,128)(2,1)S(1)} %get-tuple-element.22.sel_ref, bf16[64,384]{1,0:T(8,128)(2,1)S(1)} %copy-done.8, f32[2,16,128]{2,1,0:T(8,128)S(1)} %copy-done.9, ...), custom_call_target="tpu_custom_call" | custom-call | flops 1073741824 | bytes 4194304 | tf_op jit(solution)/shard_map/pallas_call | solution.py:478
  34.9 1.3 %collective-permute-start = (bf16[64,1152]{1,0:T(8,128)(2,1)S(1)}, bf16[64,1152]{1,0:T(8,128)(2,1)S(1)}, u32[]{:S(2)}, u32[]{:S(2)}) collective-permute-start(bf16[64,1152]{1,0:T(8,128)(2,1)S(1)} %get-tuple-element.24), channel_id=1, source_target_pairs={{0,16},{16,0},{1,17},{17,1},{2,18},{18,2},{3,19},{19,3},{4,20},{20... | collective-permute-start | bytes 442376 | tf_op jit(solution)/shard_map/ppermute | solution.py:584
  36.2 4.1 %collective-permute-done.refs_0_ = bf16[64,1152]{1,0:T(8,128)(2,1)S(1)} collective-permute-done((bf16[64,1152]{1,0:T(8,128)(2,1)S(1)}, bf16[64,1152]{1,0:T(8,128)(2,1)S(1)}, u32[]{:S(2)}, u32[]{:S(2)}) %collective-permute-start) | collective-permute-done | bytes 147488 | tf_op jit(solution)/shard_map/ppermute | solution.py:584
  40.3 0.0 copy-start.12
  40.3 1.0 %collective-permute-start.1 = (f32[2,1152]{1,0:T(2,128)S(1)}, f32[2,1152]{1,0:T(2,128)S(1)}, u32[]{:S(2)}, u32[]{:S(2)}) collective-permute-start(f32[2,1152]{1,0:T(2,128)S(1)} %get-tuple-element.26), channel_id=1, source_target_pairs={{0,1},{1,0},{2,3},{3,2},{4,5},{5,4},{6,7},{7,6},{8,9},{9,8},{10,11... | collective-permute-start | bytes 27656 | tf_op jit(solution)/shard_map/ppermute | solution.py:581
  41.3 3.2 %collective-permute-start.2 = (f32[2,1152]{1,0:T(2,128)S(1)}, f32[2,1152]{1,0:T(2,128)S(1)}, u32[]{:S(2)}, u32[]{:S(2)}) collective-permute-start(f32[2,1152]{1,0:T(2,128)S(1)} %get-tuple-element.29), channel_id=1, source_target_pairs={{1,2},{2,1},{3,4},{4,3},{5,6},{6,5},{7,8},{8,7},{9,10},{10,9},{11,... | collective-permute-start | bytes 27656 | tf_op jit(solution)/shard_map/ppermute | solution.py:581
  44.5 0.0 collective-permute-done.1.near_ref
  44.5 0.0 copy-done.12
  44.5 1.9 %shard_map.155.sum_ref = f32[80,1152]{1,0:T(8,128)S(1)} custom-call(f32[64,1152]{1,0:T(8,128)S(1)} %get-tuple-element.25.main_ref, f32[2,1152]{1,0:T(2,128)S(1)} %collective-permute-done.1.near_ref, bf16[704,224]{1,0:T(8,128)(2,1)S(1)} %get-tuple-element.27.one_ref, bf16[144,704]{1,0:T(8,128)(2,1)S(1)} %copy-done.12), custom_call_target="tpu_custom_call" | custom-call | flops 2147483648 | bytes 4194304 | tf_op jit(solution)/shard_map/pallas_call | solution.py:478
  46.5 0.0 collective-permute-done.2.far_ref
  46.5 1.8 %shard_map.156 = f32[64,1024]{1,0:T(8,128)} custom-call(f32[80,1152]{1,0:T(8,128)S(1)} %shard_map.155.sum_ref, f32[64,1152]{1,0:T(8,128)S(1)} %get-tuple-element.25.main_ref, f32[2,1152]{1,0:T(2,128)S(1)} %collective-permute-done.2.far_ref, bf16[704,224]{1,0:T(8,128)(2,1)S(1)} %get-tuple-element.27.one_ref, bf16[144,704]{1,0:T(8,128)(2,1)S(1)} %copy-done.12), custom_call_target="tpu_custom_call" | custom-call | flops 1073741824 | bytes 4194304 | tf_op jit(solution)/shard_map/pallas_call | solution.py:478
  48.3 0.0 all-to-all-done.1
  48.3 1.3 %shard_map.152 = bf16[256,512]{1,0:T(8,128)(2,1)} custom-call(s32[1,256]{1,0:T(1,128)S(1)} %get-tuple-element.16.dest_ref, bf16[512,512]{1,0:T(8,128)(2,1)S(1)} %bitcast.8), custom_call_target="tpu_custom_call" | custom-call | flops 268435456 | bytes 4194304 | tf_op jit(solution)/shard_map/pallas_call | solution.py:478
  (1 shorter events, 0.0 us)
Async XLA Ops:
  0.6 10.2 %copy-start.6 = (bf16[2,256,256]{2,1,0:T(8,128)(2,1)S(1)}, bf16[2,256,256]{2,1,0:T(8,128)(2,1)}, u32[]{:S(2)}) copy-start(bf16[2,256,256]{2,1,0:T(8,128)(2,1)} %constant.14.clone.mat_ref) | copy-start | bytes 786436
  0.6 10.2 %copy-start.7 = (bf16[128,192]{1,0:T(8,128)(2,1)S(1)}, bf16[128,192]{1,0:T(8,128)(2,1)}, u32[]{:S(2)}) copy-start(bf16[128,192]{1,0:T(8,128)(2,1)} %constant.12.clone.row_ref) | copy-start | bytes 147460
  3.3 7.5 %copy-start = (f32[64,2048]{1,0:T(8,128)S(1)}, f32[64,2048]{1,0:T(8,128)}, u32[]{:S(2)}) copy-start(f32[64,2048]{1,0:T(8,128)} %sky_hbm.1) | copy-start | bytes 1572868
  3.3 7.5 %copy-start.1 = (f32[1,64,2048]{2,1,0:T(8,128)S(1)}, f32[1,64,2048]{2,1,0:T(8,128)}, u32[]{:S(2)}) copy-start(f32[1,64,2048]{2,1,0:T(8,128)} %param.15) | copy-start | bytes 1572868
  3.3 7.5 %copy-start.3 = (f32[32,3,3]{0,2,1:T(4,128)S(1)}, f32[32,3,3]{0,2,1:T(4,128)}, u32[]{:S(2)}) copy-start(f32[32,3,3]{0,2,1:T(4,128)} %param.21) | copy-start | bytes 3460
  3.3 7.5 %copy-start.10 = (f32[2,16,128]{2,1,0:T(8,128)S(1)}, f32[2,16,128]{2,1,0:T(8,128)}, u32[]{:S(2)}) copy-start(f32[2,16,128]{2,1,0:T(8,128)} %constant.13.clone.twist_ref) | copy-start | bytes 49156
  3.3 22.0 %all-to-all-start = ((bf16[16,136,128]{2,1,0:T(8,128)(2,1)}), bf16[16,136,128]{2,1,0:T(8,128)(2,1)S(1)}, u32[]{:S(2)}, u32[]{:S(2)}) async-start(bf16[16,136,128]{2,1,0:T(8,128)(2,1)} %get-tuple-element.17), calls=%async_computation | async-start | bytes 1114112 | tf_op jit(solution)/shard_map/all_to_all | solution.py:524
  10.8 0.7 %copy-start.2 = (f32[32,3,3]{0,2,1:T(4,128)S(1)}, f32[32,3,3]{0,2,1:T(4,128)}, u32[]{:S(2)}) copy-start(f32[32,3,3]{0,2,1:T(4,128)} %param.19) | copy-start | bytes 3460
  10.8 0.7 %copy-start.4 = (f32[32]{0:T(128)S(1)}, f32[32]{0:T(128)}, u32[]{:S(2)}) copy-start(f32[32]{0:T(128)} %param.20) | copy-start | bytes 388
  12.9 0.7 %copy-start.11 = (bf16[144,704]{1,0:T(8,128)(2,1)}, bf16[144,704]{1,0:T(8,128)(2,1)S(1)}, u32[]{:S(2)}) copy-start(bf16[144,704]{1,0:T(8,128)(2,1)S(1)} %get-tuple-element.28.two_ref) | copy-start | bytes 608260
  27.2 4.7 %copy-start.5 = (bf16[2,256,256]{2,1,0:T(8,128)(2,1)S(1)}, bf16[2,256,256]{2,1,0:T(8,128)(2,1)}, u32[]{:S(2)}) copy-start(bf16[2,256,256]{2,1,0:T(8,128)(2,1)} %constant.17.clone.mat_ref) | copy-start | bytes 786436
  27.2 4.7 %copy-start.8 = (bf16[64,384]{1,0:T(8,128)(2,1)S(1)}, bf16[64,384]{1,0:T(8,128)(2,1)}, u32[]{:S(2)}) copy-start(bf16[64,384]{1,0:T(8,128)(2,1)} %constant.15.clone.row_ref) | copy-start | bytes 147460
  27.2 4.7 %copy-start.9 = (f32[2,16,128]{2,1,0:T(8,128)S(1)}, f32[2,16,128]{2,1,0:T(8,128)}, u32[]{:S(2)}) copy-start(f32[2,16,128]{2,1,0:T(8,128)} %constant.16.clone.twist_ref) | copy-start | bytes 49156
  27.3 21.0 %all-to-all-start.1 = ((bf16[16,32,512]{2,1,0:T(8,128)(2,1)}), bf16[16,32,512]{2,1,0:T(8,128)(2,1)S(1)}, u32[]{:S(2)}, u32[]{:S(2)}) async-start(bf16[16,32,512]{2,1,0:T(8,128)(2,1)} %bitcast.6), calls=%async_computation.1 | async-start | bytes 1048576 | tf_op jit(solution)/shard_map/all_to_all | solution.py:553
  34.9 5.4 %collective-permute-start = (bf16[64,1152]{1,0:T(8,128)(2,1)S(1)}, bf16[64,1152]{1,0:T(8,128)(2,1)S(1)}, u32[]{:S(2)}, u32[]{:S(2)}) collective-permute-start(bf16[64,1152]{1,0:T(8,128)(2,1)S(1)} %get-tuple-element.24), channel_id=1, source_target_pairs={{0,16},{16,0},{1,17},{17,1},{2,18},{18,2},{3,19},{19,3},{4,20},{20... | collective-permute-start | bytes 442376 | tf_op jit(solution)/shard_map/ppermute | solution.py:584
  40.3 4.3 %copy-start.12 = (bf16[144,704]{1,0:T(8,128)(2,1)S(1)}, bf16[144,704]{1,0:T(8,128)(2,1)}, u32[]{:S(2)}) copy-start(bf16[144,704]{1,0:T(8,128)(2,1)} %copy-done.11) | copy-start | bytes 608260
  40.3 4.2 %collective-permute-start.1 = (f32[2,1152]{1,0:T(2,128)S(1)}, f32[2,1152]{1,0:T(2,128)S(1)}, u32[]{:S(2)}, u32[]{:S(2)}) collective-permute-start(f32[2,1152]{1,0:T(2,128)S(1)} %get-tuple-element.26), channel_id=1, source_target_pairs={{0,1},{1,0},{2,3},{3,2},{4,5},{5,4},{6,7},{7,6},{8,9},{9,8},{10,11... | collective-permute-start | bytes 27656 | tf_op jit(solution)/shard_map/ppermute | solution.py:581
  41.3 5.1 %collective-permute-start.2 = (f32[2,1152]{1,0:T(2,128)S(1)}, f32[2,1152]{1,0:T(2,128)S(1)}, u32[]{:S(2)}, u32[]{:S(2)}) collective-permute-start(f32[2,1152]{1,0:T(2,128)S(1)} %get-tuple-element.29), channel_id=1, source_target_pairs={{1,2},{2,1},{3,4},{4,3},{5,6},{6,5},{7,8},{8,7},{9,10},{10,9},{11,... | collective-permute-start | bytes 27656 | tf_op jit(solution)/shard_map/ppermute | solution.py:581
where the time goes:
time: 50.1 us; the launch traced here: 49.6 us
  starting transfers between devices  17.7 us (35%)
  waiting for transfers between devices  15.8 us (32%)
  Pallas kernels  13.8 us (28%)
  local copies, waits for them, and re-layouts  1.36 us (3%)
  between operations  0.87 us (2%)
    pallas_call x8, Pallas kernels, run(): pl.pallas_call(kernel, out_shape=out_shape, in_specs=[far if i in loaded...  13.8 us
    all_to_all x1, waiting for transfers between devices, on_device(): got = lax.all_to_all(send, 'facet', split_axis=0, concat_axis=0, tiled=True)  11.8 us
    all_to_all x1, starting transfers between devices, on_device(): got = lax.all_to_all(send, 'facet', split_axis=0, concat_axis=0, tiled=True)  7.46 us
    all_to_all x1, starting transfers between devices, on_device(): lax.all_to_all(residual.reshape(facets, cap, width), 'facet', split_axis=...  4.7 us
    ppermute x2, starting transfers between devices, beside(): return lax.ppermute(value, 'facet', pairs)  4.19 us
    ppermute x1, waiting for transfers between devices, on_device(): lax.ppermute(value, 'freq', [(f, (f + d + 1) % count) for f in range(coun...  4.05 us
    unnamed x26, local copies, waits for them, and re-layouts  1.36 us
    ppermute x1, starting transfers between devices, on_device(): lax.ppermute(value, 'freq', [(f, (f + d + 1) % count) for f in range(coun...  1.31 us
  transfers between devices with their start and end apart: 5, of which 2 were waited for; matrix products, arithmetic and copies ran while one was open for 0% of the time, Pallas kernels for 16%

commit v1 on v0

--- a/solution.py
+++ b/solution.py
@@ -258,7 +258,7 @@
     *rest,
 ):
     send_refs = rest[: count - 1]
-    sky_ref, beam_ref, lines_ref, shift_ref, sems = rest[count - 1 :]
+    rim_ref, sky_ref, edge_ref, beam_ref, lines_ref, shift_ref, sems = rest[count - 1 :]
     rows, cols = beam_ref.shape
     outer = cols // LANES
     me = lax.axis_index("freq")
@@ -267,6 +267,8 @@
     loads = [
         pltpu.make_async_copy(beam_hbm, beam_ref, sems.at[0]),
         pltpu.make_async_copy(sky_part, sky_ref, sems.at[1]),
+        pltpu.make_async_copy(sky_hbm.at[0:8, :], edge_ref.at[0:8, :], sems.at[2]),
+        pltpu.make_async_copy(sky_hbm.at[rows - 8 : rows, :], edge_ref.at[8:16, :], sems.at[3]),
     ]
     for load in loads:
         load.start()
@@ -312,6 +314,9 @@
     for load in loads:
         load.wait()
     shift_ref[...] = back * beam_ref[...] * (-STEP)
+    even = (lax.axis_index("facet") & 1) == 0
+    rim_ref[0:2, :] = jnp.where(even, shift_ref[0:2, :], shift_ref[rows - 2 : rows, :])
+    rim_ref[2:4, :] = jnp.where(even, edge_ref[0:2, :], edge_ref[14:16, :])
     for d in range(count):
         start, width = window(lax.rem(me + d, count), count, cols)
         at = pl.ds(pl.multiple_of(start, LANES), width)
@@ -322,16 +327,14 @@
 
 
 def sum_kernel(keep_ref, *refs):
-    main_ref, near_ref, far_ref = refs[-3:]
+    main_ref, near_ref = refs[-2:]
     rows = keep_ref.shape[0]
     main = keep_ref[...]
-    for ref in refs[:-3]:
+    for ref in refs[:-2]:
         main = main + ref[...].astype(F32)
     main_ref[...] = main
     even = (lax.axis_index("facet") & 1) == 0
-    top, bottom = main[0:2], main[rows - 2 : rows]
-    near_ref[...] = jnp.where(even, bottom, top)
-    far_ref[...] = jnp.where(even, top, bottom)
+    near_ref[...] = jnp.where(even, main[rows - 2 : rows], main[0:2])
 
 
 def prepare(first_ref, bias_ref, second_ref, one_ref, two_ref):
@@ -436,13 +439,20 @@
     sum_ref[spots[-1], :] = sum_ref[spots[-1], :] + jnp.where(even, share, 0.0)
 
 
-def edge_kernel(count, part, sum_ref, main_ref, far_ref, one_ref, two_ref, out_ref, base_ref, all_ref):
-    rows, _ = main_ref.shape
+def edge_kernel(count, part, sum_ref, main_ref, *refs):
+    far_refs = refs[:count]
+    one_ref, two_ref, out_ref, base_ref, all_ref = refs[count:]
+    rows, width = main_ref.shape
     tall = BAND + 2
     place = lax.axis_index("facet")
     last = lax.axis_size("facet") - 1
     even = (place & 1) == 0
-    far = far_ref[...]
+    me = lax.axis_index("freq")
+    start, _ = window(me, count, part * count)
+    at = pl.ds(pl.multiple_of(start, LANES), width)
+    far = far_refs[0][2:4, at]
+    for ref in far_refs:
+        far = far + ref[0:2, at]
     base_ref[0:2, :] = far
     base_ref[2:tall, :] = main_ref[0:BAND, :]
     base_ref[32 : 32 + BAND, :] = main_ref[rows - BAND : rows, :]
@@ -453,8 +463,6 @@
     head, tail = slice(6, 6 + tall), slice(rows + 10 - tall, rows + 10)
     all_ref[head, :] = all_ref[head, :] + jnp.where(even, share, 0.0)
     all_ref[tail, :] = all_ref[tail, :] + jnp.where(even, 0.0, share)
-    me = lax.axis_index("freq")
-    start, _ = window(me, count, part * count)
     out_ref[...] = all_ref[8 : rows + 8, pl.ds(pl.multiple_of(me * part - start, LANES), part)]
 
 
@@ -555,16 +563,19 @@
     ).reshape(total, width)
 
     _, wide = window(0, count, cols)
-    keep, *sends = call(
+    keep, *shares, rim = call(
         functools.partial(inverse_kernel, count),
-        [shape((rows, wide), F32)] + [shape((rows, wide), BF16)] * (count - 1),
+        [shape((rows, wide), F32)]
+        + [shape((rows, wide), BF16)] * (count - 1)
+        + [shape((4, cols), F32)],
         1 << 30,
         scratch=[
             pltpu.VMEM((rows, wide), F32),
+            pltpu.VMEM((16, cols), F32),
             pltpu.VMEM((rows, cols), F32),
             pltpu.VMEM((4 * rows, cols), BF16),
             pltpu.VMEM((rows, cols), F32),
-            pltpu.SemaphoreType.DMA((2,)),
+            pltpu.SemaphoreType.DMA((4,)),
         ],
         loaded=(5, 6),
     )(
@@ -580,17 +591,16 @@
         pairs = [(p, to(p)) for p in range(facets) if 0 <= to(p) < facets]
         return lax.ppermute(value, "facet", pairs)
 
-    gots = [
-        lax.ppermute(value, "freq", [(f, (f + d + 1) % count) for f in range(count)])
-        for d, value in enumerate(sends)
-    ]
-    main, near, far = call(
-        sum_kernel,
-        [shape((rows, wide), F32), shape((2, wide), F32), shape((2, wide), F32)],
-        1 << 24,
+    def across(value, d):
+        return lax.ppermute(value, "freq", [(f, (f + d) % count) for f in range(count)])
+
+    gots = [across(value, d + 1) for d, value in enumerate(shares)]
+    fars = [beside(rim, lambda p: p + 1 if p & 1 else p - 1)]
+    main, near = call(
+        sum_kernel, [shape((rows, wide), F32), shape((2, wide), F32)], 1 << 24
     )(keep, *gots)
-    far = beside(far, lambda p: p + 1 if p & 1 else p - 1)
     near = beside(near, lambda p: p ^ 1)
+    fars += [across(fars[0], d) for d in range(1, count)]
     tall_rows = pltpu.VMEM((rows + 16, wide), F32)
     partial = call(
         prior_kernel, shape((rows + 16, wide), F32), 1 << 31, scratch=[tall_rows]
@@ -600,7 +610,7 @@
         shape((rows, cols // count), F32),
         1 << 30,
         scratch=[pltpu.VMEM((64, wide), F32), tall_rows],
-    )(partial, main, far, first, second)
+    )(partial, main, *fars, first, second)
 
     tiles_out = call(unpack_kernel, shape((tiles, width), BF16), 1 << 28)(dest, returned)
     return tiles_out, image

time: 50.1 us -> 52.4 us (1.046)
  the two profiles are of different devices: /device:TPU:1 before, /device:TPU:16 now
where the time goes in v1:
time: 52.4 us; the launch traced here: 52 us
  waiting for transfers between devices  18.8 us (36%)
  starting transfers between devices  17 us (32%)
  Pallas kernels  13.9 us (27%)
  local copies, waits for them, and re-layouts  1.36 us (3%)
  between operations  0.86 us (2%)
    pallas_call x8, Pallas kernels, run(): pl.pallas_call(kernel, out_shape=out_shape, in_specs=[far if i in loaded...  13.9 us
    all_to_all x1, waiting for transfers between devices, on_device(): got = lax.all_to_all(send, 'facet', split_axis=0, concat_axis=0, tiled=True)  11.7 us
    all_to_all x1, starting transfers between devices, on_device(): got = lax.all_to_all(send, 'facet', split_axis=0, concat_axis=0, tiled=True)  6.3 us
    ppermute x2, waiting for transfers between devices, beside(): return lax.ppermute(value, 'facet', pairs)  5.07 us
    all_to_all x1, starting transfers between devices, on_device(): lax.all_to_all(residual.reshape(facets, cap, width), 'facet', split_axis=...  4.72 us
    ppermute x2, starting transfers between devices, across(): lax.ppermute(value, 'freq', [(f, (f + d) % count) for f in range(count)])  3.11 us
    ppermute x2, starting transfers between devices, beside(): return lax.ppermute(value, 'facet', pairs)  2.87 us
    ppermute x2, waiting for transfers between devices, across(): lax.ppermute(value, 'freq', [(f, (f + d) % count) for f in range(count)])  2 us
  transfers between devices with their start and end apart: 6, of which 4 were waited for; matrix products, arithmetic and copies ran while one was open for 0% of the time, Pallas kernels for 16%

profile of v1, /device:TPU:16, one launch (start us, length us, event | category | flops | bytes accessed | tf_op | source)
XLA Modules:
  0.0 52.0 jit_solution(3521583854696545539)
XLA Ops:
  0.6 0.0 copy-start.6
  0.6 0.0 copy-start.7
  0.7 2.6 %shard_map.149 = (bf16[16,136,128]{2,1,0:T(8,128)(2,1)}, s32[1,256]{1,0:T(1,128)S(1)}) custom-call(s32[1,256]{1,0:T(1,128)} %bitcast.14, s32[1,256]{1,0:T(1,128)} %bitcast.15, bf16[256,512]{1,0:T(8,128)(2,1)} %seen_hbm.1), custom_call_target="tpu_custom_call" | custom-call | flops 268435456 | bytes 4194304 | tf_op jit(solution)/shard_map/pallas_call | solution.py:486
  3.3 0.0 copy-start
  3.3 0.0 copy-start.1
  3.3 0.0 copy-start.3
  3.3 0.0 copy-start.10
  3.3 6.3 %all-to-all-start = ((bf16[16,136,128]{2,1,0:T(8,128)(2,1)}), bf16[16,136,128]{2,1,0:T(8,128)(2,1)S(1)}, u32[]{:S(2)}, u32[]{:S(2)}) async-start(bf16[16,136,128]{2,1,0:T(8,128)(2,1)} %get-tuple-element.17), calls=%async_computation | async-start | bytes 1114112 | tf_op jit(solution)/shard_map/all_to_all | solution.py:532
  9.6 0.0 copy-start.2
  9.7 0.0 copy-start.4
  9.7 0.0 copy-done.6
  9.7 0.0 copy-done.7
  9.7 0.0 copy-done
  9.7 0.0 copy-done.1
  9.7 0.0 copy-done.3
  9.7 0.0 copy-done.10
  9.7 0.6 %copy-done.2 = f32[32,3,3]{0,2,1:T(4,128)S(1)} copy-done((f32[32,3,3]{0,2,1:T(4,128)S(1)}, f32[32,3,3]{0,2,1:T(4,128)}, u32[]{:S(2)}) %copy-start.2) | copy-done | bytes 1176
  10.3 0.0 copy-done.4
  10.3 1.4 %shard_map.150 = (bf16[512,512]{1,0:T(8,128)(2,1)S(1)}, bf16[512,512]{1,0:T(8,128)(2,1)S(1)}, bf16[704,224]{1,0:T(8,128)(2,1)S(1)}, bf16[144,704]{1,0:T(8,128)(2,1)S(1)}) custom-call(f32[64,2048]{1,0:T(8,128)S(1)} %copy-done, f32[64,2048]{1,0:T(8,128)S(1)} %bitcast.10, bf16[128,192]{1,0:T(8,128)(2,1)S(1)} %copy-done.7, f32[2,16,128]{2,1,0:T(8,128)S(1)} %copy-done.10, ...), custom_call_target="tpu_custom_call" | custom-call | flops 1073741824 | bytes 4194304 | tf_op jit(solution)/shard_map/pallas_call | solution.py:486
  11.8 0.0 copy-start.11
  11.8 0.7 %copy-done.11 = bf16[144,704]{1,0:T(8,128)(2,1)} copy-done((bf16[144,704]{1,0:T(8,128)(2,1)}, bf16[144,704]{1,0:T(8,128)(2,1)S(1)}, u32[]{:S(2)}) %copy-start.11) | copy-done | bytes 202776
  12.5 11.7 %all-to-all-done.got_ref = bf16[16,136,128]{2,1,0:T(8,128)(2,1)S(1)} async-done(((bf16[16,136,128]{2,1,0:T(8,128)(2,1)}), bf16[16,136,128]{2,1,0:T(8,128)(2,1)S(1)}, u32[]{:S(2)}, u32[]{:S(2)}) %all-to-all-start) | async-done | bytes 557088 | tf_op jit(solution)/shard_map/all_to_all | solution.py:532
  24.2 1.8 %shard_map.151 = (bf16[512,512]{1,0:T(8,128)(2,1)}, bf16[512,512]{1,0:T(8,128)(2,1)S(1)}, bf16[512,512]{1,0:T(8,128)(2,1)S(1)}) custom-call(bf16[16,136,128]{2,1,0:T(8,128)(2,1)S(1)} %all-to-all-done.got_ref, bf16[512,512]{1,0:T(8,128)(2,1)S(1)} %get-tuple-element.18.high_ref, bf16[512,512]{1,0:T(8,128)(2,1)S(1)} %get-tuple-element.19.low_ref), custom_call_target="tpu_custom_call" | custom-call | flops 1073741824 | bytes 4194304 | tf_op jit(solution)/shard_map/pallas_call | solution.py:486
  26.1 0.0 copy-start.5
  26.1 0.0 copy-start.8
  26.1 0.0 copy-start.9
  26.1 4.7 %all-to-all-start.1 = ((bf16[16,32,512]{2,1,0:T(8,128)(2,1)}), bf16[16,32,512]{2,1,0:T(8,128)(2,1)S(1)}, u32[]{:S(2)}, u32[]{:S(2)}) async-start(bf16[16,32,512]{2,1,0:T(8,128)(2,1)} %bitcast.6), calls=%async_computation.1 | async-start | bytes 1048576 | tf_op jit(solution)/shard_map/all_to_all | solution.py:561
  30.8 0.0 copy-done.5
  30.8 0.0 copy-done.8
  30.8 0.0 copy-done.9
  30.8 3.0 %shard_map.153 = (f32[64,1152]{1,0:T(8,128)S(1)}, bf16[64,1152]{1,0:T(8,128)(2,1)S(1)}, f32[4,2048]{1,0:T(4,128)S(1)}) custom-call(bf16[512,512]{1,0:T(8,128)(2,1)S(1)} %get-tuple-element.21.res_ref, bf16[512,512]{1,0:T(8,128)(2,1)S(1)} %get-tuple-element.22.sel_ref, bf16[64,384]{1,0:T(8,128)(2,1)S(1)} %copy-done.8, f32[2,16,128]{2,1,0:T(8,128)S(1)} %copy-done.9, ...), custom_call_target="tpu_custom_call" | custom-call | flops 1073741824 | bytes 4194304 | tf_op jit(solution)/shard_map/pallas_call | solution.py:486
  33.8 1.6 %collective-permute-start = (bf16[64,1152]{1,0:T(8,128)(2,1)S(1)}, bf16[64,1152]{1,0:T(8,128)(2,1)S(1)}, u32[]{:S(2)}, u32[]{:S(2)}) collective-permute-start(bf16[64,1152]{1,0:T(8,128)(2,1)S(1)} %get-tuple-element.24), channel_id=1, source_target_pairs={{0,16},{16,0},{1,17},{17,1},{2,18},{18,2},{3,19},{19,3},{4,20},{20... | collective-permute-start | bytes 442376 | tf_op jit(solution)/shard_map/ppermute | solution.py:595
  35.4 2.8 %collective-permute-start.2 = (f32[4,2048]{1,0:T(4,128)S(1)}, f32[4,2048]{1,0:T(4,128)S(1)}, u32[]{:S(2)}, u32[]{:S(2)}) collective-permute-start(f32[4,2048]{1,0:T(4,128)S(1)} %get-tuple-element.29), channel_id=1, source_target_pairs={{1,2},{2,1},{3,4},{4,3},{5,6},{6,5},{7,8},{8,7},{9,10},{10,9},{11,... | collective-permute-start | bytes 98312 | tf_op jit(solution)/shard_map/ppermute | solution.py:592
  38.2 1.5 %collective-permute-done.refs_0_ = bf16[64,1152]{1,0:T(8,128)(2,1)S(1)} collective-permute-done((bf16[64,1152]{1,0:T(8,128)(2,1)S(1)}, bf16[64,1152]{1,0:T(8,128)(2,1)S(1)}, u32[]{:S(2)}, u32[]{:S(2)}) %collective-permute-start) | collective-permute-done | bytes 147488 | tf_op jit(solution)/shard_map/ppermute | solution.py:595
  39.7 0.0 copy-start.12
  39.8 0.1 collective-permute-start.1
  39.9 5.1 %collective-permute-done.2.refs_0_ = f32[4,2048]{1,0:T(4,128)S(1)} collective-permute-done((f32[4,2048]{1,0:T(4,128)S(1)}, f32[4,2048]{1,0:T(4,128)S(1)}, u32[]{:S(2)}, u32[]{:S(2)}) %collective-permute-start.2) | collective-permute-done | bytes 32800 | tf_op jit(solution)/shard_map/ppermute | solution.py:592
  44.9 1.5 %collective-permute-start.3 = (f32[4,2048]{1,0:T(4,128)S(1)}, f32[4,2048]{1,0:T(4,128)S(1)}, u32[]{:S(2)}, u32[]{:S(2)}) collective-permute-start(f32[4,2048]{1,0:T(4,128)S(1)} %collective-permute-done.2.refs_0_), channel_id=1, source_target_pairs={{0,16},{16,0},{1,17},{17,1},{2,18},{18,2},{3,19},{19,3},{4,20},{20... | collective-permute-start | bytes 98312 | tf_op jit(solution)/shard_map/ppermute | solution.py:595
  46.5 0.0 collective-permute-done.1.near_ref
  46.5 0.0 copy-done.12
  46.5 1.9 %shard_map.155.sum_ref = f32[80,1152]{1,0:T(8,128)S(1)} custom-call(f32[64,1152]{1,0:T(8,128)S(1)} %get-tuple-element.25.main_ref, f32[2,1152]{1,0:T(2,128)S(1)} %collective-permute-done.1.near_ref, bf16[704,224]{1,0:T(8,128)(2,1)S(1)} %get-tuple-element.27.one_ref.refs_2_, bf16[144,704]{1,0:T(8,128)(2,1)S(1)} %copy-done.12), custom_call_target="tpu_custom_call" | custom-call | flops 2147483648 | bytes 4194304 | tf_op jit(solution)/shard_map/pallas_call | solution.py:486
  48.4 0.5 collective-permute-done.3.refs_1_
  48.8 1.8 %shard_map.156 = f32[64,1024]{1,0:T(8,128)} custom-call(f32[80,1152]{1,0:T(8,128)S(1)} %shard_map.155.sum_ref, f32[64,1152]{1,0:T(8,128)S(1)} %get-tuple-element.25.main_ref, f32[4,2048]{1,0:T(4,128)S(1)} %collective-permute-done.2.refs_0_, f32[4,2048]{1,0:T(4,128)S(1)} %collective-permute-done.3.refs_1_, ...), custom_call_target="tpu_custom_call" | custom-call | flops 1073741824 | bytes 4194304 | tf_op jit(solution)/shard_map/pallas_call | solution.py:486
  50.7 0.0 all-to-all-done.1
  50.7 1.3 %shard_map.152 = bf16[256,512]{1,0:T(8,128)(2,1)} custom-call(s32[1,256]{1,0:T(1,128)S(1)} %get-tuple-element.16.dest_ref, bf16[512,512]{1,0:T(8,128)(2,1)S(1)} %bitcast.8), custom_call_target="tpu_custom_call" | custom-call | flops 268435456 | bytes 4194304 | tf_op jit(solution)/shard_map/pallas_call | solution.py:486
  (1 shorter events, 0.0 us)
Async XLA Ops:
  0.6 9.0 %copy-start.6 = (bf16[2,256,256]{2,1,0:T(8,128)(2,1)S(1)}, bf16[2,256,256]{2,1,0:T(8,128)(2,1)}, u32[]{:S(2)}) copy-start(bf16[2,256,256]{2,1,0:T(8,128)(2,1)} %constant.14.clone.mat_ref) | copy-start | bytes 786436
  0.6 9.0 %copy-start.7 = (bf16[128,192]{1,0:T(8,128)(2,1)S(1)}, bf16[128,192]{1,0:T(8,128)(2,1)}, u32[]{:S(2)}) copy-start(bf16[128,192]{1,0:T(8,128)(2,1)} %constant.12.clone.row_ref) | copy-start | bytes 147460
  3.3 6.4 %copy-start = (f32[64,2048]{1,0:T(8,128)S(1)}, f32[64,2048]{1,0:T(8,128)}, u32[]{:S(2)}) copy-start(f32[64,2048]{1,0:T(8,128)} %sky_hbm.1) | copy-start | bytes 1572868
  3.3 6.4 %copy-start.1 = (f32[1,64,2048]{2,1,0:T(8,128)S(1)}, f32[1,64,2048]{2,1,0:T(8,128)}, u32[]{:S(2)}) copy-start(f32[1,64,2048]{2,1,0:T(8,128)} %param.15) | copy-start | bytes 1572868
  3.3 6.4 %copy-start.3 = (f32[32,3,3]{0,2,1:T(4,128)S(1)}, f32[32,3,3]{0,2,1:T(4,128)}, u32[]{:S(2)}) copy-start(f32[32,3,3]{0,2,1:T(4,128)} %param.21) | copy-start | bytes 3460
  3.3 6.4 %copy-start.10 = (f32[2,16,128]{2,1,0:T(8,128)S(1)}, f32[2,16,128]{2,1,0:T(8,128)}, u32[]{:S(2)}) copy-start(f32[2,16,128]{2,1,0:T(8,128)} %constant.13.clone.twist_ref) | copy-start | bytes 49156
  3.3 20.9 %all-to-all-start = ((bf16[16,136,128]{2,1,0:T(8,128)(2,1)}), bf16[16,136,128]{2,1,0:T(8,128)(2,1)S(1)}, u32[]{:S(2)}, u32[]{:S(2)}) async-start(bf16[16,136,128]{2,1,0:T(8,128)(2,1)} %get-tuple-element.17), calls=%async_computation | async-start | bytes 1114112 | tf_op jit(solution)/shard_map/all_to_all | solution.py:532
  9.6 0.7 %copy-start.2 = (f32[32,3,3]{0,2,1:T(4,128)S(1)}, f32[32,3,3]{0,2,1:T(4,128)}, u32[]{:S(2)}) copy-start(f32[32,3,3]{0,2,1:T(4,128)} %param.19) | copy-start | bytes 3460
  9.7 0.7 %copy-start.4 = (f32[32]{0:T(128)S(1)}, f32[32]{0:T(128)}, u32[]{:S(2)}) copy-start(f32[32]{0:T(128)} %param.20) | copy-start | bytes 388
  11.8 0.7 %copy-start.11 = (bf16[144,704]{1,0:T(8,128)(2,1)}, bf16[144,704]{1,0:T(8,128)(2,1)S(1)}, u32[]{:S(2)}) copy-start(bf16[144,704]{1,0:T(8,128)(2,1)S(1)} %get-tuple-element.28.two_ref.refs_3_) | copy-start | bytes 608260
  26.1 4.8 %copy-start.5 = (bf16[2,256,256]{2,1,0:T(8,128)(2,1)S(1)}, bf16[2,256,256]{2,1,0:T(8,128)(2,1)}, u32[]{:S(2)}) copy-start(bf16[2,256,256]{2,1,0:T(8,128)(2,1)} %constant.17.clone.mat_ref) | copy-start | bytes 786436
  26.1 4.8 %copy-start.8 = (bf16[64,384]{1,0:T(8,128)(2,1)S(1)}, bf16[64,384]{1,0:T(8,128)(2,1)}, u32[]{:S(2)}) copy-start(bf16[64,384]{1,0:T(8,128)(2,1)} %constant.15.clone.row_ref) | copy-start | bytes 147460
  26.1 4.8 %copy-start.9 = (f32[2,16,128]{2,1,0:T(8,128)S(1)}, f32[2,16,128]{2,1,0:T(8,128)}, u32[]{:S(2)}) copy-start(f32[2,16,128]{2,1,0:T(8,128)} %constant.16.clone.twist_ref) | copy-start | bytes 49156
  26.1 24.6 %all-to-all-start.1 = ((bf16[16,32,512]{2,1,0:T(8,128)(2,1)}), bf16[16,32,512]{2,1,0:T(8,128)(2,1)S(1)}, u32[]{:S(2)}, u32[]{:S(2)}) async-start(bf16[16,32,512]{2,1,0:T(8,128)(2,1)} %bitcast.6), calls=%async_computation.1 | async-start | bytes 1048576 | tf_op jit(solution)/shard_map/all_to_all | solution.py:561
  33.8 5.9 %collective-permute-start = (bf16[64,1152]{1,0:T(8,128)(2,1)S(1)}, bf16[64,1152]{1,0:T(8,128)(2,1)S(1)}, u32[]{:S(2)}, u32[]{:S(2)}) collective-permute-start(bf16[64,1152]{1,0:T(8,128)(2,1)S(1)} %get-tuple-element.24), channel_id=1, source_target_pairs={{0,16},{16,0},{1,17},{17,1},{2,18},{18,2},{3,19},{19,3},{4,20},{20... | collective-permute-start | bytes 442376 | tf_op jit(solution)/shard_map/ppermute | solution.py:595
  35.4 9.5 %collective-permute-start.2 = (f32[4,2048]{1,0:T(4,128)S(1)}, f32[4,2048]{1,0:T(4,128)S(1)}, u32[]{:S(2)}, u32[]{:S(2)}) collective-permute-start(f32[4,2048]{1,0:T(4,128)S(1)} %get-tuple-element.29), channel_id=1, source_target_pairs={{1,2},{2,1},{3,4},{4,3},{5,6},{6,5},{7,8},{8,7},{9,10},{10,9},{11,... | collective-permute-start | bytes 98312 | tf_op jit(solution)/shard_map/ppermute | solution.py:592
  39.7 6.7 %copy-start.12 = (bf16[144,704]{1,0:T(8,128)(2,1)S(1)}, bf16[144,704]{1,0:T(8,128)(2,1)}, u32[]{:S(2)}) copy-start(bf16[144,704]{1,0:T(8,128)(2,1)} %copy-done.11) | copy-start | bytes 608260
  39.8 6.7 %collective-permute-start.1 = (f32[2,1152]{1,0:T(2,128)S(1)}, f32[2,1152]{1,0:T(2,128)S(1)}, u32[]{:S(2)}, u32[]{:S(2)}) collective-permute-start(f32[2,1152]{1,0:T(2,128)S(1)} %get-tuple-element.26), channel_id=1, source_target_pairs={{0,1},{1,0},{2,3},{3,2},{4,5},{5,4},{6,7},{7,6},{8,9},{9,8},{10,11... | collective-permute-start | bytes 27656 | tf_op jit(solution)/shard_map/ppermute | solution.py:592
  44.9 3.9 %collective-permute-start.3 = (f32[4,2048]{1,0:T(4,128)S(1)}, f32[4,2048]{1,0:T(4,128)S(1)}, u32[]{:S(2)}, u32[]{:S(2)}) collective-permute-start(f32[4,2048]{1,0:T(4,128)S(1)} %collective-permute-done.2.refs_0_), channel_id=1, source_target_pairs={{0,16},{16,0},{1,17},{17,1},{2,18},{18,2},{3,19},{19,3},{4,20},{20... | collective-permute-start | bytes 98312 | tf_op jit(solution)/shard_map/ppermute | solution.py:595

commit v2 on v0

--- a/solution.py
+++ b/solution.py
@@ -51,8 +51,7 @@
         row_high, row_low = np_split(np.concatenate([cos_r, sin_r], 0))
         row = np.concatenate([row_high, row_high, row_low], 1)
     else:
-        row_high, row_low = np_split(np.concatenate([cos_r, -sin_r], 1))
-        row = np.concatenate([row_high, row_high, row_low], 1)
+        row = np.concatenate(np_split(np.concatenate([cos_r, -sin_r], 1)), 1)
     i2 = np.arange(LANES)
     w = np.arange(outer)
     twist = sign * 2.0 * np.pi * ((w[:, None] * i2[None, :]) % cols) / cols
@@ -291,9 +290,8 @@
                 axis=0,
             )
         )
-    high, low = split(jnp.concatenate(blocks, axis=0))
-    mat_high, mat_low = mat_ref[0], mat_ref[1]
-    mid = mm(high, mat_high) + mm(low, mat_high) + mm(high, mat_low)
+    cells = jnp.concatenate(blocks, axis=0).astype(BF16)
+    mid = mm(jnp.concatenate([cells, cells], axis=1), mat_ref[...].reshape(4 * LANES, 2 * LANES))
     lines = []
     for w in range(outer):
         re = mid[w * rows : (w + 1) * rows, :LANES]
@@ -303,12 +301,10 @@
     spread = dft16(lines, 1)
     for i, pair in enumerate(spread):
         for e in range(2):
-            high, low = split(pair[e])
-            lines_ref[e * rows : (e + 1) * rows, i * LANES : (i + 1) * LANES] = high
-            lines_ref[(2 + e) * rows : (3 + e) * rows, i * LANES : (i + 1) * LANES] = low
-    back = mm(row_ref[:, : 4 * rows], lines_ref[...]) + mm(
-        row_ref[:, 4 * rows :], lines_ref[: 2 * rows, :]
-    )
+            line = pair[e].astype(BF16)
+            lines_ref[e * rows : (e + 1) * rows, i * LANES : (i + 1) * LANES] = line
+            lines_ref[(2 + e) * rows : (3 + e) * rows, i * LANES : (i + 1) * LANES] = line
+    back = mm(row_ref[...], lines_ref[...])
     for load in loads:
         load.wait()
     shift_ref[...] = back * beam_ref[...] * (-STEP)
@@ -436,26 +432,56 @@
     sum_ref[spots[-1], :] = sum_ref[spots[-1], :] + jnp.where(even, share, 0.0)
 
 
-def edge_kernel(count, part, sum_ref, main_ref, far_ref, one_ref, two_ref, out_ref, base_ref, all_ref):
-    rows, _ = main_ref.shape
+def edge_kernel(
+    count,
+    part,
+    sum_ref,
+    main_ref,
+    far_ref,
+    one_ref,
+    two_ref,
+    out_hbm,
+    base_ref,
+    share_ref,
+    last_ref,
+    sems,
+):
+    rows, width = main_ref.shape
     tall = BAND + 2
     place = lax.axis_index("facet")
-    last = lax.axis_size("facet") - 1
+    final = lax.axis_size("facet") - 1
     even = (place & 1) == 0
+    me = lax.axis_index("freq")
+    start, _ = window(me, count, part * count)
+    at = pl.ds(pl.multiple_of(me * part - start, LANES), part)
+    done = rows - tall
+    first = pl.multiple_of(jnp.where(even, tall, 0), 8)
+    early = pltpu.make_async_copy(
+        sum_ref.at[pl.ds(pl.multiple_of(first + 8, 8), done), at],
+        out_hbm.at[pl.ds(first, done), :],
+        sems.at[0],
+    )
+    early.start()
     far = far_ref[...]
     base_ref[0:2, :] = far
     base_ref[2:tall, :] = main_ref[0:BAND, :]
     base_ref[32 : 32 + BAND, :] = main_ref[rows - BAND : rows, :]
     base_ref[32 + BAND : 32 + tall, :] = far
     band = jnp.where(even, base_ref[0:tall, :], base_ref[32 : 32 + tall, :])
-    share = band_prior(band, one_ref, two_ref, (place == 0, place == last))
-    all_ref[...] = sum_ref[...]
-    head, tail = slice(6, 6 + tall), slice(rows + 10 - tall, rows + 10)
-    all_ref[head, :] = all_ref[head, :] + jnp.where(even, share, 0.0)
-    all_ref[tail, :] = all_ref[tail, :] + jnp.where(even, 0.0, share)
-    me = lax.axis_index("freq")
-    start, _ = window(me, count, part * count)
-    out_ref[...] = all_ref[8 : rows + 8, pl.ds(pl.multiple_of(me * part - start, LANES), part)]
+    share_ref[0:8, :] = jnp.zeros((8, width), F32)
+    share_ref[8 : tall + 8, :] = band_prior(band, one_ref, two_ref, (place == 0, place == final))
+    share_ref[tall + 8 : tall + 16, :] = jnp.zeros((8, width), F32)
+    near_sum = jnp.where(even, sum_ref[8 : tall + 8, :], sum_ref[rows + 8 - tall : rows + 8, :])
+    share = jnp.where(even, share_ref[10 : tall + 10, :], share_ref[6 : tall + 6, :])
+    last_ref[...] = near_sum + share
+    late = pltpu.make_async_copy(
+        last_ref.at[:, at],
+        out_hbm.at[pl.ds(pl.multiple_of(jnp.where(even, 0, done), 8), tall), :],
+        sems.at[1],
+    )
+    late.start()
+    early.wait()
+    late.wait()
 
 
 def unpack_kernel(dest_ref, back_ref, out_ref):
@@ -595,11 +621,17 @@
     partial = call(
         prior_kernel, shape((rows + 16, wide), F32), 1 << 31, scratch=[tall_rows]
     )(main, near, first, second)
-    image = call(
+    (image,) = call(
         functools.partial(edge_kernel, count, cols // count),
-        shape((rows, cols // count), F32),
+        [shape((rows, cols // count), F32)],
         1 << 30,
-        scratch=[pltpu.VMEM((64, wide), F32), tall_rows],
+        scratch=[
+            pltpu.VMEM((64, wide), F32),
+            pltpu.VMEM((BAND + 18, wide), F32),
+            pltpu.VMEM((BAND + 2, wide), F32),
+            pltpu.SemaphoreType.DMA((2,)),
+        ],
+        saved=(0,),
     )(partial, main, far, first, second)
 
     tiles_out = call(unpack_kernel, shape((tiles, width), BF16), 1 << 28)(dest, returned)

time: 50.1 us -> 49.6 us (0.990)
    pallas_call x8, Pallas kernels: 13.8 us -> 13.3 us  [run(): pl.pallas_call(kernel, out_shape=out_shape, in_specs=[far if i in loaded...]
where the time goes in v2:
time: 49.6 us; the launch traced here: 49.1 us
  starting transfers between devices  17.7 us (36%)
  waiting for transfers between devices  15.8 us (32%)
  Pallas kernels  13.3 us (27%)
  local copies, waits for them, and re-layouts  1.36 us (3%)
  between operations  0.88 us (2%)
    pallas_call x8, Pallas kernels, run(): pl.pallas_call(kernel, out_shape=out_shape, in_specs=[far if i in loaded...  13.3 us
    all_to_all x1, waiting for transfers between devices, on_device(): got = lax.all_to_all(send, 'facet', split_axis=0, concat_axis=0, tiled=True)  11.8 us
    all_to_all x1, starting transfers between devices, on_device(): got = lax.all_to_all(send, 'facet', split_axis=0, concat_axis=0, tiled=True)  7.46 us
    all_to_all x1, starting transfers between devices, on_device(): lax.all_to_all(residual.reshape(facets, cap, width), 'facet', split_axis=...  4.7 us
    ppermute x2, starting transfers between devices, beside(): return lax.ppermute(value, 'facet', pairs)  4.19 us
    ppermute x1, waiting for transfers between devices, on_device(): lax.ppermute(value, 'freq', [(f, (f + d + 1) % count) for f in range(coun...  4.05 us
    unnamed x26, local copies, waits for them, and re-layouts  1.36 us
    ppermute x1, starting transfers between devices, on_device(): lax.ppermute(value, 'freq', [(f, (f + d + 1) % count) for f in range(coun...  1.32 us
  transfers between devices with their start and end apart: 5, of which 2 were waited for; matrix products, arithmetic and copies ran while one was open for 0% of the time, Pallas kernels for 16%

profile of v2, /device:TPU:1, one launch (start us, length us, event | category | flops | bytes accessed | tf_op | source)
XLA Modules:
  0.0 49.1 jit_solution(3221978355600556277)
XLA Ops:
  0.6 0.0 copy-start.6
  0.6 0.0 copy-start.7
  0.7 2.6 %shard_map.149 = (bf16[16,136,128]{2,1,0:T(8,128)(2,1)}, s32[1,256]{1,0:T(1,128)S(1)}) custom-call(s32[1,256]{1,0:T(1,128)} %bitcast.14, s32[1,256]{1,0:T(1,128)} %bitcast.15, bf16[256,512]{1,0:T(8,128)(2,1)} %seen_hbm.1), custom_call_target="tpu_custom_call" | custom-call | flops 268435456 | bytes 4194304 | tf_op jit(solution)/shard_map/pallas_call | solution.py:504
  3.3 0.0 copy-start
  3.3 0.0 copy-start.1
  3.3 0.0 copy-start.3
  3.3 0.0 copy-start.10
  3.3 7.5 %all-to-all-start = ((bf16[16,136,128]{2,1,0:T(8,128)(2,1)}), bf16[16,136,128]{2,1,0:T(8,128)(2,1)S(1)}, u32[]{:S(2)}, u32[]{:S(2)}) async-start(bf16[16,136,128]{2,1,0:T(8,128)(2,1)} %get-tuple-element.17), calls=%async_computation | async-start | bytes 1114112 | tf_op jit(solution)/shard_map/all_to_all | solution.py:550
  10.8 0.0 copy-start.2
  10.8 0.0 copy-start.4
  10.8 0.0 copy-done.6
  10.8 0.0 copy-done.7
  10.8 0.0 copy-done
  10.8 0.0 copy-done.1
  10.8 0.0 copy-done.3
  10.9 0.0 copy-done.10
  10.9 0.6 %copy-done.2 = f32[32,3,3]{0,2,1:T(4,128)S(1)} copy-done((f32[32,3,3]{0,2,1:T(4,128)S(1)}, f32[32,3,3]{0,2,1:T(4,128)}, u32[]{:S(2)}) %copy-start.2) | copy-done | bytes 1176
  11.5 0.0 copy-done.4
  11.5 1.4 %shard_map.150 = (bf16[512,512]{1,0:T(8,128)(2,1)S(1)}, bf16[512,512]{1,0:T(8,128)(2,1)S(1)}, bf16[704,224]{1,0:T(8,128)(2,1)S(1)}, bf16[144,704]{1,0:T(8,128)(2,1)S(1)}) custom-call(f32[64,2048]{1,0:T(8,128)S(1)} %copy-done, f32[64,2048]{1,0:T(8,128)S(1)} %bitcast.10, bf16[128,192]{1,0:T(8,128)(2,1)S(1)} %copy-done.7, f32[2,16,128]{2,1,0:T(8,128)S(1)} %copy-done.10, ...), custom_call_target="tpu_custom_call" | custom-call | flops 1073741824 | bytes 4194304 | tf_op jit(solution)/shard_map/pallas_call | solution.py:504
  12.9 0.0 copy-start.11
  12.9 0.7 %copy-done.11 = bf16[144,704]{1,0:T(8,128)(2,1)} copy-done((bf16[144,704]{1,0:T(8,128)(2,1)}, bf16[144,704]{1,0:T(8,128)(2,1)S(1)}, u32[]{:S(2)}) %copy-start.11) | copy-done | bytes 202776
  13.6 11.8 %all-to-all-done.got_ref = bf16[16,136,128]{2,1,0:T(8,128)(2,1)S(1)} async-done(((bf16[16,136,128]{2,1,0:T(8,128)(2,1)}), bf16[16,136,128]{2,1,0:T(8,128)(2,1)S(1)}, u32[]{:S(2)}, u32[]{:S(2)}) %all-to-all-start) | async-done | bytes 557088 | tf_op jit(solution)/shard_map/all_to_all | solution.py:550
  25.4 1.8 %shard_map.151 = (bf16[512,512]{1,0:T(8,128)(2,1)}, bf16[512,512]{1,0:T(8,128)(2,1)S(1)}, bf16[512,512]{1,0:T(8,128)(2,1)S(1)}) custom-call(bf16[16,136,128]{2,1,0:T(8,128)(2,1)S(1)} %all-to-all-done.got_ref, bf16[512,512]{1,0:T(8,128)(2,1)S(1)} %get-tuple-element.18.high_ref, bf16[512,512]{1,0:T(8,128)(2,1)S(1)} %get-tuple-element.19.low_ref), custom_call_target="tpu_custom_call" | custom-call | flops 1073741824 | bytes 4194304 | tf_op jit(solution)/shard_map/pallas_call | solution.py:504
  27.2 0.0 copy-start.5
  27.2 0.0 copy-start.8
  27.2 0.0 copy-start.9
  27.3 4.7 %all-to-all-start.1 = ((bf16[16,32,512]{2,1,0:T(8,128)(2,1)}), bf16[16,32,512]{2,1,0:T(8,128)(2,1)S(1)}, u32[]{:S(2)}, u32[]{:S(2)}) async-start(bf16[16,32,512]{2,1,0:T(8,128)(2,1)} %bitcast.6), calls=%async_computation.1 | async-start | bytes 1048576 | tf_op jit(solution)/shard_map/all_to_all | solution.py:579
  32.0 0.0 copy-done.5
  32.0 0.0 copy-done.8
  32.0 0.0 copy-done.9
  32.0 2.5 %shard_map.153 = (f32[64,1152]{1,0:T(8,128)S(1)}, bf16[64,1152]{1,0:T(8,128)(2,1)S(1)}) custom-call(bf16[512,512]{1,0:T(8,128)(2,1)S(1)} %get-tuple-element.21.res_ref, bf16[512,512]{1,0:T(8,128)(2,1)S(1)} %get-tuple-element.22.sel_ref, bf16[64,256]{1,0:T(8,128)(2,1)S(1)} %copy-done.8, f32[2,16,128]{2,1,0:T(8,128)S(1)} %copy-done.9, ...), custom_call_target="tpu_custom_call" | custom-call | flops 1073741824 | bytes 4194304 | tf_op jit(solution)/shard_map/pallas_call | solution.py:504
  34.4 1.3 %collective-permute-start = (bf16[64,1152]{1,0:T(8,128)(2,1)S(1)}, bf16[64,1152]{1,0:T(8,128)(2,1)S(1)}, u32[]{:S(2)}, u32[]{:S(2)}) collective-permute-start(bf16[64,1152]{1,0:T(8,128)(2,1)S(1)} %get-tuple-element.24), channel_id=1, source_target_pairs={{0,16},{16,0},{1,17},{17,1},{2,18},{18,2},{3,19},{19,3},{4,20},{20... | collective-permute-start | bytes 442376 | tf_op jit(solution)/shard_map/ppermute | solution.py:610
  35.8 4.0 %collective-permute-done.refs_0_ = bf16[64,1152]{1,0:T(8,128)(2,1)S(1)} collective-permute-done((bf16[64,1152]{1,0:T(8,128)(2,1)S(1)}, bf16[64,1152]{1,0:T(8,128)(2,1)S(1)}, u32[]{:S(2)}, u32[]{:S(2)}) %collective-permute-start) | collective-permute-done | bytes 147488 | tf_op jit(solution)/shard_map/ppermute | solution.py:610
  39.8 0.0 copy-start.12
  39.9 1.0 %collective-permute-start.1 = (f32[2,1152]{1,0:T(2,128)S(1)}, f32[2,1152]{1,0:T(2,128)S(1)}, u32[]{:S(2)}, u32[]{:S(2)}) collective-permute-start(f32[2,1152]{1,0:T(2,128)S(1)} %get-tuple-element.26), channel_id=1, source_target_pairs={{0,1},{1,0},{2,3},{3,2},{4,5},{5,4},{6,7},{7,6},{8,9},{9,8},{10,11... | collective-permute-start | bytes 27656 | tf_op jit(solution)/shard_map/ppermute | solution.py:607
  40.9 3.2 %collective-permute-start.2 = (f32[2,1152]{1,0:T(2,128)S(1)}, f32[2,1152]{1,0:T(2,128)S(1)}, u32[]{:S(2)}, u32[]{:S(2)}) collective-permute-start(f32[2,1152]{1,0:T(2,128)S(1)} %get-tuple-element.29), channel_id=1, source_target_pairs={{1,2},{2,1},{3,4},{4,3},{5,6},{6,5},{7,8},{8,7},{9,10},{10,9},{11,... | collective-permute-start | bytes 27656 | tf_op jit(solution)/shard_map/ppermute | solution.py:607
  44.1 0.0 collective-permute-done.1.near_ref
  44.1 0.0 copy-done.12
  44.1 1.9 %shard_map.155.sum_ref = f32[80,1152]{1,0:T(8,128)S(1)} custom-call(f32[64,1152]{1,0:T(8,128)S(1)} %get-tuple-element.25.main_ref, f32[2,1152]{1,0:T(2,128)S(1)} %collective-permute-done.1.near_ref, bf16[704,224]{1,0:T(8,128)(2,1)S(1)} %get-tuple-element.27.one_ref, bf16[144,704]{1,0:T(8,128)(2,1)S(1)} %copy-done.12), custom_call_target="tpu_custom_call" | custom-call | flops 2147483648 | bytes 4194304 | tf_op jit(solution)/shard_map/pallas_call | solution.py:504
  46.0 0.0 collective-permute-done.2.far_ref
  46.0 1.8 %shard_map.156 = f32[64,1024]{1,0:T(8,128)} custom-call(f32[80,1152]{1,0:T(8,128)S(1)} %shard_map.155.sum_ref, f32[64,1152]{1,0:T(8,128)S(1)} %get-tuple-element.25.main_ref, f32[2,1152]{1,0:T(2,128)S(1)} %collective-permute-done.2.far_ref, bf16[704,224]{1,0:T(8,128)(2,1)S(1)} %get-tuple-element.27.one_ref, bf16[144,704]{1,0:T(8,128)(2,1)S(1)} %copy-done.12), custom_call_target="tpu_custom_call" | custom-call | flops 1073741824 | bytes 4194304 | tf_op jit(solution)/shard_map/pallas_call | solution.py:504
  47.8 0.0 all-to-all-done.1
  47.8 1.3 %shard_map.152 = bf16[256,512]{1,0:T(8,128)(2,1)} custom-call(s32[1,256]{1,0:T(1,128)S(1)} %get-tuple-element.16.dest_ref, bf16[512,512]{1,0:T(8,128)(2,1)S(1)} %bitcast.8), custom_call_target="tpu_custom_call" | custom-call | flops 268435456 | bytes 4194304 | tf_op jit(solution)/shard_map/pallas_call | solution.py:504
  (1 shorter events, 0.0 us)
Async XLA Ops:
  0.6 10.2 %copy-start.6 = (bf16[2,256,256]{2,1,0:T(8,128)(2,1)S(1)}, bf16[2,256,256]{2,1,0:T(8,128)(2,1)}, u32[]{:S(2)}) copy-start(bf16[2,256,256]{2,1,0:T(8,128)(2,1)} %constant.14.clone.mat_ref) | copy-start | bytes 786436
  0.6 10.2 %copy-start.7 = (bf16[128,192]{1,0:T(8,128)(2,1)S(1)}, bf16[128,192]{1,0:T(8,128)(2,1)}, u32[]{:S(2)}) copy-start(bf16[128,192]{1,0:T(8,128)(2,1)} %constant.12.clone.row_ref) | copy-start | bytes 147460
  3.3 7.5 %copy-start = (f32[64,2048]{1,0:T(8,128)S(1)}, f32[64,2048]{1,0:T(8,128)}, u32[]{:S(2)}) copy-start(f32[64,2048]{1,0:T(8,128)} %sky_hbm.1) | copy-start | bytes 1572868
  3.3 7.5 %copy-start.1 = (f32[1,64,2048]{2,1,0:T(8,128)S(1)}, f32[1,64,2048]{2,1,0:T(8,128)}, u32[]{:S(2)}) copy-start(f32[1,64,2048]{2,1,0:T(8,128)} %param.15) | copy-start | bytes 1572868
  3.3 7.5 %copy-start.3 = (f32[32,3,3]{0,2,1:T(4,128)S(1)}, f32[32,3,3]{0,2,1:T(4,128)}, u32[]{:S(2)}) copy-start(f32[32,3,3]{0,2,1:T(4,128)} %param.21) | copy-start | bytes 3460
  3.3 7.5 %copy-start.10 = (f32[2,16,128]{2,1,0:T(8,128)S(1)}, f32[2,16,128]{2,1,0:T(8,128)}, u32[]{:S(2)}) copy-start(f32[2,16,128]{2,1,0:T(8,128)} %constant.13.clone.twist_ref) | copy-start | bytes 49156
  3.3 22.0 %all-to-all-start = ((bf16[16,136,128]{2,1,0:T(8,128)(2,1)}), bf16[16,136,128]{2,1,0:T(8,128)(2,1)S(1)}, u32[]{:S(2)}, u32[]{:S(2)}) async-start(bf16[16,136,128]{2,1,0:T(8,128)(2,1)} %get-tuple-element.17), calls=%async_computation | async-start | bytes 1114112 | tf_op jit(solution)/shard_map/all_to_all | solution.py:550
  10.8 0.7 %copy-start.2 = (f32[32,3,3]{0,2,1:T(4,128)S(1)}, f32[32,3,3]{0,2,1:T(4,128)}, u32[]{:S(2)}) copy-start(f32[32,3,3]{0,2,1:T(4,128)} %param.19) | copy-start | bytes 3460
  10.8 0.7 %copy-start.4 = (f32[32]{0:T(128)S(1)}, f32[32]{0:T(128)}, u32[]{:S(2)}) copy-start(f32[32]{0:T(128)} %param.20) | copy-start | bytes 388
  12.9 0.7 %copy-start.11 = (bf16[144,704]{1,0:T(8,128)(2,1)}, bf16[144,704]{1,0:T(8,128)(2,1)S(1)}, u32[]{:S(2)}) copy-start(bf16[144,704]{1,0:T(8,128)(2,1)S(1)} %get-tuple-element.28.two_ref) | copy-start | bytes 608260
  27.2 4.7 %copy-start.5 = (bf16[2,256,256]{2,1,0:T(8,128)(2,1)S(1)}, bf16[2,256,256]{2,1,0:T(8,128)(2,1)}, u32[]{:S(2)}) copy-start(bf16[2,256,256]{2,1,0:T(8,128)(2,1)} %constant.17.clone.mat_ref) | copy-start | bytes 786436
  27.2 4.7 %copy-start.8 = (bf16[64,256]{1,0:T(8,128)(2,1)S(1)}, bf16[64,256]{1,0:T(8,128)(2,1)}, u32[]{:S(2)}) copy-start(bf16[64,256]{1,0:T(8,128)(2,1)} %constant.15.clone.row_ref) | copy-start | bytes 98308
  27.2 4.7 %copy-start.9 = (f32[2,16,128]{2,1,0:T(8,128)S(1)}, f32[2,16,128]{2,1,0:T(8,128)}, u32[]{:S(2)}) copy-start(f32[2,16,128]{2,1,0:T(8,128)} %constant.16.clone.twist_ref) | copy-start | bytes 49156
  27.3 20.5 %all-to-all-start.1 = ((bf16[16,32,512]{2,1,0:T(8,128)(2,1)}), bf16[16,32,512]{2,1,0:T(8,128)(2,1)S(1)}, u32[]{:S(2)}, u32[]{:S(2)}) async-start(bf16[16,32,512]{2,1,0:T(8,128)(2,1)} %bitcast.6), calls=%async_computation.1 | async-start | bytes 1048576 | tf_op jit(solution)/shard_map/all_to_all | solution.py:579
  34.4 5.4 %collective-permute-start = (bf16[64,1152]{1,0:T(8,128)(2,1)S(1)}, bf16[64,1152]{1,0:T(8,128)(2,1)S(1)}, u32[]{:S(2)}, u32[]{:S(2)}) collective-permute-start(bf16[64,1152]{1,0:T(8,128)(2,1)S(1)} %get-tuple-element.24), channel_id=1, source_target_pairs={{0,16},{16,0},{1,17},{17,1},{2,18},{18,2},{3,19},{19,3},{4,20},{20... | collective-permute-start | bytes 442376 | tf_op jit(solution)/shard_map/ppermute | solution.py:610
  39.8 4.3 %copy-start.12 = (bf16[144,704]{1,0:T(8,128)(2,1)S(1)}, bf16[144,704]{1,0:T(8,128)(2,1)}, u32[]{:S(2)}) copy-start(bf16[144,704]{1,0:T(8,128)(2,1)} %copy-done.11) | copy-start | bytes 608260
  39.9 4.2 %collective-permute-start.1 = (f32[2,1152]{1,0:T(2,128)S(1)}, f32[2,1152]{1,0:T(2,128)S(1)}, u32[]{:S(2)}, u32[]{:S(2)}) collective-permute-start(f32[2,1152]{1,0:T(2,128)S(1)} %get-tuple-element.26), channel_id=1, source_target_pairs={{0,1},{1,0},{2,3},{3,2},{4,5},{5,4},{6,7},{7,6},{8,9},{9,8},{10,11... | collective-permute-start | bytes 27656 | tf_op jit(solution)/shard_map/ppermute | solution.py:607
  40.9 5.1 %collective-permute-start.2 = (f32[2,1152]{1,0:T(2,128)S(1)}, f32[2,1152]{1,0:T(2,128)S(1)}, u32[]{:S(2)}, u32[]{:S(2)}) collective-permute-start(f32[2,1152]{1,0:T(2,128)S(1)} %get-tuple-element.29), channel_id=1, source_target_pairs={{1,2},{2,1},{3,4},{4,3},{5,6},{6,5},{7,8},{8,7},{9,10},{10,9},{11,... | collective-permute-start | bytes 27656 | tf_op jit(solution)/shard_map/ppermute | solution.py:607

commit v3 on v2

--- a/solution.py
+++ b/solution.py
@@ -111,7 +111,20 @@
     return one_hot(iota((size, size), 0) == swapped)
 
 
-def pack_kernel(facets, cap, facet_hbm, slot_hbm, seen_hbm, send_ref, dest_ref, facet_ref, slot_ref, seen_ref, sems):
+def pack_kernel(
+    facets,
+    cap,
+    facet_hbm,
+    slot_hbm,
+    seen_hbm,
+    send_hbm,
+    dest_ref,
+    facet_ref,
+    slot_ref,
+    seen_ref,
+    send_ref,
+    sems,
+):
     tiles, width = seen_ref.shape
     total = facets * cap
     loads = [
@@ -122,20 +135,15 @@
     ]
     for load in loads:
         load.start()
-    swap = swap_matrix(width)
+    before = one_hot(iota((tiles, tiles), 0) < iota((tiles, tiles), 1))
     loads[0].wait()
     facet = facet_ref[...]
     member = iota((facets, tiles), 0) == facet
     member_f = jnp.where(member, 1.0, 0.0)
-    before = one_hot(iota((tiles, tiles), 0) < iota((tiles, tiles), 1))
     ranks = mm(member_f.astype(BF16), before)
     rank = jnp.sum(member_f * ranks, axis=0, keepdims=True).astype(jnp.int32)
     dest = facet * cap + rank
     dest_ref[...] = dest
-    placing = one_hot(iota((total, tiles), 0) == dest)
-    loads[2].wait()
-    turned = mm(seen_ref[...], swap).astype(BF16)
-    packed = mm(placing, turned).astype(BF16)
     loads[1].wait()
     code = slot_ref[...] + 1
     lane = iota((LANES, tiles), 0)
@@ -147,14 +155,28 @@
         ((1,), (1,)),
     )
     parts = width // LANES
-    for d in range(facets):
-        for part in range(parts):
-            send_ref[d, part * cap : (part + 1) * cap, :] = packed[
-                d * cap : (d + 1) * cap, part * LANES : (part + 1) * LANES
-            ]
-        send_ref[d, parts * cap : parts * cap + 8, :] = jnp.broadcast_to(
-            slots[d : d + 1, :], (8, LANES)
-        ).astype(BF16)
+    groups = 4
+    here = facets // groups
+    loads[2].wait()
+    saves = []
+    for g in range(groups):
+        placing = one_hot(iota((total // groups, tiles), 0) + g * (total // groups) == dest)
+        packed = mm(placing, seen_ref[...]).astype(BF16)
+        for i in range(here):
+            d = g * here + i
+            for part in range(parts):
+                send_ref[d, part * cap : (part + 1) * cap, :] = packed[
+                    i * cap : (i + 1) * cap, part * LANES : (part + 1) * LANES
+                ]
+            send_ref[d, parts * cap : parts * cap + 8, :] = jnp.broadcast_to(
+                slots[d : d + 1, :], (8, LANES)
+            ).astype(BF16)
+        span = pl.ds(g * here, here)
+        save = pltpu.make_async_copy(send_ref.at[span], send_hbm.at[span], sems.at[3 + g])
+        save.start()
+        saves.append(save)
+    for save in saves:
+        save.wait()
 
 
 def forward_kernel(
@@ -170,6 +192,7 @@
     low_ref,
     one_ref,
     two_ref,
+    part_ref,
 ):
     prepare(first_ref, bias_ref, second_ref, one_ref, two_ref)
     rows, cols = sky_ref.shape
@@ -201,8 +224,11 @@
                 ]
                 piece_high, piece_low = split(piece)
                 at = (pl.ds(e * 256 + w * S, S), pl.ds(r * LANES, LANES))
-                high_ref[at] = piece_high
-                low_ref[at] = piece_low
+                part_ref[(0,) + at] = piece_high
+                part_ref[(1,) + at] = piece_low
+    swap = swap_matrix(high_ref.shape[0])
+    high_ref[...] = mm(swap, part_ref[0]).astype(BF16)
+    low_ref[...] = mm(swap, part_ref[1]).astype(BF16)
 
 
 def residual_kernel(facets, cap, got_ref, high_ref, low_ref, res_hbm, sel_ref, own_ref, sems):
@@ -257,7 +283,7 @@
     *rest,
 ):
     send_refs = rest[: count - 1]
-    sky_ref, beam_ref, lines_ref, shift_ref, sems = rest[count - 1 :]
+    sky_ref, beam_ref, lines_ref, shift_ref, grid_ref, sems = rest[count - 1 :]
     rows, cols = beam_ref.shape
     outer = cols // LANES
     me = lax.axis_index("freq")
@@ -270,6 +296,8 @@
     for load in loads:
         load.start()
     grid = mm(res_ref[...], sel_ref[...], ((0,), (0,)))
+    for r in range(rows // S):
+        grid_ref[r] = grid[:, r * LANES : (r + 1) * LANES]
     blocks = []
     for w in range(outer):
         blocks.append(
@@ -277,10 +305,7 @@
                 [
                     jnp.concatenate(
                         [
-                            grid[
-                                e * 256 + w * S : e * 256 + (w + 1) * S,
-                                r * LANES : (r + 1) * LANES,
-                            ]
+                            grid_ref[r, pl.ds(e * S * S + w, S, stride=S), :]
                             for e in range(2)
                         ],
                         axis=1,
@@ -486,10 +511,9 @@
 
 def unpack_kernel(dest_ref, back_ref, out_ref):
     tiles = dest_ref.shape[1]
-    total, width = back_ref.shape
+    total, _ = back_ref.shape
     placing = one_hot(iota((total, tiles), 0) == dest_ref[...])
-    mine = mm(placing, back_ref[...], ((0,), (0,))).astype(BF16)
-    out_ref[...] = mm(mine, swap_matrix(width)).astype(BF16)
+    out_ref[...] = mm(placing, back_ref[...], ((0,), (0,))).astype(BF16)
 
 
 def shape(dims, dtype):
@@ -538,9 +562,11 @@
             pltpu.VMEM((1, tiles), jnp.int32),
             pltpu.VMEM((1, tiles), jnp.int32),
             pltpu.VMEM((tiles, width), BF16),
-            pltpu.SemaphoreType.DMA((3,)),
+            pltpu.VMEM((facets, deep, LANES), BF16),
+            pltpu.SemaphoreType.DMA((7,)),
         ],
         loaded=(0, 1, 2),
+        saved=(0,),
     )(
         *(
             pltpu.with_memory_space_constraint(value, pltpu.HBM)
@@ -558,6 +584,7 @@
             shape((6 * (BAND + 2), hidden * BAND), BF16),
         ],
         1 << 30,
+        scratch=[pltpu.VMEM((2, width, slots), BF16)],
     )(
         sky,
         beam,
@@ -590,6 +617,7 @@
             pltpu.VMEM((rows, cols), F32),
             pltpu.VMEM((4 * rows, cols), BF16),
             pltpu.VMEM((rows, cols), F32),
+            pltpu.VMEM((rows // S, width, LANES), F32),
             pltpu.SemaphoreType.DMA((2,)),
         ],
         loaded=(5, 6),

time: 49.6 us -> 49.2 us (level)
  waiting for transfers between devices: 15.8 us -> 14.5 us
  Pallas kernels: 13.3 us -> 14.3 us
    all_to_all x1, waiting for transfers between devices: 11.8 us -> 10.4 us  [on_device(): got = lax.all_to_all(send, 'facet', split_axis=0, concat_axis=0, tiled=True)]
    pallas_call x8, Pallas kernels: 13.3 us -> 14.3 us  [run(): pl.pallas_call(kernel, out_shape=out_shape, in_specs=[far if i in loaded...]
  transfers between devices with their start and end apart: 5 -> 5, of which waited for: 2 -> 2; matrix products, arithmetic and copies ran while one was open for 0% -> 0% of each run, Pallas kernels for 16% -> 19%
where the time goes in v3:
time: 49.2 us; the launch traced here: 48.6 us
  starting transfers between devices  17.7 us (36%)
  waiting for transfers between devices  14.5 us (29%)
  Pallas kernels  14.3 us (29%)
  local copies, waits for them, and re-layouts  1.36 us (3%)
  between operations  0.88 us (2%)
    pallas_call x8, Pallas kernels, run(): pl.pallas_call(kernel, out_shape=out_shape, in_specs=[far if i in loaded...  14.3 us
    all_to_all x1, waiting for transfers between devices, on_device(): got = lax.all_to_all(send, 'facet', split_axis=0, concat_axis=0, tiled=True)  10.4 us
    all_to_all x1, starting transfers between devices, on_device(): got = lax.all_to_all(send, 'facet', split_axis=0, concat_axis=0, tiled=True)  7.45 us
    all_to_all x1, starting transfers between devices, on_device(): lax.all_to_all(residual.reshape(facets, cap, width), 'facet', split_axis=...  4.7 us
    ppermute x2, starting transfers between devices, beside(): return lax.ppermute(value, 'facet', pairs)  4.18 us
    ppermute x1, waiting for transfers between devices, on_device(): lax.ppermute(value, 'freq', [(f, (f + d + 1) % count) for f in range(coun...  4.05 us
    unnamed x26, local copies, waits for them, and re-layouts  1.36 us
    ppermute x1, starting transfers between devices, on_device(): lax.ppermute(value, 'freq', [(f, (f + d + 1) % count) for f in range(coun...  1.32 us
  transfers between devices with their start and end apart: 5, of which 2 were waited for; matrix products, arithmetic and copies ran while one was open for 0% of the time, Pallas kernels for 19%

profile of v3, /device:TPU:1, one launch (start us, length us, event | category | flops | bytes accessed | tf_op | source)
XLA Modules:
  0.0 48.6 jit_solution(10292435460959918739)
XLA Ops:
  0.6 0.0 copy-start.6
  0.6 0.0 copy-start.7
  0.7 2.2 %shard_map.149 = (bf16[16,136,128]{2,1,0:T(8,128)(2,1)}, s32[1,256]{1,0:T(1,128)S(1)}) custom-call(s32[1,256]{1,0:T(1,128)} %bitcast.14, s32[1,256]{1,0:T(1,128)} %bitcast.15, bf16[256,512]{1,0:T(8,128)(2,1)} %seen_hbm.1), custom_call_target="tpu_custom_call" | custom-call | flops 268435456 | bytes 4194304 | tf_op jit(solution)/shard_map/pallas_call | solution.py:528
  2.8 0.0 copy-start
  2.8 0.0 copy-start.1
  2.9 0.0 copy-start.3
  2.9 0.0 copy-start.10
  2.9 7.5 %all-to-all-start = ((bf16[16,136,128]{2,1,0:T(8,128)(2,1)}), bf16[16,136,128]{2,1,0:T(8,128)(2,1)S(1)}, u32[]{:S(2)}, u32[]{:S(2)}) async-start(bf16[16,136,128]{2,1,0:T(8,128)(2,1)} %get-tuple-element.17), calls=%async_computation | async-start | bytes 1114112 | tf_op jit(solution)/shard_map/all_to_all | solution.py:576
  10.3 0.0 copy-start.2
  10.3 0.0 copy-start.4
  10.4 0.0 copy-done.6
  10.4 0.0 copy-done.7
  10.4 0.0 copy-done
  10.4 0.0 copy-done.1
  10.4 0.0 copy-done.3
  10.4 0.0 copy-done.10
  10.4 0.6 %copy-done.2 = f32[32,3,3]{0,2,1:T(4,128)S(1)} copy-done((f32[32,3,3]{0,2,1:T(4,128)S(1)}, f32[32,3,3]{0,2,1:T(4,128)}, u32[]{:S(2)}) %copy-start.2) | copy-done | bytes 1176
  11.0 0.0 copy-done.4
  11.0 2.8 %shard_map.150 = (bf16[512,512]{1,0:T(8,128)(2,1)S(1)}, bf16[512,512]{1,0:T(8,128)(2,1)S(1)}, bf16[704,224]{1,0:T(8,128)(2,1)S(1)}, bf16[144,704]{1,0:T(8,128)(2,1)S(1)}) custom-call(f32[64,2048]{1,0:T(8,128)S(1)} %copy-done, f32[64,2048]{1,0:T(8,128)S(1)} %bitcast.10, bf16[128,192]{1,0:T(8,128)(2,1)S(1)} %copy-done.7, f32[2,16,128]{2,1,0:T(8,128)S(1)} %copy-done.10, ...), custom_call_target="tpu_custom_call" | custom-call | flops 1073741824 | bytes 4194304 | tf_op jit(solution)/shard_map/pallas_call | solution.py:528
  13.8 0.0 copy-start.11
  13.9 0.7 %copy-done.11 = bf16[144,704]{1,0:T(8,128)(2,1)} copy-done((bf16[144,704]{1,0:T(8,128)(2,1)}, bf16[144,704]{1,0:T(8,128)(2,1)S(1)}, u32[]{:S(2)}) %copy-start.11) | copy-done | bytes 202776
  14.5 10.4 %all-to-all-done.got_ref = bf16[16,136,128]{2,1,0:T(8,128)(2,1)S(1)} async-done(((bf16[16,136,128]{2,1,0:T(8,128)(2,1)}), bf16[16,136,128]{2,1,0:T(8,128)(2,1)S(1)}, u32[]{:S(2)}, u32[]{:S(2)}) %all-to-all-start) | async-done | bytes 557088 | tf_op jit(solution)/shard_map/all_to_all | solution.py:576
  24.9 1.8 %shard_map.151 = (bf16[512,512]{1,0:T(8,128)(2,1)}, bf16[512,512]{1,0:T(8,128)(2,1)S(1)}, bf16[512,512]{1,0:T(8,128)(2,1)S(1)}) custom-call(bf16[16,136,128]{2,1,0:T(8,128)(2,1)S(1)} %all-to-all-done.got_ref, bf16[512,512]{1,0:T(8,128)(2,1)S(1)} %get-tuple-element.18.high_ref, bf16[512,512]{1,0:T(8,128)(2,1)S(1)} %get-tuple-element.19.low_ref), custom_call_target="tpu_custom_call" | custom-call | flops 1073741824 | bytes 4194304 | tf_op jit(solution)/shard_map/pallas_call | solution.py:528
  26.8 0.0 copy-start.5
  26.8 0.0 copy-start.8
  26.8 0.0 copy-start.9
  26.8 4.7 %all-to-all-start.1 = ((bf16[16,32,512]{2,1,0:T(8,128)(2,1)}), bf16[16,32,512]{2,1,0:T(8,128)(2,1)S(1)}, u32[]{:S(2)}, u32[]{:S(2)}) async-start(bf16[16,32,512]{2,1,0:T(8,128)(2,1)} %bitcast.6), calls=%async_computation.1 | async-start | bytes 1048576 | tf_op jit(solution)/shard_map/all_to_all | solution.py:606
  31.5 0.0 copy-done.5
  31.5 0.0 copy-done.8
  31.5 0.0 copy-done.9
  31.5 2.7 %shard_map.153 = (f32[64,1152]{1,0:T(8,128)S(1)}, bf16[64,1152]{1,0:T(8,128)(2,1)S(1)}) custom-call(bf16[512,512]{1,0:T(8,128)(2,1)S(1)} %get-tuple-element.21.res_ref, bf16[512,512]{1,0:T(8,128)(2,1)S(1)} %get-tuple-element.22.sel_ref, bf16[64,256]{1,0:T(8,128)(2,1)S(1)} %copy-done.8, f32[2,16,128]{2,1,0:T(8,128)S(1)} %copy-done.9, ...), custom_call_target="tpu_custom_call" | custom-call | flops 1073741824 | bytes 4194304 | tf_op jit(solution)/shard_map/pallas_call | solution.py:528
  34.2 1.3 %collective-permute-start = (bf16[64,1152]{1,0:T(8,128)(2,1)S(1)}, bf16[64,1152]{1,0:T(8,128)(2,1)S(1)}, u32[]{:S(2)}, u32[]{:S(2)}) collective-permute-start(bf16[64,1152]{1,0:T(8,128)(2,1)S(1)} %get-tuple-element.24), channel_id=1, source_target_pairs={{0,16},{16,0},{1,17},{17,1},{2,18},{18,2},{3,19},{19,3},{4,20},{20... | collective-permute-start | bytes 442376 | tf_op jit(solution)/shard_map/ppermute | solution.py:638
  35.6 4.1 %collective-permute-done.refs_0_ = bf16[64,1152]{1,0:T(8,128)(2,1)S(1)} collective-permute-done((bf16[64,1152]{1,0:T(8,128)(2,1)S(1)}, bf16[64,1152]{1,0:T(8,128)(2,1)S(1)}, u32[]{:S(2)}, u32[]{:S(2)}) %collective-permute-start) | collective-permute-done | bytes 147488 | tf_op jit(solution)/shard_map/ppermute | solution.py:638
  39.6 0.0 copy-start.12
  39.6 1.0 %collective-permute-start.1 = (f32[2,1152]{1,0:T(2,128)S(1)}, f32[2,1152]{1,0:T(2,128)S(1)}, u32[]{:S(2)}, u32[]{:S(2)}) collective-permute-start(f32[2,1152]{1,0:T(2,128)S(1)} %get-tuple-element.26), channel_id=1, source_target_pairs={{0,1},{1,0},{2,3},{3,2},{4,5},{5,4},{6,7},{7,6},{8,9},{9,8},{10,11... | collective-permute-start | bytes 27656 | tf_op jit(solution)/shard_map/ppermute | solution.py:635
  40.7 3.2 %collective-permute-start.2 = (f32[2,1152]{1,0:T(2,128)S(1)}, f32[2,1152]{1,0:T(2,128)S(1)}, u32[]{:S(2)}, u32[]{:S(2)}) collective-permute-start(f32[2,1152]{1,0:T(2,128)S(1)} %get-tuple-element.29), channel_id=1, source_target_pairs={{1,2},{2,1},{3,4},{4,3},{5,6},{6,5},{7,8},{8,7},{9,10},{10,9},{11,... | collective-permute-start | bytes 27656 | tf_op jit(solution)/shard_map/ppermute | solution.py:635
  43.8 0.0 collective-permute-done.1.near_ref
  43.9 0.0 copy-done.12
  43.9 1.9 %shard_map.155.sum_ref = f32[80,1152]{1,0:T(8,128)S(1)} custom-call(f32[64,1152]{1,0:T(8,128)S(1)} %get-tuple-element.25.main_ref, f32[2,1152]{1,0:T(2,128)S(1)} %collective-permute-done.1.near_ref, bf16[704,224]{1,0:T(8,128)(2,1)S(1)} %get-tuple-element.27.one_ref, bf16[144,704]{1,0:T(8,128)(2,1)S(1)} %copy-done.12), custom_call_target="tpu_custom_call" | custom-call | flops 2147483648 | bytes 4194304 | tf_op jit(solution)/shard_map/pallas_call | solution.py:528
  45.8 0.0 collective-permute-done.2.far_ref
  45.8 1.8 %shard_map.156 = f32[64,1024]{1,0:T(8,128)} custom-call(f32[80,1152]{1,0:T(8,128)S(1)} %shard_map.155.sum_ref, f32[64,1152]{1,0:T(8,128)S(1)} %get-tuple-element.25.main_ref, f32[2,1152]{1,0:T(2,128)S(1)} %collective-permute-done.2.far_ref, bf16[704,224]{1,0:T(8,128)(2,1)S(1)} %get-tuple-element.27.one_ref, bf16[144,704]{1,0:T(8,128)(2,1)S(1)} %copy-done.12), custom_call_target="tpu_custom_call" | custom-call | flops 1073741824 | bytes 4194304 | tf_op jit(solution)/shard_map/pallas_call | solution.py:528
  47.6 0.0 all-to-all-done.1
  47.6 1.0 %shard_map.152 = bf16[256,512]{1,0:T(8,128)(2,1)} custom-call(s32[1,256]{1,0:T(1,128)S(1)} %get-tuple-element.16.dest_ref, bf16[512,512]{1,0:T(8,128)(2,1)S(1)} %bitcast.8), custom_call_target="tpu_custom_call" | custom-call | flops 268435456 | bytes 4194304 | tf_op jit(solution)/shard_map/pallas_call | solution.py:528
  (1 shorter events, 0.0 us)
Async XLA Ops:
  0.6 9.7 %copy-start.6 = (bf16[2,256,256]{2,1,0:T(8,128)(2,1)S(1)}, bf16[2,256,256]{2,1,0:T(8,128)(2,1)}, u32[]{:S(2)}) copy-start(bf16[2,256,256]{2,1,0:T(8,128)(2,1)} %constant.14.clone.mat_ref) | copy-start | bytes 786436
  0.6 9.7 %copy-start.7 = (bf16[128,192]{1,0:T(8,128)(2,1)S(1)}, bf16[128,192]{1,0:T(8,128)(2,1)}, u32[]{:S(2)}) copy-start(bf16[128,192]{1,0:T(8,128)(2,1)} %constant.12.clone.row_ref) | copy-start | bytes 147460
  2.8 7.5 %copy-start = (f32[64,2048]{1,0:T(8,128)S(1)}, f32[64,2048]{1,0:T(8,128)}, u32[]{:S(2)}) copy-start(f32[64,2048]{1,0:T(8,128)} %sky_hbm.1) | copy-start | bytes 1572868
  2.8 7.5 %copy-start.1 = (f32[1,64,2048]{2,1,0:T(8,128)S(1)}, f32[1,64,2048]{2,1,0:T(8,128)}, u32[]{:S(2)}) copy-start(f32[1,64,2048]{2,1,0:T(8,128)} %param.15) | copy-start | bytes 1572868
  2.9 7.5 %copy-start.3 = (f32[32,3,3]{0,2,1:T(4,128)S(1)}, f32[32,3,3]{0,2,1:T(4,128)}, u32[]{:S(2)}) copy-start(f32[32,3,3]{0,2,1:T(4,128)} %param.21) | copy-start | bytes 3460
  2.9 7.5 %copy-start.10 = (f32[2,16,128]{2,1,0:T(8,128)S(1)}, f32[2,16,128]{2,1,0:T(8,128)}, u32[]{:S(2)}) copy-start(f32[2,16,128]{2,1,0:T(8,128)} %constant.13.clone.twist_ref) | copy-start | bytes 49156
  2.9 22.0 %all-to-all-start = ((bf16[16,136,128]{2,1,0:T(8,128)(2,1)}), bf16[16,136,128]{2,1,0:T(8,128)(2,1)S(1)}, u32[]{:S(2)}, u32[]{:S(2)}) async-start(bf16[16,136,128]{2,1,0:T(8,128)(2,1)} %get-tuple-element.17), calls=%async_computation | async-start | bytes 1114112 | tf_op jit(solution)/shard_map/all_to_all | solution.py:576
  10.3 0.7 %copy-start.2 = (f32[32,3,3]{0,2,1:T(4,128)S(1)}, f32[32,3,3]{0,2,1:T(4,128)}, u32[]{:S(2)}) copy-start(f32[32,3,3]{0,2,1:T(4,128)} %param.19) | copy-start | bytes 3460
  10.3 0.7 %copy-start.4 = (f32[32]{0:T(128)S(1)}, f32[32]{0:T(128)}, u32[]{:S(2)}) copy-start(f32[32]{0:T(128)} %param.20) | copy-start | bytes 388
  13.8 0.7 %copy-start.11 = (bf16[144,704]{1,0:T(8,128)(2,1)}, bf16[144,704]{1,0:T(8,128)(2,1)S(1)}, u32[]{:S(2)}) copy-start(bf16[144,704]{1,0:T(8,128)(2,1)S(1)} %get-tuple-element.28.two_ref) | copy-start | bytes 608260
  26.8 4.7 %copy-start.5 = (bf16[2,256,256]{2,1,0:T(8,128)(2,1)S(1)}, bf16[2,256,256]{2,1,0:T(8,128)(2,1)}, u32[]{:S(2)}) copy-start(bf16[2,256,256]{2,1,0:T(8,128)(2,1)} %constant.17.clone.mat_ref) | copy-start | bytes 786436
  26.8 4.7 %copy-start.8 = (bf16[64,256]{1,0:T(8,128)(2,1)S(1)}, bf16[64,256]{1,0:T(8,128)(2,1)}, u32[]{:S(2)}) copy-start(bf16[64,256]{1,0:T(8,128)(2,1)} %constant.15.clone.row_ref) | copy-start | bytes 98308
  26.8 4.7 %copy-start.9 = (f32[2,16,128]{2,1,0:T(8,128)S(1)}, f32[2,16,128]{2,1,0:T(8,128)}, u32[]{:S(2)}) copy-start(f32[2,16,128]{2,1,0:T(8,128)} %constant.16.clone.twist_ref) | copy-start | bytes 49156
  26.8 20.8 %all-to-all-start.1 = ((bf16[16,32,512]{2,1,0:T(8,128)(2,1)}), bf16[16,32,512]{2,1,0:T(8,128)(2,1)S(1)}, u32[]{:S(2)}, u32[]{:S(2)}) async-start(bf16[16,32,512]{2,1,0:T(8,128)(2,1)} %bitcast.6), calls=%async_computation.1 | async-start | bytes 1048576 | tf_op jit(solution)/shard_map/all_to_all | solution.py:606
  34.2 5.4 %collective-permute-start = (bf16[64,1152]{1,0:T(8,128)(2,1)S(1)}, bf16[64,1152]{1,0:T(8,128)(2,1)S(1)}, u32[]{:S(2)}, u32[]{:S(2)}) collective-permute-start(bf16[64,1152]{1,0:T(8,128)(2,1)S(1)} %get-tuple-element.24), channel_id=1, source_target_pairs={{0,16},{16,0},{1,17},{17,1},{2,18},{18,2},{3,19},{19,3},{4,20},{20... | collective-permute-start | bytes 442376 | tf_op jit(solution)/shard_map/ppermute | solution.py:638
  39.6 4.2 %copy-start.12 = (bf16[144,704]{1,0:T(8,128)(2,1)S(1)}, bf16[144,704]{1,0:T(8,128)(2,1)}, u32[]{:S(2)}) copy-start(bf16[144,704]{1,0:T(8,128)(2,1)} %copy-done.11) | copy-start | bytes 608260
  39.6 4.2 %collective-permute-start.1 = (f32[2,1152]{1,0:T(2,128)S(1)}, f32[2,1152]{1,0:T(2,128)S(1)}, u32[]{:S(2)}, u32[]{:S(2)}) collective-permute-start(f32[2,1152]{1,0:T(2,128)S(1)} %get-tuple-element.26), channel_id=1, source_target_pairs={{0,1},{1,0},{2,3},{3,2},{4,5},{5,4},{6,7},{7,6},{8,9},{9,8},{10,11... | collective-permute-start | bytes 27656 | tf_op jit(solution)/shard_map/ppermute | solution.py:635
  40.7 5.1 %collective-permute-start.2 = (f32[2,1152]{1,0:T(2,128)S(1)}, f32[2,1152]{1,0:T(2,128)S(1)}, u32[]{:S(2)}, u32[]{:S(2)}) collective-permute-start(f32[2,1152]{1,0:T(2,128)S(1)} %get-tuple-element.29), channel_id=1, source_target_pairs={{1,2},{2,1},{3,4},{4,3},{5,6},{6,5},{7,8},{8,7},{9,10},{10,9},{11,... | collective-permute-start | bytes 27656 | tf_op jit(solution)/shard_map/ppermute | solution.py:635

commit v4 on v3

--- a/solution.py
+++ b/solution.py
@@ -399,12 +399,10 @@
     two_ref[...] = jnp.concatenate(blocks, axis=0).astype(BF16)
 
 
-def band_prior(band, one_ref, two_ref, trim=None):
-    tall, width = band.shape
+def band_prior(bands, one_ref, two_ref, trim=None):
+    tall, width = bands[0].shape
     lane = iota((tall, width), 1)
     ones = jnp.where(iota((8, width), 0) < 2, 1.0, 0.0)
-    high = band.astype(BF16).astype(F32)
-    low = band - high
 
     def moved(value):
         return (
@@ -412,12 +410,17 @@
             jnp.where(lane == width - 1, 0.0, pltpu.roll(value, width - 1, 1)),
         )
 
-    shifted = []
-    for value in (high, low):
-        left, right = moved(value)
-        shifted.append([left, value, right])
-    stack = jnp.concatenate(shifted[0] + shifted[1] + shifted[0] + [ones], axis=0).astype(BF16)
-    hidden = jnp.maximum(mm(one_ref[...], stack), 0.0)
+    stacks = []
+    for band in bands:
+        high = band.astype(BF16).astype(F32)
+        shifted = []
+        for value in (high, band - high):
+            left, right = moved(value)
+            shifted.append([left, value, right])
+        stacks.append(
+            jnp.concatenate(shifted[0] + shifted[1] + shifted[0] + [ones], axis=0).astype(BF16)
+        )
+    hidden = jnp.maximum(mm(one_ref[...], jnp.concatenate(stacks, axis=1)), 0.0)
     if trim is not None:
         inner = one_ref.shape[0] // BAND
         first, last = trim
@@ -430,10 +433,14 @@
             axis=0,
         )
     taps = mm(two_ref[...], hidden.astype(BF16))
-    parts = [
-        taps[b * tall : (b + 1) * tall] + taps[(3 + b) * tall : (4 + b) * tall] for b in range(3)
-    ]
-    return parts[1] + moved(parts[0])[0] + moved(parts[2])[1]
+    shares = []
+    for i in range(len(bands)):
+        own = taps[:, i * width : (i + 1) * width]
+        parts = [
+            own[b * tall : (b + 1) * tall] + own[(3 + b) * tall : (4 + b) * tall] for b in range(3)
+        ]
+        shares.append(parts[1] + moved(parts[0])[0] + moved(parts[2])[1])
+    return shares
 
 
 def prior_kernel(main_ref, near_ref, one_ref, two_ref, sum_ref, base_ref):
@@ -448,11 +455,11 @@
     sum_ref[8 : rows + 8, :] = main
     sum_ref[rows + 8 :, :] = jnp.zeros((8, width), F32)
     spots = [slice(k * BAND + 6, k * BAND + 6 + tall) for k in range((rows + 2) // BAND)]
-    for spot in spots[1:-1]:
-        share = band_prior(base_ref[spot, :], one_ref, two_ref)
-        sum_ref[spot, :] = sum_ref[spot, :] + share
-    band = jnp.where(even, base_ref[spots[-1], :], base_ref[spots[0], :])
-    share = band_prior(band, one_ref, two_ref)
+    bands = [base_ref[spot, :] for spot in spots[1:-1]]
+    bands.append(jnp.where(even, base_ref[spots[-1], :], base_ref[spots[0], :]))
+    *inner, share = band_prior(bands, one_ref, two_ref)
+    for spot, value in zip(spots[1:-1], inner):
+        sum_ref[spot, :] = sum_ref[spot, :] + value
     sum_ref[spots[0], :] = sum_ref[spots[0], :] + jnp.where(even, 0.0, share)
     sum_ref[spots[-1], :] = sum_ref[spots[-1], :] + jnp.where(even, share, 0.0)
 
@@ -465,10 +472,14 @@
     far_ref,
     one_ref,
     two_ref,
+    dest_ref,
+    back_ref,
     out_hbm,
+    tiles_hbm,
     base_ref,
     share_ref,
     last_ref,
+    tiles_ref,
     sems,
 ):
     rows, width = main_ref.shape
@@ -487,6 +498,12 @@
         sems.at[0],
     )
     early.start()
+    placing = one_hot(
+        iota((back_ref.shape[0], dest_ref.shape[1]), 0) == dest_ref[...]
+    )
+    tiles_ref[...] = mm(placing, back_ref[...], ((0,), (0,))).astype(BF16)
+    tiles = pltpu.make_async_copy(tiles_ref, tiles_hbm, sems.at[2])
+    tiles.start()
     far = far_ref[...]
     base_ref[0:2, :] = far
     base_ref[2:tall, :] = main_ref[0:BAND, :]
@@ -494,7 +511,9 @@
     base_ref[32 + BAND : 32 + tall, :] = far
     band = jnp.where(even, base_ref[0:tall, :], base_ref[32 : 32 + tall, :])
     share_ref[0:8, :] = jnp.zeros((8, width), F32)
-    share_ref[8 : tall + 8, :] = band_prior(band, one_ref, two_ref, (place == 0, place == final))
+    share_ref[8 : tall + 8, :] = band_prior(
+        [band], one_ref, two_ref, (place == 0, place == final)
+    )[0]
     share_ref[tall + 8 : tall + 16, :] = jnp.zeros((8, width), F32)
     near_sum = jnp.where(even, sum_ref[8 : tall + 8, :], sum_ref[rows + 8 - tall : rows + 8, :])
     share = jnp.where(even, share_ref[10 : tall + 10, :], share_ref[6 : tall + 6, :])
@@ -506,14 +525,8 @@
     )
     late.start()
     early.wait()
+    tiles.wait()
     late.wait()
-
-
-def unpack_kernel(dest_ref, back_ref, out_ref):
-    tiles = dest_ref.shape[1]
-    total, _ = back_ref.shape
-    placing = one_hot(iota((total, tiles), 0) == dest_ref[...])
-    out_ref[...] = mm(placing, back_ref[...], ((0,), (0,))).astype(BF16)
 
 
 def shape(dims, dtype):
@@ -649,20 +662,19 @@
     partial = call(
         prior_kernel, shape((rows + 16, wide), F32), 1 << 31, scratch=[tall_rows]
     )(main, near, first, second)
-    (image,) = call(
+    image, tiles_out = call(
         functools.partial(edge_kernel, count, cols // count),
-        [shape((rows, cols // count), F32)],
+        [shape((rows, cols // count), F32), shape((tiles, width), BF16)],
         1 << 30,
         scratch=[
             pltpu.VMEM((64, wide), F32),
             pltpu.VMEM((BAND + 18, wide), F32),
             pltpu.VMEM((BAND + 2, wide), F32),
-            pltpu.SemaphoreType.DMA((2,)),
+            pltpu.VMEM((tiles, width), BF16),
+            pltpu.SemaphoreType.DMA((3,)),
         ],
-        saved=(0,),
-    )(partial, main, far, first, second)
-
-    tiles_out = call(unpack_kernel, shape((tiles, width), BF16), 1 << 28)(dest, returned)
+        saved=(0, 1),
+    )(partial, main, far, first, second, dest, returned)
     return tiles_out, image
 
 

time: 49.2 us -> 48.3 us (0.982)
  Pallas kernels: 14.3 us -> 13.2 us
    pallas_call x8 -> x7, Pallas kernels: 14.3 us -> 13.2 us  [run(): pl.pallas_call(kernel, out_shape=out_shape, in_specs=[far if i in loaded...]
  transfers between devices with their start and end apart: 5 -> 5, of which waited for: 2 -> 2; matrix products, arithmetic and copies ran while one was open for 0% -> 0% of each run, Pallas kernels for 19% -> 15%
where the time goes in v4:
time: 48.3 us; the launch traced here: 47.6 us
  starting transfers between devices  17.7 us (37%)
  waiting for transfers between devices  14.5 us (30%)
  Pallas kernels  13.2 us (27%)
  local copies, waits for them, and re-layouts  1.36 us (3%)
  between operations  0.86 us (2%)
    pallas_call x7, Pallas kernels, run(): pl.pallas_call(kernel, out_shape=out_shape, in_specs=[far if i in loaded...  13.2 us
    all_to_all x1, waiting for transfers between devices, on_device(): got = lax.all_to_all(send, 'facet', split_axis=0, concat_axis=0, tiled=True)  10.4 us
    all_to_all x1, starting transfers between devices, on_device(): got = lax.all_to_all(send, 'facet', split_axis=0, concat_axis=0, tiled=True)  7.45 us
    all_to_all x1, starting transfers between devices, on_device(): lax.all_to_all(residual.reshape(facets, cap, width), 'facet', split_axis=...  4.7 us
    ppermute x2, starting transfers between devices, beside(): return lax.ppermute(value, 'facet', pairs)  4.18 us
    ppermute x1, waiting for transfers between devices, on_device(): lax.ppermute(value, 'freq', [(f, (f + d + 1) % count) for f in range(coun...  4.05 us
    unnamed x26, local copies, waits for them, and re-layouts  1.36 us
    ppermute x1, starting transfers between devices, on_device(): lax.ppermute(value, 'freq', [(f, (f + d + 1) % count) for f in range(coun...  1.31 us
  transfers between devices with their start and end apart: 5, of which 2 were waited for; matrix products, arithmetic and copies ran while one was open for 0% of the time, Pallas kernels for 15%

profile of v4, /device:TPU:1, one launch (start us, length us, event | category | flops | bytes accessed | tf_op | source)
XLA Modules:
  0.0 47.6 jit_solution(5762270729458312276)
XLA Ops:
  0.6 0.0 copy-start.6
  0.6 0.0 copy-start.7
  0.7 2.2 %shard_map.149 = (bf16[16,136,128]{2,1,0:T(8,128)(2,1)}, s32[1,256]{1,0:T(1,128)S(1)}) custom-call(s32[1,256]{1,0:T(1,128)} %bitcast.14, s32[1,256]{1,0:T(1,128)} %bitcast.15, bf16[256,512]{1,0:T(8,128)(2,1)} %seen_hbm.1), custom_call_target="tpu_custom_call" | custom-call | flops 268435456 | bytes 4194304 | tf_op jit(solution)/shard_map/pallas_call | solution.py:541
  2.9 0.0 copy-start
  2.9 0.0 copy-start.1
  2.9 0.0 copy-start.3
  2.9 0.0 copy-start.10
  2.9 7.5 %all-to-all-start = ((bf16[16,136,128]{2,1,0:T(8,128)(2,1)}), bf16[16,136,128]{2,1,0:T(8,128)(2,1)S(1)}, u32[]{:S(2)}, u32[]{:S(2)}) async-start(bf16[16,136,128]{2,1,0:T(8,128)(2,1)} %get-tuple-element.18), calls=%async_computation | async-start | bytes 1114112 | tf_op jit(solution)/shard_map/all_to_all | solution.py:589
  10.4 0.0 copy-start.2
  10.4 0.0 copy-start.4
  10.4 0.0 copy-done.6
  10.4 0.0 copy-done.7
  10.4 0.0 copy-done
  10.4 0.0 copy-done.1
  10.4 0.0 copy-done.3
  10.4 0.0 copy-done.10
  10.4 0.6 %copy-done.2 = f32[32,3,3]{0,2,1:T(4,128)S(1)} copy-done((f32[32,3,3]{0,2,1:T(4,128)S(1)}, f32[32,3,3]{0,2,1:T(4,128)}, u32[]{:S(2)}) %copy-start.2) | copy-done | bytes 1176
  11.0 0.0 copy-done.4
  11.0 2.8 %shard_map.150 = (bf16[512,512]{1,0:T(8,128)(2,1)S(1)}, bf16[512,512]{1,0:T(8,128)(2,1)S(1)}, bf16[704,224]{1,0:T(8,128)(2,1)S(1)}, bf16[144,704]{1,0:T(8,128)(2,1)S(1)}) custom-call(f32[64,2048]{1,0:T(8,128)S(1)} %copy-done, f32[64,2048]{1,0:T(8,128)S(1)} %bitcast.10, bf16[128,192]{1,0:T(8,128)(2,1)S(1)} %copy-done.7, f32[2,16,128]{2,1,0:T(8,128)S(1)} %copy-done.10, ...), custom_call_target="tpu_custom_call" | custom-call | flops 1073741824 | bytes 4194304 | tf_op jit(solution)/shard_map/pallas_call | solution.py:541
  13.9 0.0 copy-start.11
  13.9 0.7 %copy-done.11 = bf16[144,704]{1,0:T(8,128)(2,1)} copy-done((bf16[144,704]{1,0:T(8,128)(2,1)}, bf16[144,704]{1,0:T(8,128)(2,1)S(1)}, u32[]{:S(2)}) %copy-start.11) | copy-done | bytes 202776
  14.5 10.4 %all-to-all-done.got_ref = bf16[16,136,128]{2,1,0:T(8,128)(2,1)S(1)} async-done(((bf16[16,136,128]{2,1,0:T(8,128)(2,1)}), bf16[16,136,128]{2,1,0:T(8,128)(2,1)S(1)}, u32[]{:S(2)}, u32[]{:S(2)}) %all-to-all-start) | async-done | bytes 557088 | tf_op jit(solution)/shard_map/all_to_all | solution.py:589
  24.9 1.8 %shard_map.151 = (bf16[512,512]{1,0:T(8,128)(2,1)}, bf16[512,512]{1,0:T(8,128)(2,1)S(1)}, bf16[512,512]{1,0:T(8,128)(2,1)S(1)}) custom-call(bf16[16,136,128]{2,1,0:T(8,128)(2,1)S(1)} %all-to-all-done.got_ref, bf16[512,512]{1,0:T(8,128)(2,1)S(1)} %get-tuple-element.19.high_ref, bf16[512,512]{1,0:T(8,128)(2,1)S(1)} %get-tuple-element.20.low_ref), custom_call_target="tpu_custom_call" | custom-call | flops 1073741824 | bytes 4194304 | tf_op jit(solution)/shard_map/pallas_call | solution.py:541
  26.8 0.0 copy-start.5
  26.8 0.0 copy-start.8
  26.8 0.0 copy-start.9
  26.8 4.7 %all-to-all-start.1 = ((bf16[16,32,512]{2,1,0:T(8,128)(2,1)}), bf16[16,32,512]{2,1,0:T(8,128)(2,1)S(1)}, u32[]{:S(2)}, u32[]{:S(2)}) async-start(bf16[16,32,512]{2,1,0:T(8,128)(2,1)} %bitcast.6), calls=%async_computation.1 | async-start | bytes 1048576 | tf_op jit(solution)/shard_map/all_to_all | solution.py:619
  31.5 0.0 copy-done.5
  31.5 0.0 copy-done.8
  31.5 0.0 copy-done.9
  31.6 2.7 %shard_map.152 = (f32[64,1152]{1,0:T(8,128)S(1)}, bf16[64,1152]{1,0:T(8,128)(2,1)S(1)}) custom-call(bf16[512,512]{1,0:T(8,128)(2,1)S(1)} %get-tuple-element.21.res_ref, bf16[512,512]{1,0:T(8,128)(2,1)S(1)} %get-tuple-element.22.sel_ref, bf16[64,256]{1,0:T(8,128)(2,1)S(1)} %copy-done.8, f32[2,16,128]{2,1,0:T(8,128)S(1)} %copy-done.9, ...), custom_call_target="tpu_custom_call" | custom-call | flops 1073741824 | bytes 4194304 | tf_op jit(solution)/shard_map/pallas_call | solution.py:541
  34.2 1.3 %collective-permute-start = (bf16[64,1152]{1,0:T(8,128)(2,1)S(1)}, bf16[64,1152]{1,0:T(8,128)(2,1)S(1)}, u32[]{:S(2)}, u32[]{:S(2)}) collective-permute-start(bf16[64,1152]{1,0:T(8,128)(2,1)S(1)} %get-tuple-element.24), channel_id=1, source_target_pairs={{0,16},{16,0},{1,17},{17,1},{2,18},{18,2},{3,19},{19,3},{4,20},{20... | collective-permute-start | bytes 442376 | tf_op jit(solution)/shard_map/ppermute | solution.py:651
  35.6 4.1 %collective-permute-done.refs_0_ = bf16[64,1152]{1,0:T(8,128)(2,1)S(1)} collective-permute-done((bf16[64,1152]{1,0:T(8,128)(2,1)S(1)}, bf16[64,1152]{1,0:T(8,128)(2,1)S(1)}, u32[]{:S(2)}, u32[]{:S(2)}) %collective-permute-start) | collective-permute-done | bytes 147488 | tf_op jit(solution)/shard_map/ppermute | solution.py:651
  39.6 0.0 copy-start.12
  39.7 1.0 %collective-permute-start.1 = (f32[2,1152]{1,0:T(2,128)S(1)}, f32[2,1152]{1,0:T(2,128)S(1)}, u32[]{:S(2)}, u32[]{:S(2)}) collective-permute-start(f32[2,1152]{1,0:T(2,128)S(1)} %get-tuple-element.26), channel_id=1, source_target_pairs={{0,1},{1,0},{2,3},{3,2},{4,5},{5,4},{6,7},{7,6},{8,9},{9,8},{10,11... | collective-permute-start | bytes 27656 | tf_op jit(solution)/shard_map/ppermute | solution.py:648
  40.7 3.2 %collective-permute-start.2 = (f32[2,1152]{1,0:T(2,128)S(1)}, f32[2,1152]{1,0:T(2,128)S(1)}, u32[]{:S(2)}, u32[]{:S(2)}) collective-permute-start(f32[2,1152]{1,0:T(2,128)S(1)} %get-tuple-element.29), channel_id=1, source_target_pairs={{1,2},{2,1},{3,4},{4,3},{5,6},{6,5},{7,8},{8,7},{9,10},{10,9},{11,... | collective-permute-start | bytes 27656 | tf_op jit(solution)/shard_map/ppermute | solution.py:648
  43.9 0.0 collective-permute-done.1.near_ref
  43.9 0.0 copy-done.12
  43.9 1.8 %shard_map.154.sum_ref = f32[80,1152]{1,0:T(8,128)S(1)} custom-call(f32[64,1152]{1,0:T(8,128)S(1)} %get-tuple-element.25.main_ref, f32[2,1152]{1,0:T(2,128)S(1)} %collective-permute-done.1.near_ref, bf16[704,224]{1,0:T(8,128)(2,1)S(1)} %get-tuple-element.27.one_ref, bf16[144,704]{1,0:T(8,128)(2,1)S(1)} %copy-done.12), custom_call_target="tpu_custom_call" | custom-call | flops 2147483648 | bytes 4194304 | tf_op jit(solution)/shard_map/pallas_call | solution.py:541
  45.6 0.0 collective-permute-done.2.far_ref
  45.7 0.0 all-to-all-done.1
  45.7 1.9 %shard_map.155 = (f32[64,1024]{1,0:T(8,128)}, bf16[256,512]{1,0:T(8,128)(2,1)}) custom-call(f32[80,1152]{1,0:T(8,128)S(1)} %shard_map.154.sum_ref, f32[64,1152]{1,0:T(8,128)S(1)} %get-tuple-element.25.main_ref, f32[2,1152]{1,0:T(2,128)S(1)} %collective-permute-done.2.far_ref, bf16[704,224]{1,0:T(8,128)(2,1)S(1)} %get-tuple-element.27.one_ref, ...), custom_call_target="tpu_custom_call" | custom-call | flops 1073741824 | bytes 4194304 | tf_op jit(solution)/shard_map/pallas_call | solution.py:541
  (1 shorter events, 0.0 us)
Async XLA Ops:
  0.6 9.7 %copy-start.6 = (bf16[2,256,256]{2,1,0:T(8,128)(2,1)S(1)}, bf16[2,256,256]{2,1,0:T(8,128)(2,1)}, u32[]{:S(2)}) copy-start(bf16[2,256,256]{2,1,0:T(8,128)(2,1)} %constant.14.clone.mat_ref) | copy-start | bytes 786436
  0.6 9.7 %copy-start.7 = (bf16[128,192]{1,0:T(8,128)(2,1)S(1)}, bf16[128,192]{1,0:T(8,128)(2,1)}, u32[]{:S(2)}) copy-start(bf16[128,192]{1,0:T(8,128)(2,1)} %constant.12.clone.row_ref) | copy-start | bytes 147460
  2.9 7.5 %copy-start = (f32[64,2048]{1,0:T(8,128)S(1)}, f32[64,2048]{1,0:T(8,128)}, u32[]{:S(2)}) copy-start(f32[64,2048]{1,0:T(8,128)} %sky_hbm.1) | copy-start | bytes 1572868
  2.9 7.5 %copy-start.1 = (f32[1,64,2048]{2,1,0:T(8,128)S(1)}, f32[1,64,2048]{2,1,0:T(8,128)}, u32[]{:S(2)}) copy-start(f32[1,64,2048]{2,1,0:T(8,128)} %param.15) | copy-start | bytes 1572868
  2.9 7.5 %copy-start.3 = (f32[32,3,3]{0,2,1:T(4,128)S(1)}, f32[32,3,3]{0,2,1:T(4,128)}, u32[]{:S(2)}) copy-start(f32[32,3,3]{0,2,1:T(4,128)} %param.21) | copy-start | bytes 3460
  2.9 7.5 %copy-start.10 = (f32[2,16,128]{2,1,0:T(8,128)S(1)}, f32[2,16,128]{2,1,0:T(8,128)}, u32[]{:S(2)}) copy-start(f32[2,16,128]{2,1,0:T(8,128)} %constant.13.clone.twist_ref) | copy-start | bytes 49156
  2.9 22.0 %all-to-all-start = ((bf16[16,136,128]{2,1,0:T(8,128)(2,1)}), bf16[16,136,128]{2,1,0:T(8,128)(2,1)S(1)}, u32[]{:S(2)}, u32[]{:S(2)}) async-start(bf16[16,136,128]{2,1,0:T(8,128)(2,1)} %get-tuple-element.18), calls=%async_computation | async-start | bytes 1114112 | tf_op jit(solution)/shard_map/all_to_all | solution.py:589
  10.4 0.7 %copy-start.2 = (f32[32,3,3]{0,2,1:T(4,128)S(1)}, f32[32,3,3]{0,2,1:T(4,128)}, u32[]{:S(2)}) copy-start(f32[32,3,3]{0,2,1:T(4,128)} %param.19) | copy-start | bytes 3460
  10.4 0.7 %copy-start.4 = (f32[32]{0:T(128)S(1)}, f32[32]{0:T(128)}, u32[]{:S(2)}) copy-start(f32[32]{0:T(128)} %param.20) | copy-start | bytes 388
  13.9 0.7 %copy-start.11 = (bf16[144,704]{1,0:T(8,128)(2,1)}, bf16[144,704]{1,0:T(8,128)(2,1)S(1)}, u32[]{:S(2)}) copy-start(bf16[144,704]{1,0:T(8,128)(2,1)S(1)} %get-tuple-element.28.two_ref) | copy-start | bytes 608260
  26.8 4.7 %copy-start.5 = (bf16[2,256,256]{2,1,0:T(8,128)(2,1)S(1)}, bf16[2,256,256]{2,1,0:T(8,128)(2,1)}, u32[]{:S(2)}) copy-start(bf16[2,256,256]{2,1,0:T(8,128)(2,1)} %constant.17.clone.mat_ref) | copy-start | bytes 786436
  26.8 4.7 %copy-start.8 = (bf16[64,256]{1,0:T(8,128)(2,1)S(1)}, bf16[64,256]{1,0:T(8,128)(2,1)}, u32[]{:S(2)}) copy-start(bf16[64,256]{1,0:T(8,128)(2,1)} %constant.15.clone.row_ref) | copy-start | bytes 98308
  26.8 4.7 %copy-start.9 = (f32[2,16,128]{2,1,0:T(8,128)S(1)}, f32[2,16,128]{2,1,0:T(8,128)}, u32[]{:S(2)}) copy-start(f32[2,16,128]{2,1,0:T(8,128)} %constant.16.clone.twist_ref) | copy-start | bytes 49156
  26.8 18.8 %all-to-all-start.1 = ((bf16[16,32,512]{2,1,0:T(8,128)(2,1)}), bf16[16,32,512]{2,1,0:T(8,128)(2,1)S(1)}, u32[]{:S(2)}, u32[]{:S(2)}) async-start(bf16[16,32,512]{2,1,0:T(8,128)(2,1)} %bitcast.6), calls=%async_computation.1 | async-start | bytes 1048576 | tf_op jit(solution)/shard_map/all_to_all | solution.py:619
  34.2 5.4 %collective-permute-start = (bf16[64,1152]{1,0:T(8,128)(2,1)S(1)}, bf16[64,1152]{1,0:T(8,128)(2,1)S(1)}, u32[]{:S(2)}, u32[]{:S(2)}) collective-permute-start(bf16[64,1152]{1,0:T(8,128)(2,1)S(1)} %get-tuple-element.24), channel_id=1, source_target_pairs={{0,16},{16,0},{1,17},{17,1},{2,18},{18,2},{3,19},{19,3},{4,20},{20... | collective-permute-start | bytes 442376 | tf_op jit(solution)/shard_map/ppermute | solution.py:651
  39.6 4.2 %copy-start.12 = (bf16[144,704]{1,0:T(8,128)(2,1)S(1)}, bf16[144,704]{1,0:T(8,128)(2,1)}, u32[]{:S(2)}) copy-start(bf16[144,704]{1,0:T(8,128)(2,1)} %copy-done.11) | copy-start | bytes 608260
  39.7 4.2 %collective-permute-start.1 = (f32[2,1152]{1,0:T(2,128)S(1)}, f32[2,1152]{1,0:T(2,128)S(1)}, u32[]{:S(2)}, u32[]{:S(2)}) collective-permute-start(f32[2,1152]{1,0:T(2,128)S(1)} %get-tuple-element.26), channel_id=1, source_target_pairs={{0,1},{1,0},{2,3},{3,2},{4,5},{5,4},{6,7},{7,6},{8,9},{9,8},{10,11... | collective-permute-start | bytes 27656 | tf_op jit(solution)/shard_map/ppermute | solution.py:648
  40.7 5.0 %collective-permute-start.2 = (f32[2,1152]{1,0:T(2,128)S(1)}, f32[2,1152]{1,0:T(2,128)S(1)}, u32[]{:S(2)}, u32[]{:S(2)}) collective-permute-start(f32[2,1152]{1,0:T(2,128)S(1)} %get-tuple-element.29), channel_id=1, source_target_pairs={{1,2},{2,1},{3,4},{4,3},{5,6},{6,5},{7,8},{8,7},{9,10},{10,9},{11,... | collective-permute-start | bytes 27656 | tf_op jit(solution)/shard_map/ppermute | solution.py:648

commit v5 on v3

--- a/solution.py
+++ b/solution.py
@@ -399,37 +399,27 @@
     two_ref[...] = jnp.concatenate(blocks, axis=0).astype(BF16)
 
 
-def band_prior(band, one_ref, two_ref, trim=None):
-    tall, width = band.shape
-    lane = iota((tall, width), 1)
-    ones = jnp.where(iota((8, width), 0) < 2, 1.0, 0.0)
+def moved(value):
+    width = value.shape[1]
+    lane = iota(value.shape, 1)
+    return (
+        jnp.where(lane == 0, 0.0, pltpu.roll(value, 1, 1)),
+        jnp.where(lane == width - 1, 0.0, pltpu.roll(value, width - 1, 1)),
+    )
+
+
+def stack_of(band):
+    ones = jnp.where(iota((8, band.shape[1]), 0) < 2, 1.0, 0.0)
     high = band.astype(BF16).astype(F32)
-    low = band - high
-
-    def moved(value):
-        return (
-            jnp.where(lane == 0, 0.0, pltpu.roll(value, 1, 1)),
-            jnp.where(lane == width - 1, 0.0, pltpu.roll(value, width - 1, 1)),
-        )
-
     shifted = []
-    for value in (high, low):
+    for value in (high, band - high):
         left, right = moved(value)
         shifted.append([left, value, right])
-    stack = jnp.concatenate(shifted[0] + shifted[1] + shifted[0] + [ones], axis=0).astype(BF16)
-    hidden = jnp.maximum(mm(one_ref[...], stack), 0.0)
-    if trim is not None:
-        inner = one_ref.shape[0] // BAND
-        first, last = trim
-        hidden = jnp.concatenate(
-            [
-                jnp.where(first, 0.0, hidden[:inner]),
-                hidden[inner:-inner],
-                jnp.where(last, 0.0, hidden[-inner:]),
-            ],
-            axis=0,
-        )
-    taps = mm(two_ref[...], hidden.astype(BF16))
+    return jnp.concatenate(shifted[0] + shifted[1] + shifted[0] + [ones], axis=0).astype(BF16)
+
+
+def share_of(taps):
+    tall = BAND + 2
     parts = [
         taps[b * tall : (b + 1) * tall] + taps[(3 + b) * tall : (4 + b) * tall] for b in range(3)
     ]
@@ -439,22 +429,25 @@
 def prior_kernel(main_ref, near_ref, one_ref, two_ref, sum_ref, base_ref):
     rows, width = main_ref.shape
     tall = BAND + 2
+    pair = 2 * one_ref.shape[0] // BAND
     main, near = main_ref[...], near_ref[...]
     even = (lax.axis_index("facet") & 1) == 0
     base_ref[8 : rows + 8, :] = main
-    base_ref[6:8, :] = near
-    base_ref[rows + 8 : rows + 10, :] = near
+    base_ref[6:8, :] = jnp.where(even, 0.0, near)
+    base_ref[rows + 8 : rows + 10, :] = jnp.where(even, near, 0.0)
     sum_ref[0:8, :] = jnp.zeros((8, width), F32)
     sum_ref[8 : rows + 8, :] = main
     sum_ref[rows + 8 :, :] = jnp.zeros((8, width), F32)
     spots = [slice(k * BAND + 6, k * BAND + 6 + tall) for k in range((rows + 2) // BAND)]
-    for spot in spots[1:-1]:
-        share = band_prior(base_ref[spot, :], one_ref, two_ref)
-        sum_ref[spot, :] = sum_ref[spot, :] + share
-    band = jnp.where(even, base_ref[spots[-1], :], base_ref[spots[0], :])
-    share = band_prior(band, one_ref, two_ref)
-    sum_ref[spots[0], :] = sum_ref[spots[0], :] + jnp.where(even, 0.0, share)
-    sum_ref[spots[-1], :] = sum_ref[spots[-1], :] + jnp.where(even, share, 0.0)
+    stack = jnp.concatenate([stack_of(base_ref[spot, :]) for spot in spots], axis=1)
+    hidden = jnp.maximum(mm(one_ref[...], stack), 0.0)
+    head, body, foot = hidden[:pair], hidden[pair:-pair], hidden[-pair:]
+    head = jnp.concatenate([jnp.where(even, 0.0, head[:, :width]), head[:, width:]], axis=1)
+    foot = jnp.concatenate([foot[:, :-width], jnp.where(even, foot[:, -width:], 0.0)], axis=1)
+    hidden = jnp.concatenate([head, body, foot], axis=0).astype(BF16)
+    taps = mm(two_ref[...], hidden)
+    for k, spot in enumerate(spots):
+        sum_ref[spot, :] = sum_ref[spot, :] + share_of(taps[:, k * width : (k + 1) * width])
 
 
 def edge_kernel(
@@ -465,55 +458,71 @@
     far_ref,
     one_ref,
     two_ref,
+    dest_ref,
+    back_ref,
     out_hbm,
+    tiles_hbm,
     base_ref,
     share_ref,
     last_ref,
+    tiles_ref,
     sems,
 ):
     rows, width = main_ref.shape
     tall = BAND + 2
+    height = one_ref.shape[0]
+    inner = height // BAND
+    pair = 2 * inner
     place = lax.axis_index("facet")
     final = lax.axis_size("facet") - 1
     even = (place & 1) == 0
     me = lax.axis_index("freq")
     start, _ = window(me, count, part * count)
     at = pl.ds(pl.multiple_of(me * part - start, LANES), part)
-    done = rows - tall
-    first = pl.multiple_of(jnp.where(even, tall, 0), 8)
+    done = rows - 8
+    first = pl.multiple_of(jnp.where(even, 8, 0), 8)
     early = pltpu.make_async_copy(
         sum_ref.at[pl.ds(pl.multiple_of(first + 8, 8), done), at],
         out_hbm.at[pl.ds(first, done), :],
         sems.at[0],
     )
     early.start()
+    placing = one_hot(iota((back_ref.shape[0], dest_ref.shape[1]), 0) == dest_ref[...])
+    tiles_ref[...] = mm(placing, back_ref[...], ((0,), (0,))).astype(BF16)
+    tiles = pltpu.make_async_copy(tiles_ref, tiles_hbm, sems.at[2])
+    tiles.start()
     far = far_ref[...]
     base_ref[0:2, :] = far
     base_ref[2:tall, :] = main_ref[0:BAND, :]
     base_ref[32 : 32 + BAND, :] = main_ref[rows - BAND : rows, :]
     base_ref[32 + BAND : 32 + tall, :] = far
     band = jnp.where(even, base_ref[0:tall, :], base_ref[32 : 32 + tall, :])
+    table = one_ref[pl.ds(pl.multiple_of(jnp.where(even, 0, height - pair), 16), pair), :]
+    hidden = jnp.maximum(mm(table, stack_of(band)), 0.0)
+    hidden = jnp.concatenate(
+        [
+            jnp.where(place == 0, 0.0, hidden[:inner]),
+            jnp.where(place == final, 0.0, hidden[inner:]),
+        ],
+        axis=0,
+    )
+    second = jnp.where(
+        even, two_ref[:, :pair].astype(F32), two_ref[:, height - pair :].astype(F32)
+    )
     share_ref[0:8, :] = jnp.zeros((8, width), F32)
-    share_ref[8 : tall + 8, :] = band_prior(band, one_ref, two_ref, (place == 0, place == final))
-    share_ref[tall + 8 : tall + 16, :] = jnp.zeros((8, width), F32)
-    near_sum = jnp.where(even, sum_ref[8 : tall + 8, :], sum_ref[rows + 8 - tall : rows + 8, :])
-    share = jnp.where(even, share_ref[10 : tall + 10, :], share_ref[6 : tall + 6, :])
+    share_ref[8 : tall + 8, :] = share_of(mm(second.astype(BF16), hidden.astype(BF16)))
+    near_sum = jnp.where(even, sum_ref[8:16, :], sum_ref[rows : rows + 8, :])
+    share = jnp.where(even, share_ref[10:18, :], share_ref[tall - 2 : tall + 6, :])
     last_ref[...] = near_sum + share
     late = pltpu.make_async_copy(
         last_ref.at[:, at],
-        out_hbm.at[pl.ds(pl.multiple_of(jnp.where(even, 0, done), 8), tall), :],
+        out_hbm.at[pl.ds(pl.multiple_of(jnp.where(even, 0, done), 8), 8), :],
         sems.at[1],
     )
     late.start()
     early.wait()
+    tiles.wait()
     late.wait()
-
-
-def unpack_kernel(dest_ref, back_ref, out_ref):
-    tiles = dest_ref.shape[1]
-    total, _ = back_ref.shape
-    placing = one_hot(iota((total, tiles), 0) == dest_ref[...])
-    out_ref[...] = mm(placing, back_ref[...], ((0,), (0,))).astype(BF16)
 
 
 def shape(dims, dtype):
@@ -647,22 +656,21 @@
     near = beside(near, lambda p: p ^ 1)
     tall_rows = pltpu.VMEM((rows + 16, wide), F32)
     partial = call(
-        prior_kernel, shape((rows + 16, wide), F32), 1 << 31, scratch=[tall_rows]
+        prior_kernel, shape((rows + 16, wide), F32), 1 << 31, scratch=[tall_rows], limit=32
     )(main, near, first, second)
-    (image,) = call(
+    image, tiles_out = call(
         functools.partial(edge_kernel, count, cols // count),
-        [shape((rows, cols // count), F32)],
+        [shape((rows, cols // count), F32), shape((tiles, width), BF16)],
         1 << 30,
         scratch=[
             pltpu.VMEM((64, wide), F32),
-            pltpu.VMEM((BAND + 18, wide), F32),
-            pltpu.VMEM((BAND + 2, wide), F32),
-            pltpu.SemaphoreType.DMA((2,)),
+            pltpu.VMEM((BAND + 10, wide), F32),
+            pltpu.VMEM((8, wide), F32),
+            pltpu.VMEM((tiles, width), BF16),
+            pltpu.SemaphoreType.DMA((3,)),
         ],
-        saved=(0,),
-    )(partial, main, far, first, second)
-
-    tiles_out = call(unpack_kernel, shape((tiles, width), BF16), 1 << 28)(dest, returned)
+        saved=(0, 1),
+    )(partial, main, far, first, second, dest, returned)
     return tiles_out, image
 
 

time: 49.2 us -> 48.3 us (0.982)
  Pallas kernels: 14.3 us -> 13.5 us
    pallas_call x8 -> x7, Pallas kernels: 14.3 us -> 13.5 us  [run(): pl.pallas_call(kernel, out_shape=out_shape, in_specs=[far if i in loaded...]
  transfers between devices with their start and end apart: 5 -> 5, of which waited for: 2 -> 2; matrix products, arithmetic and copies ran while one was open for 0% -> 0% of each run, Pallas kernels for 19% -> 17%
where the time goes in v5:
time: 48.3 us; the launch traced here: 47.9 us
  starting transfers between devices  17.7 us (37%)
  waiting for transfers between devices  14.5 us (30%)
  Pallas kernels  13.5 us (28%)
  local copies, waits for them, and re-layouts  1.36 us (3%)
  between operations  0.88 us (2%)
    pallas_call x7, Pallas kernels, run(): pl.pallas_call(kernel, out_shape=out_shape, in_specs=[far if i in loaded...  13.5 us
    all_to_all x1, waiting for transfers between devices, on_device(): got = lax.all_to_all(send, 'facet', split_axis=0, concat_axis=0, tiled=True)  10.4 us
    all_to_all x1, starting transfers between devices, on_device(): got = lax.all_to_all(send, 'facet', split_axis=0, concat_axis=0, tiled=True)  7.45 us
    all_to_all x1, starting transfers between devices, on_device(): lax.all_to_all(residual.reshape(facets, cap, width), 'facet', split_axis=...  4.7 us
    ppermute x2, starting transfers between devices, beside(): return lax.ppermute(value, 'facet', pairs)  4.18 us
    ppermute x1, waiting for transfers between devices, on_device(): lax.ppermute(value, 'freq', [(f, (f + d + 1) % count) for f in range(coun...  4.05 us
    unnamed x26, local copies, waits for them, and re-layouts  1.36 us
    ppermute x1, starting transfers between devices, on_device(): lax.ppermute(value, 'freq', [(f, (f + d + 1) % count) for f in range(coun...  1.31 us
  transfers between devices with their start and end apart: 5, of which 2 were waited for; matrix products, arithmetic and copies ran while one was open for 0% of the time, Pallas kernels for 17%

profile of v5, /device:TPU:1, one launch (start us, length us, event | category | flops | bytes accessed | tf_op | source)
XLA Modules:
  0.0 47.9 jit_solution(14989354725942595050)
XLA Ops:
  0.6 0.0 copy-start.6
  0.6 0.0 copy-start.7
  0.7 2.2 %shard_map.149 = (bf16[16,136,128]{2,1,0:T(8,128)(2,1)}, s32[1,256]{1,0:T(1,128)S(1)}) custom-call(s32[1,256]{1,0:T(1,128)} %bitcast.14, s32[1,256]{1,0:T(1,128)} %bitcast.15, bf16[256,512]{1,0:T(8,128)(2,1)} %seen_hbm.1), custom_call_target="tpu_custom_call" | custom-call | flops 268435456 | bytes 4194304 | tf_op jit(solution)/shard_map/pallas_call | solution.py:537
  2.9 0.0 copy-start
  2.9 0.0 copy-start.1
  2.9 0.0 copy-start.3
  2.9 0.0 copy-start.10
  2.9 7.5 %all-to-all-start = ((bf16[16,136,128]{2,1,0:T(8,128)(2,1)}), bf16[16,136,128]{2,1,0:T(8,128)(2,1)S(1)}, u32[]{:S(2)}, u32[]{:S(2)}) async-start(bf16[16,136,128]{2,1,0:T(8,128)(2,1)} %get-tuple-element.18), calls=%async_computation | async-start | bytes 1114112 | tf_op jit(solution)/shard_map/all_to_all | solution.py:585
  10.4 0.0 copy-start.2
  10.4 0.0 copy-start.4
  10.4 0.0 copy-done.6
  10.4 0.0 copy-done.7
  10.4 0.0 copy-done
  10.4 0.0 copy-done.1
  10.4 0.0 copy-done.3
  10.4 0.0 copy-done.10
  10.4 0.6 %copy-done.2 = f32[32,3,3]{0,2,1:T(4,128)S(1)} copy-done((f32[32,3,3]{0,2,1:T(4,128)S(1)}, f32[32,3,3]{0,2,1:T(4,128)}, u32[]{:S(2)}) %copy-start.2) | copy-done | bytes 1176
  11.0 0.0 copy-done.4
  11.0 2.8 %shard_map.150 = (bf16[512,512]{1,0:T(8,128)(2,1)S(1)}, bf16[512,512]{1,0:T(8,128)(2,1)S(1)}, bf16[704,224]{1,0:T(8,128)(2,1)S(1)}, bf16[144,704]{1,0:T(8,128)(2,1)S(1)}) custom-call(f32[64,2048]{1,0:T(8,128)S(1)} %copy-done, f32[64,2048]{1,0:T(8,128)S(1)} %bitcast.10, bf16[128,192]{1,0:T(8,128)(2,1)S(1)} %copy-done.7, f32[2,16,128]{2,1,0:T(8,128)S(1)} %copy-done.10, ...), custom_call_target="tpu_custom_call" | custom-call | flops 1073741824 | bytes 4194304 | tf_op jit(solution)/shard_map/pallas_call | solution.py:537
  13.9 0.0 copy-start.11
  13.9 0.7 %copy-done.11 = bf16[144,704]{1,0:T(8,128)(2,1)} copy-done((bf16[144,704]{1,0:T(8,128)(2,1)}, bf16[144,704]{1,0:T(8,128)(2,1)S(1)}, u32[]{:S(2)}) %copy-start.11) | copy-done | bytes 202776
  14.5 10.4 %all-to-all-done.got_ref = bf16[16,136,128]{2,1,0:T(8,128)(2,1)S(1)} async-done(((bf16[16,136,128]{2,1,0:T(8,128)(2,1)}), bf16[16,136,128]{2,1,0:T(8,128)(2,1)S(1)}, u32[]{:S(2)}, u32[]{:S(2)}) %all-to-all-start) | async-done | bytes 557088 | tf_op jit(solution)/shard_map/all_to_all | solution.py:585
  24.9 1.8 %shard_map.151 = (bf16[512,512]{1,0:T(8,128)(2,1)}, bf16[512,512]{1,0:T(8,128)(2,1)S(1)}, bf16[512,512]{1,0:T(8,128)(2,1)S(1)}) custom-call(bf16[16,136,128]{2,1,0:T(8,128)(2,1)S(1)} %all-to-all-done.got_ref, bf16[512,512]{1,0:T(8,128)(2,1)S(1)} %get-tuple-element.19.high_ref, bf16[512,512]{1,0:T(8,128)(2,1)S(1)} %get-tuple-element.20.low_ref), custom_call_target="tpu_custom_call" | custom-call | flops 1073741824 | bytes 4194304 | tf_op jit(solution)/shard_map/pallas_call | solution.py:537
  26.8 0.0 copy-start.5
  26.8 0.0 copy-start.8
  26.8 0.0 copy-start.9
  26.8 4.7 %all-to-all-start.1 = ((bf16[16,32,512]{2,1,0:T(8,128)(2,1)}), bf16[16,32,512]{2,1,0:T(8,128)(2,1)S(1)}, u32[]{:S(2)}, u32[]{:S(2)}) async-start(bf16[16,32,512]{2,1,0:T(8,128)(2,1)} %bitcast.6), calls=%async_computation.1 | async-start | bytes 1048576 | tf_op jit(solution)/shard_map/all_to_all | solution.py:615
  31.5 0.0 copy-done.5
  31.5 0.0 copy-done.8
  31.5 0.0 copy-done.9
  31.6 2.7 %shard_map.152 = (f32[64,1152]{1,0:T(8,128)S(1)}, bf16[64,1152]{1,0:T(8,128)(2,1)S(1)}) custom-call(bf16[512,512]{1,0:T(8,128)(2,1)S(1)} %get-tuple-element.21.res_ref, bf16[512,512]{1,0:T(8,128)(2,1)S(1)} %get-tuple-element.22.sel_ref, bf16[64,256]{1,0:T(8,128)(2,1)S(1)} %copy-done.8, f32[2,16,128]{2,1,0:T(8,128)S(1)} %copy-done.9, ...), custom_call_target="tpu_custom_call" | custom-call | flops 1073741824 | bytes 4194304 | tf_op jit(solution)/shard_map/pallas_call | solution.py:537
  34.2 1.3 %collective-permute-start = (bf16[64,1152]{1,0:T(8,128)(2,1)S(1)}, bf16[64,1152]{1,0:T(8,128)(2,1)S(1)}, u32[]{:S(2)}, u32[]{:S(2)}) collective-permute-start(bf16[64,1152]{1,0:T(8,128)(2,1)S(1)} %get-tuple-element.24), channel_id=1, source_target_pairs={{0,16},{16,0},{1,17},{17,1},{2,18},{18,2},{3,19},{19,3},{4,20},{20... | collective-permute-start | bytes 442376 | tf_op jit(solution)/shard_map/ppermute | solution.py:647
  35.6 4.1 %collective-permute-done.refs_0_ = bf16[64,1152]{1,0:T(8,128)(2,1)S(1)} collective-permute-done((bf16[64,1152]{1,0:T(8,128)(2,1)S(1)}, bf16[64,1152]{1,0:T(8,128)(2,1)S(1)}, u32[]{:S(2)}, u32[]{:S(2)}) %collective-permute-start) | collective-permute-done | bytes 147488 | tf_op jit(solution)/shard_map/ppermute | solution.py:647
  39.6 0.0 copy-start.12
  39.7 1.0 %collective-permute-start.1 = (f32[2,1152]{1,0:T(2,128)S(1)}, f32[2,1152]{1,0:T(2,128)S(1)}, u32[]{:S(2)}, u32[]{:S(2)}) collective-permute-start(f32[2,1152]{1,0:T(2,128)S(1)} %get-tuple-element.26), channel_id=1, source_target_pairs={{0,1},{1,0},{2,3},{3,2},{4,5},{5,4},{6,7},{7,6},{8,9},{9,8},{10,11... | collective-permute-start | bytes 27656 | tf_op jit(solution)/shard_map/ppermute | solution.py:644
  40.7 3.2 %collective-permute-start.2 = (f32[2,1152]{1,0:T(2,128)S(1)}, f32[2,1152]{1,0:T(2,128)S(1)}, u32[]{:S(2)}, u32[]{:S(2)}) collective-permute-start(f32[2,1152]{1,0:T(2,128)S(1)} %get-tuple-element.29), channel_id=1, source_target_pairs={{1,2},{2,1},{3,4},{4,3},{5,6},{6,5},{7,8},{8,7},{9,10},{10,9},{11,... | collective-permute-start | bytes 27656 | tf_op jit(solution)/shard_map/ppermute | solution.py:644
  43.9 0.0 collective-permute-done.1.near_ref
  43.9 0.0 copy-done.12
  43.9 2.5 %shard_map.154.sum_ref = f32[80,1152]{1,0:T(8,128)S(1)} custom-call(f32[64,1152]{1,0:T(8,128)S(1)} %get-tuple-element.25.main_ref, f32[2,1152]{1,0:T(2,128)S(1)} %collective-permute-done.1.near_ref, bf16[704,224]{1,0:T(8,128)(2,1)S(1)} %get-tuple-element.27.one_ref, bf16[144,704]{1,0:T(8,128)(2,1)S(1)} %copy-done.12), custom_call_target="tpu_custom_call" | custom-call | flops 2147483648 | bytes 4194304 | tf_op jit(solution)/shard_map/pallas_call | solution.py:537
  46.4 0.0 collective-permute-done.2.far_ref
  46.4 0.0 all-to-all-done.1
  46.4 1.4 %shard_map.155 = (f32[64,1024]{1,0:T(8,128)}, bf16[256,512]{1,0:T(8,128)(2,1)}) custom-call(f32[80,1152]{1,0:T(8,128)S(1)} %shard_map.154.sum_ref, f32[64,1152]{1,0:T(8,128)S(1)} %get-tuple-element.25.main_ref, f32[2,1152]{1,0:T(2,128)S(1)} %collective-permute-done.2.far_ref, bf16[704,224]{1,0:T(8,128)(2,1)S(1)} %get-tuple-element.27.one_ref, ...), custom_call_target="tpu_custom_call" | custom-call | flops 1073741824 | bytes 4194304 | tf_op jit(solution)/shard_map/pallas_call | solution.py:537
  (1 shorter events, 0.0 us)
Async XLA Ops:
  0.6 9.7 %copy-start.6 = (bf16[2,256,256]{2,1,0:T(8,128)(2,1)S(1)}, bf16[2,256,256]{2,1,0:T(8,128)(2,1)}, u32[]{:S(2)}) copy-start(bf16[2,256,256]{2,1,0:T(8,128)(2,1)} %constant.14.clone.mat_ref) | copy-start | bytes 786436
  0.6 9.7 %copy-start.7 = (bf16[128,192]{1,0:T(8,128)(2,1)S(1)}, bf16[128,192]{1,0:T(8,128)(2,1)}, u32[]{:S(2)}) copy-start(bf16[128,192]{1,0:T(8,128)(2,1)} %constant.12.clone.row_ref) | copy-start | bytes 147460
  2.9 7.5 %copy-start = (f32[64,2048]{1,0:T(8,128)S(1)}, f32[64,2048]{1,0:T(8,128)}, u32[]{:S(2)}) copy-start(f32[64,2048]{1,0:T(8,128)} %sky_hbm.1) | copy-start | bytes 1572868
  2.9 7.5 %copy-start.1 = (f32[1,64,2048]{2,1,0:T(8,128)S(1)}, f32[1,64,2048]{2,1,0:T(8,128)}, u32[]{:S(2)}) copy-start(f32[1,64,2048]{2,1,0:T(8,128)} %param.15) | copy-start | bytes 1572868
  2.9 7.5 %copy-start.3 = (f32[32,3,3]{0,2,1:T(4,128)S(1)}, f32[32,3,3]{0,2,1:T(4,128)}, u32[]{:S(2)}) copy-start(f32[32,3,3]{0,2,1:T(4,128)} %param.21) | copy-start | bytes 3460
  2.9 7.5 %copy-start.10 = (f32[2,16,128]{2,1,0:T(8,128)S(1)}, f32[2,16,128]{2,1,0:T(8,128)}, u32[]{:S(2)}) copy-start(f32[2,16,128]{2,1,0:T(8,128)} %constant.13.clone.twist_ref) | copy-start | bytes 49156
  2.9 22.0 %all-to-all-start = ((bf16[16,136,128]{2,1,0:T(8,128)(2,1)}), bf16[16,136,128]{2,1,0:T(8,128)(2,1)S(1)}, u32[]{:S(2)}, u32[]{:S(2)}) async-start(bf16[16,136,128]{2,1,0:T(8,128)(2,1)} %get-tuple-element.18), calls=%async_computation | async-start | bytes 1114112 | tf_op jit(solution)/shard_map/all_to_all | solution.py:585
  10.4 0.7 %copy-start.2 = (f32[32,3,3]{0,2,1:T(4,128)S(1)}, f32[32,3,3]{0,2,1:T(4,128)}, u32[]{:S(2)}) copy-start(f32[32,3,3]{0,2,1:T(4,128)} %param.19) | copy-start | bytes 3460
  10.4 0.7 %copy-start.4 = (f32[32]{0:T(128)S(1)}, f32[32]{0:T(128)}, u32[]{:S(2)}) copy-start(f32[32]{0:T(128)} %param.20) | copy-start | bytes 388
  13.9 0.7 %copy-start.11 = (bf16[144,704]{1,0:T(8,128)(2,1)}, bf16[144,704]{1,0:T(8,128)(2,1)S(1)}, u32[]{:S(2)}) copy-start(bf16[144,704]{1,0:T(8,128)(2,1)S(1)} %get-tuple-element.28.two_ref) | copy-start | bytes 608260
  26.8 4.7 %copy-start.5 = (bf16[2,256,256]{2,1,0:T(8,128)(2,1)S(1)}, bf16[2,256,256]{2,1,0:T(8,128)(2,1)}, u32[]{:S(2)}) copy-start(bf16[2,256,256]{2,1,0:T(8,128)(2,1)} %constant.17.clone.mat_ref) | copy-start | bytes 786436
  26.8 4.7 %copy-start.8 = (bf16[64,256]{1,0:T(8,128)(2,1)S(1)}, bf16[64,256]{1,0:T(8,128)(2,1)}, u32[]{:S(2)}) copy-start(bf16[64,256]{1,0:T(8,128)(2,1)} %constant.15.clone.row_ref) | copy-start | bytes 98308
  26.8 4.7 %copy-start.9 = (f32[2,16,128]{2,1,0:T(8,128)S(1)}, f32[2,16,128]{2,1,0:T(8,128)}, u32[]{:S(2)}) copy-start(f32[2,16,128]{2,1,0:T(8,128)} %constant.16.clone.twist_ref) | copy-start | bytes 49156
  26.8 19.6 %all-to-all-start.1 = ((bf16[16,32,512]{2,1,0:T(8,128)(2,1)}), bf16[16,32,512]{2,1,0:T(8,128)(2,1)S(1)}, u32[]{:S(2)}, u32[]{:S(2)}) async-start(bf16[16,32,512]{2,1,0:T(8,128)(2,1)} %bitcast.6), calls=%async_computation.1 | async-start | bytes 1048576 | tf_op jit(solution)/shard_map/all_to_all | solution.py:615
  34.2 5.4 %collective-permute-start = (bf16[64,1152]{1,0:T(8,128)(2,1)S(1)}, bf16[64,1152]{1,0:T(8,128)(2,1)S(1)}, u32[]{:S(2)}, u32[]{:S(2)}) collective-permute-start(bf16[64,1152]{1,0:T(8,128)(2,1)S(1)} %get-tuple-element.24), channel_id=1, source_target_pairs={{0,16},{16,0},{1,17},{17,1},{2,18},{18,2},{3,19},{19,3},{4,20},{20... | collective-permute-start | bytes 442376 | tf_op jit(solution)/shard_map/ppermute | solution.py:647
  39.6 4.2 %copy-start.12 = (bf16[144,704]{1,0:T(8,128)(2,1)S(1)}, bf16[144,704]{1,0:T(8,128)(2,1)}, u32[]{:S(2)}) copy-start(bf16[144,704]{1,0:T(8,128)(2,1)} %copy-done.11) | copy-start | bytes 608260
  39.7 4.2 %collective-permute-start.1 = (f32[2,1152]{1,0:T(2,128)S(1)}, f32[2,1152]{1,0:T(2,128)S(1)}, u32[]{:S(2)}, u32[]{:S(2)}) collective-permute-start(f32[2,1152]{1,0:T(2,128)S(1)} %get-tuple-element.26), channel_id=1, source_target_pairs={{0,1},{1,0},{2,3},{3,2},{4,5},{5,4},{6,7},{7,6},{8,9},{9,8},{10,11... | collective-permute-start | bytes 27656 | tf_op jit(solution)/shard_map/ppermute | solution.py:644
  40.7 5.7 %collective-permute-start.2 = (f32[2,1152]{1,0:T(2,128)S(1)}, f32[2,1152]{1,0:T(2,128)S(1)}, u32[]{:S(2)}, u32[]{:S(2)}) collective-permute-start(f32[2,1152]{1,0:T(2,128)S(1)} %get-tuple-element.29), channel_id=1, source_target_pairs={{1,2},{2,1},{3,4},{4,3},{5,6},{6,5},{7,8},{8,7},{9,10},{10,9},{11,... | collective-permute-start | bytes 27656 | tf_op jit(solution)/shard_map/ppermute | solution.py:644

commit v6 on v5

--- a/solution.py
+++ b/solution.py
@@ -232,31 +232,33 @@
 
 
 def residual_kernel(facets, cap, got_ref, high_ref, low_ref, res_hbm, sel_ref, own_ref, sems):
-    total = facets * cap
     slots = high_ref.shape[1]
     parts = high_ref.shape[0] // LANES
-    code = got_ref[:, parts * cap : parts * cap + 8, :].astype(F32).reshape(facets * 8, LANES)
-    source = iota((total, facets * 8), 0) // cap
-    spread = mm(one_hot(iota((total, facets * 8), 1) == source * 8), code.astype(BF16))
-    lane = iota((total, LANES), 1)
-    rank = iota((total, LANES), 0) % cap
-    kept = jnp.where((lane & (LANES // 2 - 1)) == rank, spread, 0.0).astype(BF16)
-    digit = jnp.where(iota((LANES, slots), 0) < LANES // 2, 16.0, 1.0).astype(BF16)
-    code_all = mm(kept, digit)
-    sel = one_hot(code_all.astype(jnp.int32) == iota((total, slots), 1) + 1)
-    sel_ref[...] = sel
+    pieces = sems.shape[0]
+    here = facets // pieces
+    count = here * cap
     contract = ((1,), (1,))
-    predicted = mm(sel, high_ref[...], contract) + mm(sel, low_ref[...], contract)
+    lane = iota((count, LANES), 1)
+    rank = iota((count, LANES), 0) % cap
+    mine = (lane & (LANES // 2 - 1)) == rank
+    digit = jnp.where(iota((LANES, LANES), 0) < LANES // 2, 16.0, 1.0).astype(BF16)
     saves = []
-    pieces = sems.shape[0]
     for i in range(pieces):
-        here = facets // pieces
-        at = slice(i * here * cap, (i + 1) * here * cap)
+        group = slice(i * here, (i + 1) * here)
+        at = slice(i * count, (i + 1) * count)
+        code = got_ref[group, parts * cap : parts * cap + 8, :].astype(F32)
+        code = jnp.broadcast_to(code[:, 0:1, :], (here, cap, LANES)).reshape(count, LANES)
+        slot = mm(jnp.where(mine, code, 0.0).astype(BF16), digit).astype(jnp.int32) - 1
+        sel = jnp.concatenate(
+            [one_hot(slot == lane + r * LANES) for r in range(slots // LANES)], axis=1
+        )
+        sel_ref[at, :] = sel
+        predicted = mm(sel, high_ref[...], contract) + mm(sel, low_ref[...], contract)
         for part in range(parts):
             cols = slice(part * LANES, (part + 1) * LANES)
-            seen = got_ref[i * here : (i + 1) * here, part * cap : (part + 1) * cap, :]
-            seen = seen.astype(F32).reshape(here * cap, LANES)
-            own_ref[at, cols] = (predicted[at, cols] - seen).astype(BF16)
+            seen = got_ref[group, part * cap : (part + 1) * cap, :]
+            seen = seen.astype(F32).reshape(count, LANES)
+            own_ref[at, cols] = (predicted[:, cols] - seen).astype(BF16)
         save = pltpu.make_async_copy(own_ref.at[at, :], res_hbm.at[at, :], sems.at[i])
         save.start()
         saves.append(save)
@@ -609,7 +611,7 @@
         functools.partial(residual_kernel, facets, cap),
         [shape((total, width), BF16), shape((total, slots), BF16), shape((total, width), BF16)],
         1 << 30,
-        scratch=[pltpu.SemaphoreType.DMA((4,))],
+        scratch=[pltpu.SemaphoreType.DMA((2,))],
         saved=(0,),
     )(got, *(pltpu.with_memory_space_constraint(value, pltpu.VMEM) for value in (high, low)))
     returned = lax.all_to_all(

time: 48.3 us -> 48.3 us (level)
  no operation moved by 1% of the time
where the time goes in v6:
time: 48.3 us; the launch traced here: 47.8 us
  starting transfers between devices  17.6 us (36%)
  waiting for transfers between devices  14.5 us (30%)
  Pallas kernels  13.5 us (28%)
  local copies, waits for them, and re-layouts  1.36 us (3%)
  between operations  0.88 us (2%)
    pallas_call x7, Pallas kernels, run(): pl.pallas_call(kernel, out_shape=out_shape, in_specs=[far if i in loaded...  13.5 us
    all_to_all x1, waiting for transfers between devices, on_device(): got = lax.all_to_all(send, 'facet', split_axis=0, concat_axis=0, tiled=True)  10.4 us
    all_to_all x1, starting transfers between devices, on_device(): got = lax.all_to_all(send, 'facet', split_axis=0, concat_axis=0, tiled=True)  7.45 us
    all_to_all x1, starting transfers between devices, on_device(): lax.all_to_all(residual.reshape(facets, cap, width), 'facet', split_axis=...  4.7 us
    ppermute x2, starting transfers between devices, beside(): return lax.ppermute(value, 'facet', pairs)  4.19 us
    ppermute x1, waiting for transfers between devices, on_device(): lax.ppermute(value, 'freq', [(f, (f + d + 1) % count) for f in range(coun...  4.06 us
    unnamed x26, local copies, waits for them, and re-layouts  1.36 us
    ppermute x1, starting transfers between devices, on_device(): lax.ppermute(value, 'freq', [(f, (f + d + 1) % count) for f in range(coun...  1.31 us
  transfers between devices with their start and end apart: 5, of which 2 were waited for; matrix products, arithmetic and copies ran while one was open for 0% of the time, Pallas kernels for 17%

profile of v6, /device:TPU:1, one launch (start us, length us, event | category | flops | bytes accessed | tf_op | source)
XLA Modules:
  0.0 47.8 jit_solution(11521398715204387183)
XLA Ops:
  0.6 0.0 copy-start.6
  0.6 0.0 copy-start.7
  0.7 2.2 %shard_map.149 = (bf16[16,136,128]{2,1,0:T(8,128)(2,1)}, s32[1,256]{1,0:T(1,128)S(1)}) custom-call(s32[1,256]{1,0:T(1,128)} %bitcast.14, s32[1,256]{1,0:T(1,128)} %bitcast.15, bf16[256,512]{1,0:T(8,128)(2,1)} %seen_hbm.1), custom_call_target="tpu_custom_call" | custom-call | flops 268435456 | bytes 4194304 | tf_op jit(solution)/shard_map/pallas_call | solution.py:539
  2.9 0.0 copy-start
  2.9 0.0 copy-start.1
  2.9 0.0 copy-start.3
  2.9 0.0 copy-start.10
  2.9 7.5 %all-to-all-start = ((bf16[16,136,128]{2,1,0:T(8,128)(2,1)}), bf16[16,136,128]{2,1,0:T(8,128)(2,1)S(1)}, u32[]{:S(2)}, u32[]{:S(2)}) async-start(bf16[16,136,128]{2,1,0:T(8,128)(2,1)} %get-tuple-element.18), calls=%async_computation | async-start | bytes 1114112 | tf_op jit(solution)/shard_map/all_to_all | solution.py:587
  10.4 0.0 copy-start.2
  10.4 0.0 copy-start.4
  10.4 0.0 copy-done.6
  10.4 0.0 copy-done.7
  10.4 0.0 copy-done
  10.4 0.0 copy-done.1
  10.4 0.0 copy-done.3
  10.4 0.0 copy-done.10
  10.4 0.6 %copy-done.2 = f32[32,3,3]{0,2,1:T(4,128)S(1)} copy-done((f32[32,3,3]{0,2,1:T(4,128)S(1)}, f32[32,3,3]{0,2,1:T(4,128)}, u32[]{:S(2)}) %copy-start.2) | copy-done | bytes 1176
  11.0 0.0 copy-done.4
  11.0 2.8 %shard_map.150 = (bf16[512,512]{1,0:T(8,128)(2,1)S(1)}, bf16[512,512]{1,0:T(8,128)(2,1)S(1)}, bf16[704,224]{1,0:T(8,128)(2,1)S(1)}, bf16[144,704]{1,0:T(8,128)(2,1)S(1)}) custom-call(f32[64,2048]{1,0:T(8,128)S(1)} %copy-done, f32[64,2048]{1,0:T(8,128)S(1)} %bitcast.10, bf16[128,192]{1,0:T(8,128)(2,1)S(1)} %copy-done.7, f32[2,16,128]{2,1,0:T(8,128)S(1)} %copy-done.10, ...), custom_call_target="tpu_custom_call" | custom-call | flops 1073741824 | bytes 4194304 | tf_op jit(solution)/shard_map/pallas_call | solution.py:539
  13.9 0.0 copy-start.11
  13.9 0.7 %copy-done.11 = bf16[144,704]{1,0:T(8,128)(2,1)} copy-done((bf16[144,704]{1,0:T(8,128)(2,1)}, bf16[144,704]{1,0:T(8,128)(2,1)S(1)}, u32[]{:S(2)}) %copy-start.11) | copy-done | bytes 202776
  14.5 10.4 %all-to-all-done.got_ref = bf16[16,136,128]{2,1,0:T(8,128)(2,1)S(1)} async-done(((bf16[16,136,128]{2,1,0:T(8,128)(2,1)}), bf16[16,136,128]{2,1,0:T(8,128)(2,1)S(1)}, u32[]{:S(2)}, u32[]{:S(2)}) %all-to-all-start) | async-done | bytes 557088 | tf_op jit(solution)/shard_map/all_to_all | solution.py:587
  24.9 1.8 %shard_map.151 = (bf16[512,512]{1,0:T(8,128)(2,1)}, bf16[512,512]{1,0:T(8,128)(2,1)S(1)}, bf16[512,512]{1,0:T(8,128)(2,1)S(1)}) custom-call(bf16[16,136,128]{2,1,0:T(8,128)(2,1)S(1)} %all-to-all-done.got_ref, bf16[512,512]{1,0:T(8,128)(2,1)S(1)} %get-tuple-element.19.high_ref, bf16[512,512]{1,0:T(8,128)(2,1)S(1)} %get-tuple-element.20.low_ref), custom_call_target="tpu_custom_call" | custom-call | flops 1073741824 | bytes 4194304 | tf_op jit(solution)/shard_map/pallas_call | solution.py:539
  26.8 0.0 copy-start.5
  26.8 0.0 copy-start.8
  26.8 0.0 copy-start.9
  26.8 4.7 %all-to-all-start.1 = ((bf16[16,32,512]{2,1,0:T(8,128)(2,1)}), bf16[16,32,512]{2,1,0:T(8,128)(2,1)S(1)}, u32[]{:S(2)}, u32[]{:S(2)}) async-start(bf16[16,32,512]{2,1,0:T(8,128)(2,1)} %bitcast.6), calls=%async_computation.1 | async-start | bytes 1048576 | tf_op jit(solution)/shard_map/all_to_all | solution.py:617
  31.5 0.0 copy-done.5
  31.5 0.0 copy-done.8
  31.5 0.0 copy-done.9
  31.5 2.7 %shard_map.152 = (f32[64,1152]{1,0:T(8,128)S(1)}, bf16[64,1152]{1,0:T(8,128)(2,1)S(1)}) custom-call(bf16[512,512]{1,0:T(8,128)(2,1)S(1)} %get-tuple-element.21.res_ref, bf16[512,512]{1,0:T(8,128)(2,1)S(1)} %get-tuple-element.22.sel_ref, bf16[64,256]{1,0:T(8,128)(2,1)S(1)} %copy-done.8, f32[2,16,128]{2,1,0:T(8,128)S(1)} %copy-done.9, ...), custom_call_target="tpu_custom_call" | custom-call | flops 1073741824 | bytes 4194304 | tf_op jit(solution)/shard_map/pallas_call | solution.py:539
  34.2 1.3 %collective-permute-start = (bf16[64,1152]{1,0:T(8,128)(2,1)S(1)}, bf16[64,1152]{1,0:T(8,128)(2,1)S(1)}, u32[]{:S(2)}, u32[]{:S(2)}) collective-permute-start(bf16[64,1152]{1,0:T(8,128)(2,1)S(1)} %get-tuple-element.24), channel_id=1, source_target_pairs={{0,16},{16,0},{1,17},{17,1},{2,18},{18,2},{3,19},{19,3},{4,20},{20... | collective-permute-start | bytes 442376 | tf_op jit(solution)/shard_map/ppermute | solution.py:649
  35.5 4.1 %collective-permute-done.refs_0_ = bf16[64,1152]{1,0:T(8,128)(2,1)S(1)} collective-permute-done((bf16[64,1152]{1,0:T(8,128)(2,1)S(1)}, bf16[64,1152]{1,0:T(8,128)(2,1)S(1)}, u32[]{:S(2)}, u32[]{:S(2)}) %collective-permute-start) | collective-permute-done | bytes 147488 | tf_op jit(solution)/shard_map/ppermute | solution.py:649
  39.6 0.0 copy-start.12
  39.6 1.0 %collective-permute-start.1 = (f32[2,1152]{1,0:T(2,128)S(1)}, f32[2,1152]{1,0:T(2,128)S(1)}, u32[]{:S(2)}, u32[]{:S(2)}) collective-permute-start(f32[2,1152]{1,0:T(2,128)S(1)} %get-tuple-element.26), channel_id=1, source_target_pairs={{0,1},{1,0},{2,3},{3,2},{4,5},{5,4},{6,7},{7,6},{8,9},{9,8},{10,11... | collective-permute-start | bytes 27656 | tf_op jit(solution)/shard_map/ppermute | solution.py:646
  40.7 3.2 %collective-permute-start.2 = (f32[2,1152]{1,0:T(2,128)S(1)}, f32[2,1152]{1,0:T(2,128)S(1)}, u32[]{:S(2)}, u32[]{:S(2)}) collective-permute-start(f32[2,1152]{1,0:T(2,128)S(1)} %get-tuple-element.29), channel_id=1, source_target_pairs={{1,2},{2,1},{3,4},{4,3},{5,6},{6,5},{7,8},{8,7},{9,10},{10,9},{11,... | collective-permute-start | bytes 27656 | tf_op jit(solution)/shard_map/ppermute | solution.py:646
  43.8 0.0 collective-permute-done.1.near_ref
  43.8 0.0 copy-done.12
  43.8 2.6 %shard_map.154.sum_ref = f32[80,1152]{1,0:T(8,128)S(1)} custom-call(f32[64,1152]{1,0:T(8,128)S(1)} %get-tuple-element.25.main_ref, f32[2,1152]{1,0:T(2,128)S(1)} %collective-permute-done.1.near_ref, bf16[704,224]{1,0:T(8,128)(2,1)S(1)} %get-tuple-element.27.one_ref, bf16[144,704]{1,0:T(8,128)(2,1)S(1)} %copy-done.12), custom_call_target="tpu_custom_call" | custom-call | flops 2147483648 | bytes 4194304 | tf_op jit(solution)/shard_map/pallas_call | solution.py:539
  46.4 0.0 collective-permute-done.2.far_ref
  46.4 0.0 all-to-all-done.1
  46.4 1.4 %shard_map.155 = (f32[64,1024]{1,0:T(8,128)}, bf16[256,512]{1,0:T(8,128)(2,1)}) custom-call(f32[80,1152]{1,0:T(8,128)S(1)} %shard_map.154.sum_ref, f32[64,1152]{1,0:T(8,128)S(1)} %get-tuple-element.25.main_ref, f32[2,1152]{1,0:T(2,128)S(1)} %collective-permute-done.2.far_ref, bf16[704,224]{1,0:T(8,128)(2,1)S(1)} %get-tuple-element.27.one_ref, ...), custom_call_target="tpu_custom_call" | custom-call | flops 1073741824 | bytes 4194304 | tf_op jit(solution)/shard_map/pallas_call | solution.py:539
  (1 shorter events, 0.0 us)
Async XLA Ops:
  0.6 9.7 %copy-start.6 = (bf16[2,256,256]{2,1,0:T(8,128)(2,1)S(1)}, bf16[2,256,256]{2,1,0:T(8,128)(2,1)}, u32[]{:S(2)}) copy-start(bf16[2,256,256]{2,1,0:T(8,128)(2,1)} %constant.14.clone.mat_ref) | copy-start | bytes 786436
  0.6 9.7 %copy-start.7 = (bf16[128,192]{1,0:T(8,128)(2,1)S(1)}, bf16[128,192]{1,0:T(8,128)(2,1)}, u32[]{:S(2)}) copy-start(bf16[128,192]{1,0:T(8,128)(2,1)} %constant.12.clone.row_ref) | copy-start | bytes 147460
  2.9 7.5 %copy-start = (f32[64,2048]{1,0:T(8,128)S(1)}, f32[64,2048]{1,0:T(8,128)}, u32[]{:S(2)}) copy-start(f32[64,2048]{1,0:T(8,128)} %sky_hbm.1) | copy-start | bytes 1572868
  2.9 7.5 %copy-start.1 = (f32[1,64,2048]{2,1,0:T(8,128)S(1)}, f32[1,64,2048]{2,1,0:T(8,128)}, u32[]{:S(2)}) copy-start(f32[1,64,2048]{2,1,0:T(8,128)} %param.15) | copy-start | bytes 1572868
  2.9 7.5 %copy-start.3 = (f32[32,3,3]{0,2,1:T(4,128)S(1)}, f32[32,3,3]{0,2,1:T(4,128)}, u32[]{:S(2)}) copy-start(f32[32,3,3]{0,2,1:T(4,128)} %param.21) | copy-start | bytes 3460
  2.9 7.5 %copy-start.10 = (f32[2,16,128]{2,1,0:T(8,128)S(1)}, f32[2,16,128]{2,1,0:T(8,128)}, u32[]{:S(2)}) copy-start(f32[2,16,128]{2,1,0:T(8,128)} %constant.13.clone.twist_ref) | copy-start | bytes 49156
  2.9 22.0 %all-to-all-start = ((bf16[16,136,128]{2,1,0:T(8,128)(2,1)}), bf16[16,136,128]{2,1,0:T(8,128)(2,1)S(1)}, u32[]{:S(2)}, u32[]{:S(2)}) async-start(bf16[16,136,128]{2,1,0:T(8,128)(2,1)} %get-tuple-element.18), calls=%async_computation | async-start | bytes 1114112 | tf_op jit(solution)/shard_map/all_to_all | solution.py:587
  10.4 0.7 %copy-start.2 = (f32[32,3,3]{0,2,1:T(4,128)S(1)}, f32[32,3,3]{0,2,1:T(4,128)}, u32[]{:S(2)}) copy-start(f32[32,3,3]{0,2,1:T(4,128)} %param.19) | copy-start | bytes 3460
  10.4 0.7 %copy-start.4 = (f32[32]{0:T(128)S(1)}, f32[32]{0:T(128)}, u32[]{:S(2)}) copy-start(f32[32]{0:T(128)} %param.20) | copy-start | bytes 388
  13.9 0.7 %copy-start.11 = (bf16[144,704]{1,0:T(8,128)(2,1)}, bf16[144,704]{1,0:T(8,128)(2,1)S(1)}, u32[]{:S(2)}) copy-start(bf16[144,704]{1,0:T(8,128)(2,1)S(1)} %get-tuple-element.28.two_ref) | copy-start | bytes 608260
  26.8 4.7 %copy-start.5 = (bf16[2,256,256]{2,1,0:T(8,128)(2,1)S(1)}, bf16[2,256,256]{2,1,0:T(8,128)(2,1)}, u32[]{:S(2)}) copy-start(bf16[2,256,256]{2,1,0:T(8,128)(2,1)} %constant.17.clone.mat_ref) | copy-start | bytes 786436
  26.8 4.7 %copy-start.8 = (bf16[64,256]{1,0:T(8,128)(2,1)S(1)}, bf16[64,256]{1,0:T(8,128)(2,1)}, u32[]{:S(2)}) copy-start(bf16[64,256]{1,0:T(8,128)(2,1)} %constant.15.clone.row_ref) | copy-start | bytes 98308
  26.8 4.7 %copy-start.9 = (f32[2,16,128]{2,1,0:T(8,128)S(1)}, f32[2,16,128]{2,1,0:T(8,128)}, u32[]{:S(2)}) copy-start(f32[2,16,128]{2,1,0:T(8,128)} %constant.16.clone.twist_ref) | copy-start | bytes 49156
  26.8 19.6 %all-to-all-start.1 = ((bf16[16,32,512]{2,1,0:T(8,128)(2,1)}), bf16[16,32,512]{2,1,0:T(8,128)(2,1)S(1)}, u32[]{:S(2)}, u32[]{:S(2)}) async-start(bf16[16,32,512]{2,1,0:T(8,128)(2,1)} %bitcast.6), calls=%async_computation.1 | async-start | bytes 1048576 | tf_op jit(solution)/shard_map/all_to_all | solution.py:617
  34.2 5.4 %collective-permute-start = (bf16[64,1152]{1,0:T(8,128)(2,1)S(1)}, bf16[64,1152]{1,0:T(8,128)(2,1)S(1)}, u32[]{:S(2)}, u32[]{:S(2)}) collective-permute-start(bf16[64,1152]{1,0:T(8,128)(2,1)S(1)} %get-tuple-element.24), channel_id=1, source_target_pairs={{0,16},{16,0},{1,17},{17,1},{2,18},{18,2},{3,19},{19,3},{4,20},{20... | collective-permute-start | bytes 442376 | tf_op jit(solution)/shard_map/ppermute | solution.py:649
  39.6 4.3 %copy-start.12 = (bf16[144,704]{1,0:T(8,128)(2,1)S(1)}, bf16[144,704]{1,0:T(8,128)(2,1)}, u32[]{:S(2)}) copy-start(bf16[144,704]{1,0:T(8,128)(2,1)} %copy-done.11) | copy-start | bytes 608260
  39.6 4.2 %collective-permute-start.1 = (f32[2,1152]{1,0:T(2,128)S(1)}, f32[2,1152]{1,0:T(2,128)S(1)}, u32[]{:S(2)}, u32[]{:S(2)}) collective-permute-start(f32[2,1152]{1,0:T(2,128)S(1)} %get-tuple-element.26), channel_id=1, source_target_pairs={{0,1},{1,0},{2,3},{3,2},{4,5},{5,4},{6,7},{7,6},{8,9},{9,8},{10,11... | collective-permute-start | bytes 27656 | tf_op jit(solution)/shard_map/ppermute | solution.py:646
  40.7 5.8 %collective-permute-start.2 = (f32[2,1152]{1,0:T(2,128)S(1)}, f32[2,1152]{1,0:T(2,128)S(1)}, u32[]{:S(2)}, u32[]{:S(2)}) collective-permute-start(f32[2,1152]{1,0:T(2,128)S(1)} %get-tuple-element.29), channel_id=1, source_target_pairs={{1,2},{2,1},{3,4},{4,3},{5,6},{6,5},{7,8},{8,7},{9,10},{10,9},{11,... | collective-permute-start | bytes 27656 | tf_op jit(solution)/shard_map/ppermute | solution.py:646

commit v7 on v6

--- a/solution.py
+++ b/solution.py
@@ -188,12 +188,16 @@
     first_ref,
     bias_ref,
     second_ref,
+    dest_ref,
     high_ref,
     low_ref,
     one_ref,
     two_ref,
+    place_ref,
     part_ref,
 ):
+    spots = iota(place_ref.shape[::-1], 0)
+    place_ref[...] = jnp.where(spots == dest_ref[...], 1.0, 0.0).T.astype(BF16)
     prepare(first_ref, bias_ref, second_ref, one_ref, two_ref)
     rows, cols = sky_ref.shape
     outer = cols // LANES
@@ -460,7 +464,7 @@
     far_ref,
     one_ref,
     two_ref,
-    dest_ref,
+    place_ref,
     back_ref,
     out_hbm,
     tiles_hbm,
@@ -489,8 +493,7 @@
         sems.at[0],
     )
     early.start()
-    placing = one_hot(iota((back_ref.shape[0], dest_ref.shape[1]), 0) == dest_ref[...])
-    tiles_ref[...] = mm(placing, back_ref[...], ((0,), (0,))).astype(BF16)
+    tiles_ref[...] = mm(place_ref[...], back_ref[...]).astype(BF16)
     tiles = pltpu.make_async_copy(tiles_ref, tiles_hbm, sems.at[2])
     tiles.start()
     far = far_ref[...]
@@ -586,13 +589,14 @@
     )
     got = lax.all_to_all(send, "facet", split_axis=0, concat_axis=0, tiled=True)
 
-    high, low, first, second = call(
+    high, low, first, second, placed = call(
         forward_kernel,
         [
             shape((width, slots), BF16),
             shape((width, slots), BF16),
             shape((hidden * BAND, 9 * (BAND + 2) + 8), BF16),
             shape((6 * (BAND + 2), hidden * BAND), BF16),
+            shape((tiles, total), BF16),
         ],
         1 << 30,
         scratch=[pltpu.VMEM((2, width, slots), BF16)],
@@ -605,6 +609,7 @@
         conv_first.transpose(1, 2, 0),
         bias_first.reshape(1, hidden),
         conv_second.transpose(1, 2, 0),
+        dest,
     )
 
     residual, select, own = call(
@@ -672,7 +677,7 @@
             pltpu.SemaphoreType.DMA((3,)),
         ],
         saved=(0, 1),
-    )(partial, main, far, first, second, dest, returned)
+    )(partial, main, far, first, second, placed, returned)
     return tiles_out, image
 
 

time: 48.3 us -> 48.3 us (level)
  local copies, waits for them, and re-layouts: 1.36 us -> 2.07 us
  waiting for transfers between devices: 14.5 us -> 13.8 us
    unnamed x26 -> x30, local copies, waits for them, and re-layouts: 1.36 us -> 2.07 us
    all_to_all x1, waiting for transfers between devices: 10.4 us -> 9.7 us  [on_device(): got = lax.all_to_all(send, 'facet', split_axis=0, concat_axis=0, tiled=True)]
where the time goes in v7:
time: 48.3 us; the launch traced here: 47.8 us
  starting transfers between devices  17.6 us (36%)
  waiting for transfers between devices  13.8 us (29%)
  Pallas kernels  13.5 us (28%)
  local copies, waits for them, and re-layouts  2.07 us (4%)
  between operations  0.89 us (2%)
    pallas_call x7, Pallas kernels, run(): pl.pallas_call(kernel, out_shape=out_shape, in_specs=[far if i in loaded...  13.5 us
    all_to_all x1, waiting for transfers between devices, on_device(): got = lax.all_to_all(send, 'facet', split_axis=0, concat_axis=0, tiled=True)  9.7 us
    all_to_all x1, starting transfers between devices, on_device(): got = lax.all_to_all(send, 'facet', split_axis=0, concat_axis=0, tiled=True)  7.45 us
    all_to_all x1, starting transfers between devices, on_device(): lax.all_to_all(residual.reshape(facets, cap, width), 'facet', split_axis=...  4.7 us
    ppermute x2, starting transfers between devices, beside(): return lax.ppermute(value, 'facet', pairs)  4.18 us
    ppermute x1, waiting for transfers between devices, on_device(): lax.ppermute(value, 'freq', [(f, (f + d + 1) % count) for f in range(coun...  4.06 us
    unnamed x30, local copies, waits for them, and re-layouts  2.07 us
    ppermute x1, starting transfers between devices, on_device(): lax.ppermute(value, 'freq', [(f, (f + d + 1) % count) for f in range(coun...  1.31 us
  transfers between devices with their start and end apart: 5, of which 2 were waited for; matrix products, arithmetic and copies ran while one was open for 0% of the time, Pallas kernels for 17%

profile of v7, /device:TPU:1, one launch (start us, length us, event | category | flops | bytes accessed | tf_op | source)
XLA Modules:
  0.0 47.8 jit_solution(4914897362422837803)
XLA Ops:
  0.6 0.0 copy-start.6
  0.6 0.0 copy-start.7
  0.7 2.2 %shard_map.149 = (bf16[16,136,128]{2,1,0:T(8,128)(2,1)}, s32[1,256]{1,0:T(1,128)S(1)}) custom-call(s32[1,256]{1,0:T(1,128)} %bitcast.14, s32[1,256]{1,0:T(1,128)} %bitcast.15, bf16[256,512]{1,0:T(8,128)(2,1)} %seen_hbm.1), custom_call_target="tpu_custom_call" | custom-call | flops 268435456 | bytes 4194304 | tf_op jit(solution)/shard_map/pallas_call | solution.py:542
  2.9 0.0 copy-start
  2.9 0.0 copy-start.1
  2.9 0.0 copy-start.3
  2.9 0.0 copy-start.10
  2.9 7.5 %all-to-all-start = ((bf16[16,136,128]{2,1,0:T(8,128)(2,1)}), bf16[16,136,128]{2,1,0:T(8,128)(2,1)S(1)}, u32[]{:S(2)}, u32[]{:S(2)}) async-start(bf16[16,136,128]{2,1,0:T(8,128)(2,1)} %get-tuple-element.19), calls=%async_computation | async-start | bytes 1114112 | tf_op jit(solution)/shard_map/all_to_all | solution.py:590
  10.4 0.0 copy-start.2
  10.4 0.0 copy-start.4
  10.4 0.0 copy-done.6
  10.4 0.0 copy-done.7
  10.4 0.0 copy-done
  10.4 0.0 copy-done.1
  10.4 0.0 copy-done.3
  10.4 0.0 copy-done.10
  10.4 0.6 %copy-done.2 = f32[32,3,3]{0,2,1:T(4,128)S(1)} copy-done((f32[32,3,3]{0,2,1:T(4,128)S(1)}, f32[32,3,3]{0,2,1:T(4,128)}, u32[]{:S(2)}) %copy-start.2) | copy-done | bytes 1176
  11.1 0.0 copy-done.4
  11.1 2.8 %shard_map.150 = (bf16[512,512]{1,0:T(8,128)(2,1)S(1)}, bf16[512,512]{1,0:T(8,128)(2,1)S(1)}, bf16[704,224]{1,0:T(8,128)(2,1)S(1)}, bf16[144,704]{1,0:T(8,128)(2,1)S(1)}, bf16[256,512]{1,0:T(8,128)(2,1)S(1)}) custom-call(f32[64,2048]{1,0:T(8,128)S(1)} %copy-done, f32[64,2048]{1,0:T(8,128)S(1)} %bitcast.10, bf16[128,192]{1,0:T(8,128)(2,1)S(1)} %copy-done.7, ...), custom_call_target="tpu_custom_call" | custom-call | flops 1073741824 | bytes 4194304 | tf_op jit(solution)/shard_map/pallas_call | solution.py:542
  13.9 0.0 copy-start.11
  13.9 0.7 %copy-done.11 = bf16[256,512]{1,0:T(8,128)(2,1)} copy-done((bf16[256,512]{1,0:T(8,128)(2,1)}, bf16[256,512]{1,0:T(8,128)(2,1)S(1)}, u32[]{:S(2)}) %copy-start.11) | copy-done | bytes 262168
  14.6 0.0 copy-start.13
  14.6 0.7 %copy-done.13 = bf16[144,704]{1,0:T(8,128)(2,1)} copy-done((bf16[144,704]{1,0:T(8,128)(2,1)}, bf16[144,704]{1,0:T(8,128)(2,1)S(1)}, u32[]{:S(2)}) %copy-start.13) | copy-done | bytes 202776
  15.3 9.7 %all-to-all-done.got_ref = bf16[16,136,128]{2,1,0:T(8,128)(2,1)S(1)} async-done(((bf16[16,136,128]{2,1,0:T(8,128)(2,1)}), bf16[16,136,128]{2,1,0:T(8,128)(2,1)S(1)}, u32[]{:S(2)}, u32[]{:S(2)}) %all-to-all-start) | async-done | bytes 557088 | tf_op jit(solution)/shard_map/all_to_all | solution.py:590
  24.9 1.8 %shard_map.151 = (bf16[512,512]{1,0:T(8,128)(2,1)}, bf16[512,512]{1,0:T(8,128)(2,1)S(1)}, bf16[512,512]{1,0:T(8,128)(2,1)S(1)}) custom-call(bf16[16,136,128]{2,1,0:T(8,128)(2,1)S(1)} %all-to-all-done.got_ref, bf16[512,512]{1,0:T(8,128)(2,1)S(1)} %get-tuple-element.21.high_ref, bf16[512,512]{1,0:T(8,128)(2,1)S(1)} %get-tuple-element.22.low_ref), custom_call_target="tpu_custom_call" | custom-call | flops 1073741824 | bytes 4194304 | tf_op jit(solution)/shard_map/pallas_call | solution.py:542
  26.8 0.0 copy-start.5
  26.8 0.0 copy-start.8
  26.8 0.0 copy-start.9
  26.8 4.7 %all-to-all-start.1 = ((bf16[16,32,512]{2,1,0:T(8,128)(2,1)}), bf16[16,32,512]{2,1,0:T(8,128)(2,1)S(1)}, u32[]{:S(2)}, u32[]{:S(2)}) async-start(bf16[16,32,512]{2,1,0:T(8,128)(2,1)} %bitcast.6), calls=%async_computation.1 | async-start | bytes 1048576 | tf_op jit(solution)/shard_map/all_to_all | solution.py:622
  31.5 0.0 copy-done.5
  31.5 0.0 copy-done.8
  31.5 0.0 copy-done.9
  31.5 2.7 %shard_map.152 = (f32[64,1152]{1,0:T(8,128)S(1)}, bf16[64,1152]{1,0:T(8,128)(2,1)S(1)}) custom-call(bf16[512,512]{1,0:T(8,128)(2,1)S(1)} %get-tuple-element.23.res_ref, bf16[512,512]{1,0:T(8,128)(2,1)S(1)} %get-tuple-element.24.sel_ref, bf16[64,256]{1,0:T(8,128)(2,1)S(1)} %copy-done.8, f32[2,16,128]{2,1,0:T(8,128)S(1)} %copy-done.9, ...), custom_call_target="tpu_custom_call" | custom-call | flops 1073741824 | bytes 4194304 | tf_op jit(solution)/shard_map/pallas_call | solution.py:542
  34.2 1.3 %collective-permute-start = (bf16[64,1152]{1,0:T(8,128)(2,1)S(1)}, bf16[64,1152]{1,0:T(8,128)(2,1)S(1)}, u32[]{:S(2)}, u32[]{:S(2)}) collective-permute-start(bf16[64,1152]{1,0:T(8,128)(2,1)S(1)} %get-tuple-element.26), channel_id=1, source_target_pairs={{0,16},{16,0},{1,17},{17,1},{2,18},{18,2},{3,19},{19,3},{4,20},{20... | collective-permute-start | bytes 442376 | tf_op jit(solution)/shard_map/ppermute | solution.py:654
  35.5 4.1 %collective-permute-done.refs_0_ = bf16[64,1152]{1,0:T(8,128)(2,1)S(1)} collective-permute-done((bf16[64,1152]{1,0:T(8,128)(2,1)S(1)}, bf16[64,1152]{1,0:T(8,128)(2,1)S(1)}, u32[]{:S(2)}, u32[]{:S(2)}) %collective-permute-start) | collective-permute-done | bytes 147488 | tf_op jit(solution)/shard_map/ppermute | solution.py:654
  39.6 0.0 copy-start.14
  39.6 1.0 %collective-permute-start.1 = (f32[2,1152]{1,0:T(2,128)S(1)}, f32[2,1152]{1,0:T(2,128)S(1)}, u32[]{:S(2)}, u32[]{:S(2)}) collective-permute-start(f32[2,1152]{1,0:T(2,128)S(1)} %get-tuple-element.28), channel_id=1, source_target_pairs={{0,1},{1,0},{2,3},{3,2},{4,5},{5,4},{6,7},{7,6},{8,9},{9,8},{10,11... | collective-permute-start | bytes 27656 | tf_op jit(solution)/shard_map/ppermute | solution.py:651
  40.7 3.2 %collective-permute-start.2 = (f32[2,1152]{1,0:T(2,128)S(1)}, f32[2,1152]{1,0:T(2,128)S(1)}, u32[]{:S(2)}, u32[]{:S(2)}) collective-permute-start(f32[2,1152]{1,0:T(2,128)S(1)} %get-tuple-element.31), channel_id=1, source_target_pairs={{1,2},{2,1},{3,4},{4,3},{5,6},{6,5},{7,8},{8,7},{9,10},{10,9},{11,... | collective-permute-start | bytes 27656 | tf_op jit(solution)/shard_map/ppermute | solution.py:651
  43.8 0.0 collective-permute-done.1.near_ref
  43.8 0.0 copy-done.14
  43.8 0.0 copy-start.12
  43.9 2.6 %shard_map.154.sum_ref = f32[80,1152]{1,0:T(8,128)S(1)} custom-call(f32[64,1152]{1,0:T(8,128)S(1)} %get-tuple-element.27.main_ref, f32[2,1152]{1,0:T(2,128)S(1)} %collective-permute-done.1.near_ref, bf16[704,224]{1,0:T(8,128)(2,1)S(1)} %get-tuple-element.29.one_ref, bf16[144,704]{1,0:T(8,128)(2,1)S(1)} %copy-done.14), custom_call_target="tpu_custom_call" | custom-call | flops 2147483648 | bytes 4194304 | tf_op jit(solution)/shard_map/pallas_call | solution.py:542
  46.4 0.0 collective-permute-done.2.far_ref
  46.4 0.0 all-to-all-done.1
  46.4 0.0 copy-done.12
  46.4 1.4 %shard_map.155 = (f32[64,1024]{1,0:T(8,128)}, bf16[256,512]{1,0:T(8,128)(2,1)}) custom-call(f32[80,1152]{1,0:T(8,128)S(1)} %shard_map.154.sum_ref, f32[64,1152]{1,0:T(8,128)S(1)} %get-tuple-element.27.main_ref, f32[2,1152]{1,0:T(2,128)S(1)} %collective-permute-done.2.far_ref, bf16[704,224]{1,0:T(8,128)(2,1)S(1)} %get-tuple-element.29.one_ref, ...), custom_call_target="tpu_custom_call" | custom-call | flops 1073741824 | bytes 4194304 | tf_op jit(solution)/shard_map/pallas_call | solution.py:542
  (1 shorter events, 0.0 us)
Async XLA Ops:
  0.6 9.8 %copy-start.6 = (bf16[2,256,256]{2,1,0:T(8,128)(2,1)S(1)}, bf16[2,256,256]{2,1,0:T(8,128)(2,1)}, u32[]{:S(2)}) copy-start(bf16[2,256,256]{2,1,0:T(8,128)(2,1)} %constant.14.clone.mat_ref) | copy-start | bytes 786436
  0.6 9.8 %copy-start.7 = (bf16[128,192]{1,0:T(8,128)(2,1)S(1)}, bf16[128,192]{1,0:T(8,128)(2,1)}, u32[]{:S(2)}) copy-start(bf16[128,192]{1,0:T(8,128)(2,1)} %constant.12.clone.row_ref) | copy-start | bytes 147460
  2.9 7.5 %copy-start = (f32[64,2048]{1,0:T(8,128)S(1)}, f32[64,2048]{1,0:T(8,128)}, u32[]{:S(2)}) copy-start(f32[64,2048]{1,0:T(8,128)} %sky_hbm.1) | copy-start | bytes 1572868
  2.9 7.5 %copy-start.1 = (f32[1,64,2048]{2,1,0:T(8,128)S(1)}, f32[1,64,2048]{2,1,0:T(8,128)}, u32[]{:S(2)}) copy-start(f32[1,64,2048]{2,1,0:T(8,128)} %param.15) | copy-start | bytes 1572868
  2.9 7.5 %copy-start.3 = (f32[32,3,3]{0,2,1:T(4,128)S(1)}, f32[32,3,3]{0,2,1:T(4,128)}, u32[]{:S(2)}) copy-start(f32[32,3,3]{0,2,1:T(4,128)} %param.21) | copy-start | bytes 3460
  2.9 7.5 %copy-start.10 = (f32[2,16,128]{2,1,0:T(8,128)S(1)}, f32[2,16,128]{2,1,0:T(8,128)}, u32[]{:S(2)}) copy-start(f32[2,16,128]{2,1,0:T(8,128)} %constant.13.clone.twist_ref) | copy-start | bytes 49156
  2.9 22.0 %all-to-all-start = ((bf16[16,136,128]{2,1,0:T(8,128)(2,1)}), bf16[16,136,128]{2,1,0:T(8,128)(2,1)S(1)}, u32[]{:S(2)}, u32[]{:S(2)}) async-start(bf16[16,136,128]{2,1,0:T(8,128)(2,1)} %get-tuple-element.19), calls=%async_computation | async-start | bytes 1114112 | tf_op jit(solution)/shard_map/all_to_all | solution.py:590
  10.4 0.7 %copy-start.2 = (f32[32,3,3]{0,2,1:T(4,128)S(1)}, f32[32,3,3]{0,2,1:T(4,128)}, u32[]{:S(2)}) copy-start(f32[32,3,3]{0,2,1:T(4,128)} %param.19) | copy-start | bytes 3460
  10.4 0.7 %copy-start.4 = (f32[32]{0:T(128)S(1)}, f32[32]{0:T(128)}, u32[]{:S(2)}) copy-start(f32[32]{0:T(128)} %param.20) | copy-start | bytes 388
  13.9 0.7 %copy-start.11 = (bf16[256,512]{1,0:T(8,128)(2,1)}, bf16[256,512]{1,0:T(8,128)(2,1)S(1)}, u32[]{:S(2)}) copy-start(bf16[256,512]{1,0:T(8,128)(2,1)S(1)} %get-tuple-element.32.place_ref) | copy-start | bytes 786436
  14.6 0.7 %copy-start.13 = (bf16[144,704]{1,0:T(8,128)(2,1)}, bf16[144,704]{1,0:T(8,128)(2,1)S(1)}, u32[]{:S(2)}) copy-start(bf16[144,704]{1,0:T(8,128)(2,1)S(1)} %get-tuple-element.30.two_ref) | copy-start | bytes 608260
  26.8 4.7 %copy-start.5 = (bf16[2,256,256]{2,1,0:T(8,128)(2,1)S(1)}, bf16[2,256,256]{2,1,0:T(8,128)(2,1)}, u32[]{:S(2)}) copy-start(bf16[2,256,256]{2,1,0:T(8,128)(2,1)} %constant.17.clone.mat_ref) | copy-start | bytes 786436
  26.8 4.7 %copy-start.8 = (bf16[64,256]{1,0:T(8,128)(2,1)S(1)}, bf16[64,256]{1,0:T(8,128)(2,1)}, u32[]{:S(2)}) copy-start(bf16[64,256]{1,0:T(8,128)(2,1)} %constant.15.clone.row_ref) | copy-start | bytes 98308
  26.8 4.7 %copy-start.9 = (f32[2,16,128]{2,1,0:T(8,128)S(1)}, f32[2,16,128]{2,1,0:T(8,128)}, u32[]{:S(2)}) copy-start(f32[2,16,128]{2,1,0:T(8,128)} %constant.16.clone.twist_ref) | copy-start | bytes 49156
  26.8 19.6 %all-to-all-start.1 = ((bf16[16,32,512]{2,1,0:T(8,128)(2,1)}), bf16[16,32,512]{2,1,0:T(8,128)(2,1)S(1)}, u32[]{:S(2)}, u32[]{:S(2)}) async-start(bf16[16,32,512]{2,1,0:T(8,128)(2,1)} %bitcast.6), calls=%async_computation.1 | async-start | bytes 1048576 | tf_op jit(solution)/shard_map/all_to_all | solution.py:622
  34.2 5.4 %collective-permute-start = (bf16[64,1152]{1,0:T(8,128)(2,1)S(1)}, bf16[64,1152]{1,0:T(8,128)(2,1)S(1)}, u32[]{:S(2)}, u32[]{:S(2)}) collective-permute-start(bf16[64,1152]{1,0:T(8,128)(2,1)S(1)} %get-tuple-element.26), channel_id=1, source_target_pairs={{0,16},{16,0},{1,17},{17,1},{2,18},{18,2},{3,19},{19,3},{4,20},{20... | collective-permute-start | bytes 442376 | tf_op jit(solution)/shard_map/ppermute | solution.py:654
  39.6 4.2 %copy-start.14 = (bf16[144,704]{1,0:T(8,128)(2,1)S(1)}, bf16[144,704]{1,0:T(8,128)(2,1)}, u32[]{:S(2)}) copy-start(bf16[144,704]{1,0:T(8,128)(2,1)} %copy-done.13) | copy-start | bytes 608260
  39.6 4.2 %collective-permute-start.1 = (f32[2,1152]{1,0:T(2,128)S(1)}, f32[2,1152]{1,0:T(2,128)S(1)}, u32[]{:S(2)}, u32[]{:S(2)}) collective-permute-start(f32[2,1152]{1,0:T(2,128)S(1)} %get-tuple-element.28), channel_id=1, source_target_pairs={{0,1},{1,0},{2,3},{3,2},{4,5},{5,4},{6,7},{7,6},{8,9},{9,8},{10,11... | collective-permute-start | bytes 27656 | tf_op jit(solution)/shard_map/ppermute | solution.py:651
  40.7 5.8 %collective-permute-start.2 = (f32[2,1152]{1,0:T(2,128)S(1)}, f32[2,1152]{1,0:T(2,128)S(1)}, u32[]{:S(2)}, u32[]{:S(2)}) collective-permute-start(f32[2,1152]{1,0:T(2,128)S(1)} %get-tuple-element.31), channel_id=1, source_target_pairs={{1,2},{2,1},{3,4},{4,3},{5,6},{6,5},{7,8},{8,7},{9,10},{10,9},{11,... | collective-permute-start | bytes 27656 | tf_op jit(solution)/shard_map/ppermute | solution.py:651
  43.8 2.6 %copy-start.12 = (bf16[256,512]{1,0:T(8,128)(2,1)S(1)}, bf16[256,512]{1,0:T(8,128)(2,1)}, u32[]{:S(2)}) copy-start(bf16[256,512]{1,0:T(8,128)(2,1)} %copy-done.11) | copy-start | bytes 786436

commit v8 on v7

--- a/solution.py
+++ b/solution.py
@@ -194,11 +194,26 @@
     one_ref,
     two_ref,
     place_ref,
+    edge_one_ref,
+    edge_two_ref,
     part_ref,
 ):
     spots = iota(place_ref.shape[::-1], 0)
     place_ref[...] = jnp.where(spots == dest_ref[...], 1.0, 0.0).T.astype(BF16)
     prepare(first_ref, bias_ref, second_ref, one_ref, two_ref)
+    pair, narrow = edge_one_ref.shape
+    height, depth = one_ref.shape
+    even = (lax.axis_index("facet") & 1) == 0
+    table = jnp.where(
+        even, one_ref[:pair, :].astype(F32), one_ref[height - pair :, :].astype(F32)
+    ).astype(BF16)
+    lane = iota((depth, narrow), 1)
+    column = (lane >> 3) * (BAND + 2) + (lane & 7)
+    column = column + jnp.where(even | (lane >= narrow - 8), 0, BAND - 6)
+    edge_one_ref[...] = mm(table, one_hot(iota((depth, narrow), 0) == column)).astype(BF16)
+    edge_two_ref[...] = jnp.where(
+        even, two_ref[:, :pair].astype(F32), two_ref[:, height - pair :].astype(F32)
+    ).astype(BF16)
     rows, cols = sky_ref.shape
     outer = cols // LANES
     weighted = sky_ref[...] * beam_ref[...]
@@ -476,9 +491,7 @@
 ):
     rows, width = main_ref.shape
     tall = BAND + 2
-    height = one_ref.shape[0]
-    inner = height // BAND
-    pair = 2 * inner
+    inner = one_ref.shape[0] // 2
     place = lax.axis_index("facet")
     final = lax.axis_size("facet") - 1
     even = (place & 1) == 0
@@ -498,12 +511,11 @@
     tiles.start()
     far = far_ref[...]
     base_ref[0:2, :] = far
-    base_ref[2:tall, :] = main_ref[0:BAND, :]
-    base_ref[32 : 32 + BAND, :] = main_ref[rows - BAND : rows, :]
-    base_ref[32 + BAND : 32 + tall, :] = far
-    band = jnp.where(even, base_ref[0:tall, :], base_ref[32 : 32 + tall, :])
-    table = one_ref[pl.ds(pl.multiple_of(jnp.where(even, 0, height - pair), 16), pair), :]
-    hidden = jnp.maximum(mm(table, stack_of(band)), 0.0)
+    base_ref[2:8, :] = main_ref[0:6, :]
+    base_ref[8:14, :] = main_ref[rows - 6 : rows, :]
+    base_ref[14:16, :] = far
+    band = jnp.where(even, base_ref[0:8, :], base_ref[8:16, :])
+    hidden = jnp.maximum(mm(one_ref[...], stack_of(band)), 0.0)
     hidden = jnp.concatenate(
         [
             jnp.where(place == 0, 0.0, hidden[:inner]),
@@ -511,11 +523,8 @@
         ],
         axis=0,
     )
-    second = jnp.where(
-        even, two_ref[:, :pair].astype(F32), two_ref[:, height - pair :].astype(F32)
-    )
     share_ref[0:8, :] = jnp.zeros((8, width), F32)
-    share_ref[8 : tall + 8, :] = share_of(mm(second.astype(BF16), hidden.astype(BF16)))
+    share_ref[8 : tall + 8, :] = share_of(mm(two_ref[...], hidden.astype(BF16)))
     near_sum = jnp.where(even, sum_ref[8:16, :], sum_ref[rows : rows + 8, :])
     share = jnp.where(even, share_ref[10:18, :], share_ref[tall - 2 : tall + 6, :])
     last_ref[...] = near_sum + share
@@ -589,7 +598,7 @@
     )
     got = lax.all_to_all(send, "facet", split_axis=0, concat_axis=0, tiled=True)
 
-    high, low, first, second, placed = call(
+    high, low, first, second, placed, edge_first, edge_second = call(
         forward_kernel,
         [
             shape((width, slots), BF16),
@@ -597,6 +606,8 @@
             shape((hidden * BAND, 9 * (BAND + 2) + 8), BF16),
             shape((6 * (BAND + 2), hidden * BAND), BF16),
             shape((tiles, total), BF16),
+            shape((2 * hidden, 80), BF16),
+            shape((6 * (BAND + 2), 2 * hidden), BF16),
         ],
         1 << 30,
         scratch=[pltpu.VMEM((2, width, slots), BF16)],
@@ -670,14 +681,14 @@
         [shape((rows, cols // count), F32), shape((tiles, width), BF16)],
         1 << 30,
         scratch=[
-            pltpu.VMEM((64, wide), F32),
+            pltpu.VMEM((16, wide), F32),
             pltpu.VMEM((BAND + 10, wide), F32),
             pltpu.VMEM((8, wide), F32),
             pltpu.VMEM((tiles, width), BF16),
             pltpu.SemaphoreType.DMA((3,)),
         ],
         saved=(0, 1),
-    )(partial, main, far, first, second, placed, returned)
+    )(partial, main, far, edge_first, edge_second, placed, returned)
     return tiles_out, image
 
 

time: 48.3 us -> 48.3 us (level)
  no operation moved by 1% of the time
where the time goes in v8:
time: 48.3 us; the launch traced here: 47.8 us
  starting transfers between devices  17.6 us (36%)
  waiting for transfers between devices  13.8 us (29%)
  Pallas kernels  13.5 us (28%)
  local copies, waits for them, and re-layouts  2.07 us (4%)
  between operations  0.89 us (2%)
    pallas_call x7, Pallas kernels, run(): pl.pallas_call(kernel, out_shape=out_shape, in_specs=[far if i in loaded...  13.5 us
    all_to_all x1, waiting for transfers between devices, on_device(): got = lax.all_to_all(send, 'facet', split_axis=0, concat_axis=0, tiled=True)  9.71 us
    all_to_all x1, starting transfers between devices, on_device(): got = lax.all_to_all(send, 'facet', split_axis=0, concat_axis=0, tiled=True)  7.45 us
    all_to_all x1, starting transfers between devices, on_device(): lax.all_to_all(residual.reshape(facets, cap, width), 'facet', split_axis=...  4.7 us
    ppermute x2, starting transfers between devices, beside(): return lax.ppermute(value, 'facet', pairs)  4.18 us
    ppermute x1, waiting for transfers between devices, on_device(): lax.ppermute(value, 'freq', [(f, (f + d + 1) % count) for f in range(coun...  4.06 us
    unnamed x30, local copies, waits for them, and re-layouts  2.07 us
    ppermute x1, starting transfers between devices, on_device(): lax.ppermute(value, 'freq', [(f, (f + d + 1) % count) for f in range(coun...  1.31 us
  transfers between devices with their start and end apart: 5, of which 2 were waited for; matrix products, arithmetic and copies ran while one was open for 0% of the time, Pallas kernels for 17%

profile of v8, /device:TPU:1, one launch (start us, length us, event | category | flops | bytes accessed | tf_op | source)
XLA Modules:
  0.0 47.8 jit_solution(11552325426417027439)
XLA Ops:
  0.6 0.0 copy-start.6
  0.6 0.0 copy-start.7
  0.7 2.2 %shard_map.149 = (bf16[16,136,128]{2,1,0:T(8,128)(2,1)}, s32[1,256]{1,0:T(1,128)S(1)}) custom-call(s32[1,256]{1,0:T(1,128)} %bitcast.14, s32[1,256]{1,0:T(1,128)} %bitcast.15, bf16[256,512]{1,0:T(8,128)(2,1)} %seen_hbm.1), custom_call_target="tpu_custom_call" | custom-call | flops 268435456 | bytes 4194304 | tf_op jit(solution)/shard_map/pallas_call | solution.py:551
  2.9 0.0 copy-start
  2.9 0.0 copy-start.1
  2.9 0.0 copy-start.3
  2.9 0.0 copy-start.10
  2.9 7.5 %all-to-all-start = ((bf16[16,136,128]{2,1,0:T(8,128)(2,1)}), bf16[16,136,128]{2,1,0:T(8,128)(2,1)S(1)}, u32[]{:S(2)}, u32[]{:S(2)}) async-start(bf16[16,136,128]{2,1,0:T(8,128)(2,1)} %get-tuple-element.21), calls=%async_computation | async-start | bytes 1114112 | tf_op jit(solution)/shard_map/all_to_all | solution.py:599
  10.4 0.0 copy-start.2
  10.4 0.0 copy-start.4
  10.4 0.0 copy-done.6
  10.4 0.0 copy-done.7
  10.4 0.0 copy-done
  10.4 0.0 copy-done.1
  10.4 0.0 copy-done.3
  10.4 0.0 copy-done.10
  10.4 0.6 %copy-done.2 = f32[32,3,3]{0,2,1:T(4,128)S(1)} copy-done((f32[32,3,3]{0,2,1:T(4,128)S(1)}, f32[32,3,3]{0,2,1:T(4,128)}, u32[]{:S(2)}) %copy-start.2) | copy-done | bytes 1176
  11.1 0.0 copy-done.4
  11.1 2.8 %shard_map.150 = (bf16[512,512]{1,0:T(8,128)(2,1)S(1)}, bf16[512,512]{1,0:T(8,128)(2,1)S(1)}, bf16[704,224]{1,0:T(8,128)(2,1)S(1)}, bf16[144,704]{1,0:T(8,128)(2...) custom-call(f32[64,2048]{1,0:T(8,128)S(1)} %copy-done, ...), custom_call_target="tpu_custom_call" | custom-call | flops 1073741824 | bytes 4194304 | tf_op jit(solution)/shard_map/pallas_call | solution.py:551
  13.8 0.0 copy-start.11
  13.9 0.7 %copy-done.11 = bf16[256,512]{1,0:T(8,128)(2,1)} copy-done((bf16[256,512]{1,0:T(8,128)(2,1)}, bf16[256,512]{1,0:T(8,128)(2,1)S(1)}, u32[]{:S(2)}) %copy-start.11) | copy-done | bytes 262168
  14.6 0.0 copy-start.13
  14.6 0.7 %copy-done.13 = bf16[144,704]{1,0:T(8,128)(2,1)} copy-done((bf16[144,704]{1,0:T(8,128)(2,1)}, bf16[144,704]{1,0:T(8,128)(2,1)S(1)}, u32[]{:S(2)}) %copy-start.13) | copy-done | bytes 202776
  15.2 9.7 %all-to-all-done.got_ref = bf16[16,136,128]{2,1,0:T(8,128)(2,1)S(1)} async-done(((bf16[16,136,128]{2,1,0:T(8,128)(2,1)}), bf16[16,136,128]{2,1,0:T(8,128)(2,1)S(1)}, u32[]{:S(2)}, u32[]{:S(2)}) %all-to-all-start) | async-done | bytes 557088 | tf_op jit(solution)/shard_map/all_to_all | solution.py:599
  24.9 1.8 %shard_map.151 = (bf16[512,512]{1,0:T(8,128)(2,1)}, bf16[512,512]{1,0:T(8,128)(2,1)S(1)}, bf16[512,512]{1,0:T(8,128)(2,1)S(1)}) custom-call(bf16[16,136,128]{2,1,0:T(8,128)(2,1)S(1)} %all-to-all-done.got_ref, bf16[512,512]{1,0:T(8,128)(2,1)S(1)} %get-tuple-element.23.high_ref, bf16[512,512]{1,0:T(8,128)(2,1)S(1)} %get-tuple-element.24.low_ref), custom_call_target="tpu_custom_call" | custom-call | flops 1073741824 | bytes 4194304 | tf_op jit(solution)/shard_map/pallas_call | solution.py:551
  26.8 0.0 copy-start.5
  26.8 0.0 copy-start.8
  26.8 0.0 copy-start.9
  26.8 4.7 %all-to-all-start.1 = ((bf16[16,32,512]{2,1,0:T(8,128)(2,1)}), bf16[16,32,512]{2,1,0:T(8,128)(2,1)S(1)}, u32[]{:S(2)}, u32[]{:S(2)}) async-start(bf16[16,32,512]{2,1,0:T(8,128)(2,1)} %bitcast.6), calls=%async_computation.1 | async-start | bytes 1048576 | tf_op jit(solution)/shard_map/all_to_all | solution.py:633
  31.5 0.0 copy-done.5
  31.5 0.0 copy-done.8
  31.5 0.0 copy-done.9
  31.5 2.7 %shard_map.152 = (f32[64,1152]{1,0:T(8,128)S(1)}, bf16[64,1152]{1,0:T(8,128)(2,1)S(1)}) custom-call(bf16[512,512]{1,0:T(8,128)(2,1)S(1)} %get-tuple-element.25.res_ref, bf16[512,512]{1,0:T(8,128)(2,1)S(1)} %get-tuple-element.26.sel_ref, bf16[64,256]{1,0:T(8,128)(2,1)S(1)} %copy-done.8, f32[2,16,128]{2,1,0:T(8,128)S(1)} %copy-done.9, ...), custom_call_target="tpu_custom_call" | custom-call | flops 1073741824 | bytes 4194304 | tf_op jit(solution)/shard_map/pallas_call | solution.py:551
  34.2 1.3 %collective-permute-start = (bf16[64,1152]{1,0:T(8,128)(2,1)S(1)}, bf16[64,1152]{1,0:T(8,128)(2,1)S(1)}, u32[]{:S(2)}, u32[]{:S(2)}) collective-permute-start(bf16[64,1152]{1,0:T(8,128)(2,1)S(1)} %get-tuple-element.28), channel_id=1, source_target_pairs={{0,16},{16,0},{1,17},{17,1},{2,18},{18,2},{3,19},{19,3},{4,20},{20... | collective-permute-start | bytes 442376 | tf_op jit(solution)/shard_map/ppermute | solution.py:665
  35.5 4.1 %collective-permute-done.refs_0_ = bf16[64,1152]{1,0:T(8,128)(2,1)S(1)} collective-permute-done((bf16[64,1152]{1,0:T(8,128)(2,1)S(1)}, bf16[64,1152]{1,0:T(8,128)(2,1)S(1)}, u32[]{:S(2)}, u32[]{:S(2)}) %collective-permute-start) | collective-permute-done | bytes 147488 | tf_op jit(solution)/shard_map/ppermute | solution.py:665
  39.6 0.0 copy-start.14
  39.6 1.0 %collective-permute-start.1 = (f32[2,1152]{1,0:T(2,128)S(1)}, f32[2,1152]{1,0:T(2,128)S(1)}, u32[]{:S(2)}, u32[]{:S(2)}) collective-permute-start(f32[2,1152]{1,0:T(2,128)S(1)} %get-tuple-element.30), channel_id=1, source_target_pairs={{0,1},{1,0},{2,3},{3,2},{4,5},{5,4},{6,7},{7,6},{8,9},{9,8},{10,11... | collective-permute-start | bytes 27656 | tf_op jit(solution)/shard_map/ppermute | solution.py:662
  40.7 3.2 %collective-permute-start.2 = (f32[2,1152]{1,0:T(2,128)S(1)}, f32[2,1152]{1,0:T(2,128)S(1)}, u32[]{:S(2)}, u32[]{:S(2)}) collective-permute-start(f32[2,1152]{1,0:T(2,128)S(1)} %get-tuple-element.33), channel_id=1, source_target_pairs={{1,2},{2,1},{3,4},{4,3},{5,6},{6,5},{7,8},{8,7},{9,10},{10,9},{11,... | collective-permute-start | bytes 27656 | tf_op jit(solution)/shard_map/ppermute | solution.py:662
  43.8 0.0 collective-permute-done.1.near_ref
  43.8 0.0 copy-done.14
  43.8 0.0 copy-start.12
  43.9 2.5 %shard_map.154.sum_ref = f32[80,1152]{1,0:T(8,128)S(1)} custom-call(f32[64,1152]{1,0:T(8,128)S(1)} %get-tuple-element.29.main_ref, f32[2,1152]{1,0:T(2,128)S(1)} %collective-permute-done.1.near_ref, bf16[704,224]{1,0:T(8,128)(2,1)S(1)} %get-tuple-element.31.one_ref, bf16[144,704]{1,0:T(8,128)(2,1)S(1)} %copy-done.14), custom_call_target="tpu_custom_call" | custom-call | flops 2147483648 | bytes 4194304 | tf_op jit(solution)/shard_map/pallas_call | solution.py:551
  46.4 0.0 collective-permute-done.2.far_ref
  46.4 0.0 all-to-all-done.1
  46.4 0.0 copy-done.12
  46.4 1.4 %shard_map.155 = (f32[64,1024]{1,0:T(8,128)}, bf16[256,512]{1,0:T(8,128)(2,1)}) custom-call(f32[80,1152]{1,0:T(8,128)S(1)} %shard_map.154.sum_ref, f32[64,1152]{1,0:T(8,128)S(1)} %get-tuple-element.29.main_ref, f32[2,1152]{1,0:T(2,128)S(1)} %collective-permute-done.2.far_ref, bf16[64,80]{1,0:T(8,128)(2,1)S(1)} %get-tuple-element.34.one_ref, ...), custom_call_target="tpu_custom_call" | custom-call | flops 1073741824 | bytes 4194304 | tf_op jit(solution)/shard_map/pallas_call | solution.py:551
  (1 shorter events, 0.0 us)
Async XLA Ops:
  0.6 9.8 %copy-start.6 = (bf16[2,256,256]{2,1,0:T(8,128)(2,1)S(1)}, bf16[2,256,256]{2,1,0:T(8,128)(2,1)}, u32[]{:S(2)}) copy-start(bf16[2,256,256]{2,1,0:T(8,128)(2,1)} %constant.14.clone.mat_ref) | copy-start | bytes 786436
  0.6 9.8 %copy-start.7 = (bf16[128,192]{1,0:T(8,128)(2,1)S(1)}, bf16[128,192]{1,0:T(8,128)(2,1)}, u32[]{:S(2)}) copy-start(bf16[128,192]{1,0:T(8,128)(2,1)} %constant.12.clone.row_ref) | copy-start | bytes 147460
  2.9 7.5 %copy-start = (f32[64,2048]{1,0:T(8,128)S(1)}, f32[64,2048]{1,0:T(8,128)}, u32[]{:S(2)}) copy-start(f32[64,2048]{1,0:T(8,128)} %sky_hbm.1) | copy-start | bytes 1572868
  2.9 7.5 %copy-start.1 = (f32[1,64,2048]{2,1,0:T(8,128)S(1)}, f32[1,64,2048]{2,1,0:T(8,128)}, u32[]{:S(2)}) copy-start(f32[1,64,2048]{2,1,0:T(8,128)} %param.15) | copy-start | bytes 1572868
  2.9 7.5 %copy-start.3 = (f32[32,3,3]{0,2,1:T(4,128)S(1)}, f32[32,3,3]{0,2,1:T(4,128)}, u32[]{:S(2)}) copy-start(f32[32,3,3]{0,2,1:T(4,128)} %param.21) | copy-start | bytes 3460
  2.9 7.5 %copy-start.10 = (f32[2,16,128]{2,1,0:T(8,128)S(1)}, f32[2,16,128]{2,1,0:T(8,128)}, u32[]{:S(2)}) copy-start(f32[2,16,128]{2,1,0:T(8,128)} %constant.13.clone.twist_ref) | copy-start | bytes 49156
  2.9 22.0 %all-to-all-start = ((bf16[16,136,128]{2,1,0:T(8,128)(2,1)}), bf16[16,136,128]{2,1,0:T(8,128)(2,1)S(1)}, u32[]{:S(2)}, u32[]{:S(2)}) async-start(bf16[16,136,128]{2,1,0:T(8,128)(2,1)} %get-tuple-element.21), calls=%async_computation | async-start | bytes 1114112 | tf_op jit(solution)/shard_map/all_to_all | solution.py:599
  10.4 0.7 %copy-start.2 = (f32[32,3,3]{0,2,1:T(4,128)S(1)}, f32[32,3,3]{0,2,1:T(4,128)}, u32[]{:S(2)}) copy-start(f32[32,3,3]{0,2,1:T(4,128)} %param.19) | copy-start | bytes 3460
  10.4 0.7 %copy-start.4 = (f32[32]{0:T(128)S(1)}, f32[32]{0:T(128)}, u32[]{:S(2)}) copy-start(f32[32]{0:T(128)} %param.20) | copy-start | bytes 388
  13.8 0.7 %copy-start.11 = (bf16[256,512]{1,0:T(8,128)(2,1)}, bf16[256,512]{1,0:T(8,128)(2,1)S(1)}, u32[]{:S(2)}) copy-start(bf16[256,512]{1,0:T(8,128)(2,1)S(1)} %get-tuple-element.36.place_ref) | copy-start | bytes 786436
  14.6 0.7 %copy-start.13 = (bf16[144,704]{1,0:T(8,128)(2,1)}, bf16[144,704]{1,0:T(8,128)(2,1)S(1)}, u32[]{:S(2)}) copy-start(bf16[144,704]{1,0:T(8,128)(2,1)S(1)} %get-tuple-element.32.two_ref) | copy-start | bytes 608260
  26.8 4.7 %copy-start.5 = (bf16[2,256,256]{2,1,0:T(8,128)(2,1)S(1)}, bf16[2,256,256]{2,1,0:T(8,128)(2,1)}, u32[]{:S(2)}) copy-start(bf16[2,256,256]{2,1,0:T(8,128)(2,1)} %constant.17.clone.mat_ref) | copy-start | bytes 786436
  26.8 4.7 %copy-start.8 = (bf16[64,256]{1,0:T(8,128)(2,1)S(1)}, bf16[64,256]{1,0:T(8,128)(2,1)}, u32[]{:S(2)}) copy-start(bf16[64,256]{1,0:T(8,128)(2,1)} %constant.15.clone.row_ref) | copy-start | bytes 98308
  26.8 4.7 %copy-start.9 = (f32[2,16,128]{2,1,0:T(8,128)S(1)}, f32[2,16,128]{2,1,0:T(8,128)}, u32[]{:S(2)}) copy-start(f32[2,16,128]{2,1,0:T(8,128)} %constant.16.clone.twist_ref) | copy-start | bytes 49156
  26.8 19.6 %all-to-all-start.1 = ((bf16[16,32,512]{2,1,0:T(8,128)(2,1)}), bf16[16,32,512]{2,1,0:T(8,128)(2,1)S(1)}, u32[]{:S(2)}, u32[]{:S(2)}) async-start(bf16[16,32,512]{2,1,0:T(8,128)(2,1)} %bitcast.6), calls=%async_computation.1 | async-start | bytes 1048576 | tf_op jit(solution)/shard_map/all_to_all | solution.py:633
  34.2 5.4 %collective-permute-start = (bf16[64,1152]{1,0:T(8,128)(2,1)S(1)}, bf16[64,1152]{1,0:T(8,128)(2,1)S(1)}, u32[]{:S(2)}, u32[]{:S(2)}) collective-permute-start(bf16[64,1152]{1,0:T(8,128)(2,1)S(1)} %get-tuple-element.28), channel_id=1, source_target_pairs={{0,16},{16,0},{1,17},{17,1},{2,18},{18,2},{3,19},{19,3},{4,20},{20... | collective-permute-start | bytes 442376 | tf_op jit(solution)/shard_map/ppermute | solution.py:665
  39.6 4.2 %copy-start.14 = (bf16[144,704]{1,0:T(8,128)(2,1)S(1)}, bf16[144,704]{1,0:T(8,128)(2,1)}, u32[]{:S(2)}) copy-start(bf16[144,704]{1,0:T(8,128)(2,1)} %copy-done.13) | copy-start | bytes 608260
  39.6 4.2 %collective-permute-start.1 = (f32[2,1152]{1,0:T(2,128)S(1)}, f32[2,1152]{1,0:T(2,128)S(1)}, u32[]{:S(2)}, u32[]{:S(2)}) collective-permute-start(f32[2,1152]{1,0:T(2,128)S(1)} %get-tuple-element.30), channel_id=1, source_target_pairs={{0,1},{1,0},{2,3},{3,2},{4,5},{5,4},{6,7},{7,6},{8,9},{9,8},{10,11... | collective-permute-start | bytes 27656 | tf_op jit(solution)/shard_map/ppermute | solution.py:662
  40.7 5.8 %collective-permute-start.2 = (f32[2,1152]{1,0:T(2,128)S(1)}, f32[2,1152]{1,0:T(2,128)S(1)}, u32[]{:S(2)}, u32[]{:S(2)}) collective-permute-start(f32[2,1152]{1,0:T(2,128)S(1)} %get-tuple-element.33), channel_id=1, source_target_pairs={{1,2},{2,1},{3,4},{4,3},{5,6},{6,5},{7,8},{8,7},{9,10},{10,9},{11,... | collective-permute-start | bytes 27656 | tf_op jit(solution)/shard_map/ppermute | solution.py:662
  43.8 2.6 %copy-start.12 = (bf16[256,512]{1,0:T(8,128)(2,1)S(1)}, bf16[256,512]{1,0:T(8,128)(2,1)}, u32[]{:S(2)}) copy-start(bf16[256,512]{1,0:T(8,128)(2,1)} %copy-done.11) | copy-start | bytes 786436

commit v9 on v8

--- a/solution.py
+++ b/solution.py
@@ -155,7 +155,7 @@
         ((1,), (1,)),
     )
     parts = width // LANES
-    groups = 4
+    groups = 8
     here = facets // groups
     loads[2].wait()
     saves = []
@@ -506,9 +506,14 @@
         sems.at[0],
     )
     early.start()
-    tiles_ref[...] = mm(place_ref[...], back_ref[...]).astype(BF16)
-    tiles = pltpu.make_async_copy(tiles_ref, tiles_hbm, sems.at[2])
-    tiles.start()
+    half = tiles_ref.shape[0] // 2
+    tiles = []
+    for i in range(2):
+        here = slice(i * half, (i + 1) * half)
+        tiles_ref[here, :] = mm(place_ref[here, :], back_ref[...]).astype(BF16)
+        save = pltpu.make_async_copy(tiles_ref.at[here, :], tiles_hbm.at[here, :], sems.at[2 + i])
+        save.start()
+        tiles.append(save)
     far = far_ref[...]
     base_ref[0:2, :] = far
     base_ref[2:8, :] = main_ref[0:6, :]
@@ -535,7 +540,8 @@
     )
     late.start()
     early.wait()
-    tiles.wait()
+    for save in tiles:
+        save.wait()
     late.wait()
 
 
@@ -586,7 +592,7 @@
             pltpu.VMEM((1, tiles), jnp.int32),
             pltpu.VMEM((tiles, width), BF16),
             pltpu.VMEM((facets, deep, LANES), BF16),
-            pltpu.SemaphoreType.DMA((7,)),
+            pltpu.SemaphoreType.DMA((11,)),
         ],
         loaded=(0, 1, 2),
         saved=(0,),
@@ -685,7 +691,7 @@
             pltpu.VMEM((BAND + 10, wide), F32),
             pltpu.VMEM((8, wide), F32),
             pltpu.VMEM((tiles, width), BF16),
-            pltpu.SemaphoreType.DMA((3,)),
+            pltpu.SemaphoreType.DMA((4,)),
         ],
         saved=(0, 1),
     )(partial, main, far, edge_first, edge_second, placed, returned)

time: 48.3 us -> 48.3 us (level)
  no operation moved by 1% of the time
where the time goes in v9:
time: 48.3 us; the launch traced here: 47.9 us
  starting transfers between devices  17.6 us (36%)
  waiting for transfers between devices  13.8 us (29%)
  Pallas kernels  13.5 us (28%)
  local copies, waits for them, and re-layouts  2.07 us (4%)
  between operations  0.89 us (2%)
    pallas_call x7, Pallas kernels, run(): pl.pallas_call(kernel, out_shape=out_shape, in_specs=[far if i in loaded...  13.5 us
    all_to_all x1, waiting for transfers between devices, on_device(): got = lax.all_to_all(send, 'facet', split_axis=0, concat_axis=0, tiled=True)  9.71 us
    all_to_all x1, starting transfers between devices, on_device(): got = lax.all_to_all(send, 'facet', split_axis=0, concat_axis=0, tiled=True)  7.45 us
    all_to_all x1, starting transfers between devices, on_device(): lax.all_to_all(residual.reshape(facets, cap, width), 'facet', split_axis=...  4.7 us
    ppermute x2, starting transfers between devices, beside(): return lax.ppermute(value, 'facet', pairs)  4.19 us
    ppermute x1, waiting for transfers between devices, on_device(): lax.ppermute(value, 'freq', [(f, (f + d + 1) % count) for f in range(coun...  4.05 us
    unnamed x30, local copies, waits for them, and re-layouts  2.07 us
    ppermute x1, starting transfers between devices, on_device(): lax.ppermute(value, 'freq', [(f, (f + d + 1) % count) for f in range(coun...  1.31 us
  transfers between devices with their start and end apart: 5, of which 2 were waited for; matrix products, arithmetic and copies ran while one was open for 0% of the time, Pallas kernels for 17%

profile of v9, /device:TPU:1, one launch (start us, length us, event | category | flops | bytes accessed | tf_op | source)
XLA Modules:
  0.0 47.9 jit_solution(15693704377412982559)
XLA Ops:
  0.6 0.0 copy-start.6
  0.6 0.0 copy-start.7
  0.7 2.3 %shard_map.149 = (bf16[16,136,128]{2,1,0:T(8,128)(2,1)}, s32[1,256]{1,0:T(1,128)S(1)}) custom-call(s32[1,256]{1,0:T(1,128)} %bitcast.14, s32[1,256]{1,0:T(1,128)} %bitcast.15, bf16[256,512]{1,0:T(8,128)(2,1)} %seen_hbm.1), custom_call_target="tpu_custom_call" | custom-call | flops 268435456 | bytes 4194304 | tf_op jit(solution)/shard_map/pallas_call | solution.py:557
  3.0 0.0 copy-start
  3.0 0.0 copy-start.1
  3.0 0.0 copy-start.3
  3.0 0.0 copy-start.10
  3.0 7.5 %all-to-all-start = ((bf16[16,136,128]{2,1,0:T(8,128)(2,1)}), bf16[16,136,128]{2,1,0:T(8,128)(2,1)S(1)}, u32[]{:S(2)}, u32[]{:S(2)}) async-start(bf16[16,136,128]{2,1,0:T(8,128)(2,1)} %get-tuple-element.21), calls=%async_computation | async-start | bytes 1114112 | tf_op jit(solution)/shard_map/all_to_all | solution.py:605
  10.5 0.0 copy-start.2
  10.5 0.0 copy-start.4
  10.5 0.0 copy-done.6
  10.5 0.0 copy-done.7
  10.5 0.0 copy-done
  10.5 0.0 copy-done.1
  10.5 0.0 copy-done.3
  10.5 0.0 copy-done.10
  10.6 0.6 %copy-done.2 = f32[32,3,3]{0,2,1:T(4,128)S(1)} copy-done((f32[32,3,3]{0,2,1:T(4,128)S(1)}, f32[32,3,3]{0,2,1:T(4,128)}, u32[]{:S(2)}) %copy-start.2) | copy-done | bytes 1176
  11.2 0.0 copy-done.4
  11.2 2.8 %shard_map.150 = (bf16[512,512]{1,0:T(8,128)(2,1)S(1)}, bf16[512,512]{1,0:T(8,128)(2,1)S(1)}, bf16[704,224]{1,0:T(8,128)(2,1)S(1)}, bf16[144,704]{1,0:T(8,128)(2...) custom-call(f32[64,2048]{1,0:T(8,128)S(1)} %copy-done, ...), custom_call_target="tpu_custom_call" | custom-call | flops 1073741824 | bytes 4194304 | tf_op jit(solution)/shard_map/pallas_call | solution.py:557
  14.0 0.0 copy-start.11
  14.0 0.7 %copy-done.11 = bf16[256,512]{1,0:T(8,128)(2,1)} copy-done((bf16[256,512]{1,0:T(8,128)(2,1)}, bf16[256,512]{1,0:T(8,128)(2,1)S(1)}, u32[]{:S(2)}) %copy-start.11) | copy-done | bytes 262168
  14.7 0.0 copy-start.13
  14.7 0.7 %copy-done.13 = bf16[144,704]{1,0:T(8,128)(2,1)} copy-done((bf16[144,704]{1,0:T(8,128)(2,1)}, bf16[144,704]{1,0:T(8,128)(2,1)S(1)}, u32[]{:S(2)}) %copy-start.13) | copy-done | bytes 202776
  15.3 9.7 %all-to-all-done.got_ref = bf16[16,136,128]{2,1,0:T(8,128)(2,1)S(1)} async-done(((bf16[16,136,128]{2,1,0:T(8,128)(2,1)}), bf16[16,136,128]{2,1,0:T(8,128)(2,1)S(1)}, u32[]{:S(2)}, u32[]{:S(2)}) %all-to-all-start) | async-done | bytes 557088 | tf_op jit(solution)/shard_map/all_to_all | solution.py:605
  25.1 1.8 %shard_map.151 = (bf16[512,512]{1,0:T(8,128)(2,1)}, bf16[512,512]{1,0:T(8,128)(2,1)S(1)}, bf16[512,512]{1,0:T(8,128)(2,1)S(1)}) custom-call(bf16[16,136,128]{2,1,0:T(8,128)(2,1)S(1)} %all-to-all-done.got_ref, bf16[512,512]{1,0:T(8,128)(2,1)S(1)} %get-tuple-element.23.high_ref, bf16[512,512]{1,0:T(8,128)(2,1)S(1)} %get-tuple-element.24.low_ref), custom_call_target="tpu_custom_call" | custom-call | flops 1073741824 | bytes 4194304 | tf_op jit(solution)/shard_map/pallas_call | solution.py:557
  26.9 0.0 copy-start.5
  26.9 0.0 copy-start.8
  26.9 0.0 copy-start.9
  26.9 4.7 %all-to-all-start.1 = ((bf16[16,32,512]{2,1,0:T(8,128)(2,1)}), bf16[16,32,512]{2,1,0:T(8,128)(2,1)S(1)}, u32[]{:S(2)}, u32[]{:S(2)}) async-start(bf16[16,32,512]{2,1,0:T(8,128)(2,1)} %bitcast.6), calls=%async_computation.1 | async-start | bytes 1048576 | tf_op jit(solution)/shard_map/all_to_all | solution.py:639
  31.6 0.0 copy-done.5
  31.6 0.0 copy-done.8
  31.6 0.0 copy-done.9
  31.6 2.7 %shard_map.152 = (f32[64,1152]{1,0:T(8,128)S(1)}, bf16[64,1152]{1,0:T(8,128)(2,1)S(1)}) custom-call(bf16[512,512]{1,0:T(8,128)(2,1)S(1)} %get-tuple-element.25.res_ref, bf16[512,512]{1,0:T(8,128)(2,1)S(1)} %get-tuple-element.26.sel_ref, bf16[64,256]{1,0:T(8,128)(2,1)S(1)} %copy-done.8, f32[2,16,128]{2,1,0:T(8,128)S(1)} %copy-done.9, ...), custom_call_target="tpu_custom_call" | custom-call | flops 1073741824 | bytes 4194304 | tf_op jit(solution)/shard_map/pallas_call | solution.py:557
  34.3 1.3 %collective-permute-start = (bf16[64,1152]{1,0:T(8,128)(2,1)S(1)}, bf16[64,1152]{1,0:T(8,128)(2,1)S(1)}, u32[]{:S(2)}, u32[]{:S(2)}) collective-permute-start(bf16[64,1152]{1,0:T(8,128)(2,1)S(1)} %get-tuple-element.28), channel_id=1, source_target_pairs={{0,16},{16,0},{1,17},{17,1},{2,18},{18,2},{3,19},{19,3},{4,20},{20... | collective-permute-start | bytes 442376 | tf_op jit(solution)/shard_map/ppermute | solution.py:671
  35.6 4.1 %collective-permute-done.refs_0_ = bf16[64,1152]{1,0:T(8,128)(2,1)S(1)} collective-permute-done((bf16[64,1152]{1,0:T(8,128)(2,1)S(1)}, bf16[64,1152]{1,0:T(8,128)(2,1)S(1)}, u32[]{:S(2)}, u32[]{:S(2)}) %collective-permute-start) | collective-permute-done | bytes 147488 | tf_op jit(solution)/shard_map/ppermute | solution.py:671
  39.7 0.0 copy-start.14
  39.7 1.0 %collective-permute-start.1 = (f32[2,1152]{1,0:T(2,128)S(1)}, f32[2,1152]{1,0:T(2,128)S(1)}, u32[]{:S(2)}, u32[]{:S(2)}) collective-permute-start(f32[2,1152]{1,0:T(2,128)S(1)} %get-tuple-element.30), channel_id=1, source_target_pairs={{0,1},{1,0},{2,3},{3,2},{4,5},{5,4},{6,7},{7,6},{8,9},{9,8},{10,11... | collective-permute-start | bytes 27656 | tf_op jit(solution)/shard_map/ppermute | solution.py:668
  40.8 3.2 %collective-permute-start.2 = (f32[2,1152]{1,0:T(2,128)S(1)}, f32[2,1152]{1,0:T(2,128)S(1)}, u32[]{:S(2)}, u32[]{:S(2)}) collective-permute-start(f32[2,1152]{1,0:T(2,128)S(1)} %get-tuple-element.33), channel_id=1, source_target_pairs={{1,2},{2,1},{3,4},{4,3},{5,6},{6,5},{7,8},{8,7},{9,10},{10,9},{11,... | collective-permute-start | bytes 27656 | tf_op jit(solution)/shard_map/ppermute | solution.py:668
  43.9 0.0 collective-permute-done.1.near_ref
  43.9 0.0 copy-done.14
  44.0 0.0 copy-start.12
  44.0 2.5 %shard_map.154.sum_ref = f32[80,1152]{1,0:T(8,128)S(1)} custom-call(f32[64,1152]{1,0:T(8,128)S(1)} %get-tuple-element.29.main_ref, f32[2,1152]{1,0:T(2,128)S(1)} %collective-permute-done.1.near_ref, bf16[704,224]{1,0:T(8,128)(2,1)S(1)} %get-tuple-element.31.one_ref, bf16[144,704]{1,0:T(8,128)(2,1)S(1)} %copy-done.14), custom_call_target="tpu_custom_call" | custom-call | flops 2147483648 | bytes 4194304 | tf_op jit(solution)/shard_map/pallas_call | solution.py:557
  46.5 0.0 collective-permute-done.2.far_ref
  46.5 0.0 all-to-all-done.1
  46.5 0.0 copy-done.12
  46.5 1.3 %shard_map.155 = (f32[64,1024]{1,0:T(8,128)}, bf16[256,512]{1,0:T(8,128)(2,1)}) custom-call(f32[80,1152]{1,0:T(8,128)S(1)} %shard_map.154.sum_ref, f32[64,1152]{1,0:T(8,128)S(1)} %get-tuple-element.29.main_ref, f32[2,1152]{1,0:T(2,128)S(1)} %collective-permute-done.2.far_ref, bf16[64,80]{1,0:T(8,128)(2,1)S(1)} %get-tuple-element.34.one_ref, ...), custom_call_target="tpu_custom_call" | custom-call | flops 1073741824 | bytes 4194304 | tf_op jit(solution)/shard_map/pallas_call | solution.py:557
  (1 shorter events, 0.0 us)
Async XLA Ops:
  0.6 9.9 %copy-start.6 = (bf16[2,256,256]{2,1,0:T(8,128)(2,1)S(1)}, bf16[2,256,256]{2,1,0:T(8,128)(2,1)}, u32[]{:S(2)}) copy-start(bf16[2,256,256]{2,1,0:T(8,128)(2,1)} %constant.14.clone.mat_ref) | copy-start | bytes 786436
  0.6 9.9 %copy-start.7 = (bf16[128,192]{1,0:T(8,128)(2,1)S(1)}, bf16[128,192]{1,0:T(8,128)(2,1)}, u32[]{:S(2)}) copy-start(bf16[128,192]{1,0:T(8,128)(2,1)} %constant.12.clone.row_ref) | copy-start | bytes 147460
  3.0 7.5 %copy-start = (f32[64,2048]{1,0:T(8,128)S(1)}, f32[64,2048]{1,0:T(8,128)}, u32[]{:S(2)}) copy-start(f32[64,2048]{1,0:T(8,128)} %sky_hbm.1) | copy-start | bytes 1572868
  3.0 7.5 %copy-start.1 = (f32[1,64,2048]{2,1,0:T(8,128)S(1)}, f32[1,64,2048]{2,1,0:T(8,128)}, u32[]{:S(2)}) copy-start(f32[1,64,2048]{2,1,0:T(8,128)} %param.15) | copy-start | bytes 1572868
  3.0 7.5 %copy-start.3 = (f32[32,3,3]{0,2,1:T(4,128)S(1)}, f32[32,3,3]{0,2,1:T(4,128)}, u32[]{:S(2)}) copy-start(f32[32,3,3]{0,2,1:T(4,128)} %param.21) | copy-start | bytes 3460
  3.0 7.5 %copy-start.10 = (f32[2,16,128]{2,1,0:T(8,128)S(1)}, f32[2,16,128]{2,1,0:T(8,128)}, u32[]{:S(2)}) copy-start(f32[2,16,128]{2,1,0:T(8,128)} %constant.13.clone.twist_ref) | copy-start | bytes 49156
  3.0 22.0 %all-to-all-start = ((bf16[16,136,128]{2,1,0:T(8,128)(2,1)}), bf16[16,136,128]{2,1,0:T(8,128)(2,1)S(1)}, u32[]{:S(2)}, u32[]{:S(2)}) async-start(bf16[16,136,128]{2,1,0:T(8,128)(2,1)} %get-tuple-element.21), calls=%async_computation | async-start | bytes 1114112 | tf_op jit(solution)/shard_map/all_to_all | solution.py:605
  10.5 0.7 %copy-start.2 = (f32[32,3,3]{0,2,1:T(4,128)S(1)}, f32[32,3,3]{0,2,1:T(4,128)}, u32[]{:S(2)}) copy-start(f32[32,3,3]{0,2,1:T(4,128)} %param.19) | copy-start | bytes 3460
  10.5 0.7 %copy-start.4 = (f32[32]{0:T(128)S(1)}, f32[32]{0:T(128)}, u32[]{:S(2)}) copy-start(f32[32]{0:T(128)} %param.20) | copy-start | bytes 388
  14.0 0.7 %copy-start.11 = (bf16[256,512]{1,0:T(8,128)(2,1)}, bf16[256,512]{1,0:T(8,128)(2,1)S(1)}, u32[]{:S(2)}) copy-start(bf16[256,512]{1,0:T(8,128)(2,1)S(1)} %get-tuple-element.36.place_ref) | copy-start | bytes 786436
  14.7 0.7 %copy-start.13 = (bf16[144,704]{1,0:T(8,128)(2,1)}, bf16[144,704]{1,0:T(8,128)(2,1)S(1)}, u32[]{:S(2)}) copy-start(bf16[144,704]{1,0:T(8,128)(2,1)S(1)} %get-tuple-element.32.two_ref) | copy-start | bytes 608260
  26.9 4.7 %copy-start.5 = (bf16[2,256,256]{2,1,0:T(8,128)(2,1)S(1)}, bf16[2,256,256]{2,1,0:T(8,128)(2,1)}, u32[]{:S(2)}) copy-start(bf16[2,256,256]{2,1,0:T(8,128)(2,1)} %constant.17.clone.mat_ref) | copy-start | bytes 786436
  26.9 4.7 %copy-start.8 = (bf16[64,256]{1,0:T(8,128)(2,1)S(1)}, bf16[64,256]{1,0:T(8,128)(2,1)}, u32[]{:S(2)}) copy-start(bf16[64,256]{1,0:T(8,128)(2,1)} %constant.15.clone.row_ref) | copy-start | bytes 98308
  26.9 4.7 %copy-start.9 = (f32[2,16,128]{2,1,0:T(8,128)S(1)}, f32[2,16,128]{2,1,0:T(8,128)}, u32[]{:S(2)}) copy-start(f32[2,16,128]{2,1,0:T(8,128)} %constant.16.clone.twist_ref) | copy-start | bytes 49156
  26.9 19.6 %all-to-all-start.1 = ((bf16[16,32,512]{2,1,0:T(8,128)(2,1)}), bf16[16,32,512]{2,1,0:T(8,128)(2,1)S(1)}, u32[]{:S(2)}, u32[]{:S(2)}) async-start(bf16[16,32,512]{2,1,0:T(8,128)(2,1)} %bitcast.6), calls=%async_computation.1 | async-start | bytes 1048576 | tf_op jit(solution)/shard_map/all_to_all | solution.py:639
  34.3 5.4 %collective-permute-start = (bf16[64,1152]{1,0:T(8,128)(2,1)S(1)}, bf16[64,1152]{1,0:T(8,128)(2,1)S(1)}, u32[]{:S(2)}, u32[]{:S(2)}) collective-permute-start(bf16[64,1152]{1,0:T(8,128)(2,1)S(1)} %get-tuple-element.28), channel_id=1, source_target_pairs={{0,16},{16,0},{1,17},{17,1},{2,18},{18,2},{3,19},{19,3},{4,20},{20... | collective-permute-start | bytes 442376 | tf_op jit(solution)/shard_map/ppermute | solution.py:671
  39.7 4.3 %copy-start.14 = (bf16[144,704]{1,0:T(8,128)(2,1)S(1)}, bf16[144,704]{1,0:T(8,128)(2,1)}, u32[]{:S(2)}) copy-start(bf16[144,704]{1,0:T(8,128)(2,1)} %copy-done.13) | copy-start | bytes 608260
  39.7 4.2 %collective-permute-start.1 = (f32[2,1152]{1,0:T(2,128)S(1)}, f32[2,1152]{1,0:T(2,128)S(1)}, u32[]{:S(2)}, u32[]{:S(2)}) collective-permute-start(f32[2,1152]{1,0:T(2,128)S(1)} %get-tuple-element.30), channel_id=1, source_target_pairs={{0,1},{1,0},{2,3},{3,2},{4,5},{5,4},{6,7},{7,6},{8,9},{9,8},{10,11... | collective-permute-start | bytes 27656 | tf_op jit(solution)/shard_map/ppermute | solution.py:668
  40.8 5.8 %collective-permute-start.2 = (f32[2,1152]{1,0:T(2,128)S(1)}, f32[2,1152]{1,0:T(2,128)S(1)}, u32[]{:S(2)}, u32[]{:S(2)}) collective-permute-start(f32[2,1152]{1,0:T(2,128)S(1)} %get-tuple-element.33), channel_id=1, source_target_pairs={{1,2},{2,1},{3,4},{4,3},{5,6},{6,5},{7,8},{8,7},{9,10},{10,9},{11,... | collective-permute-start | bytes 27656 | tf_op jit(solution)/shard_map/ppermute | solution.py:668
  44.0 2.6 %copy-start.12 = (bf16[256,512]{1,0:T(8,128)(2,1)S(1)}, bf16[256,512]{1,0:T(8,128)(2,1)}, u32[]{:S(2)}) copy-start(bf16[256,512]{1,0:T(8,128)(2,1)} %copy-done.11) | copy-start | bytes 786436
